TPU v7x, 32 devices: a whole 2x2x4 slice. The times are simulated.
32 devices in a mesh: group: 1, rows: 32 (over z, y, x, core).
Axes of the slice: x: 2, y: 2, z: 4, core: 2. Of those that a mesh axis runs over, the one named last changes fastest.
Arguments:
- embeddings: float32 [12288, 4096], P(('group', 'rows'))
- assignment: int32 [12288], P(('group', 'rows')), may hold values from 0 to 255, as said below
Outputs:
- maxima: float32 [12288], P(('group', 'rows'))
- centroids: float32 [256, 4096], P(('group', 'rows'))
Inputs may be any that keep to these rules, and one draw needn't show every extreme that they name: `assignment`: on each index of rows (384 rows in order) no cluster has more than 2 rows, and some cluster has exactly 2 rows on every index; every cluster has at least one row.
All inputs are finite; a program needn't handle non-finite values.
Results may differ from a plain program's by a relative error of at most 0.0003.
Values may be sent and summed in bfloat16 or wider, within the bound.
No kernel may reach another device: no remote copies, remote signals or barrier semaphores. Data moves between devices by JAX's collectives and lax.ppermute only.
A program may use at most 64 MiB of HBM per device.

v0:
```python
import jax
import jax.numpy as jnp
from jax import lax
from jax.sharding import PartitionSpec as P

CLUSTERS = 256
SLOTS = 2


def full_compare(block, live):
    span, width = block.shape
    scores = (
        lax.dot_general(block, block, (((1,), (1,)), ((), ())), preferred_element_type=jnp.float32)
        / width
    )
    slot_ids = jnp.arange(span, dtype=jnp.int32)
    usable = live[None, :] & (slot_ids[None, :] != slot_ids[:, None])
    return jnp.max(jnp.where(usable, scores, -1.0), axis=1)


def owner_work(pieces):
    slot_rows, slot_flags = pieces
    sources, items, slot_count, width = slot_rows.shape
    span = sources * slot_count
    by_cluster = jnp.moveaxis(slot_rows, 1, 0).reshape(items, span, width)
    live_slots = jnp.moveaxis(slot_flags, 1, 0).reshape(items, span) > 0
    found = lax.map(lambda pair: full_compare(pair[0], pair[1]), (by_cluster, live_slots))
    return jnp.moveaxis(found.reshape(items, sources, slot_count), 0, 1)


def on_device(embeddings, assignment):
    dev_count = lax.axis_size("rows")
    cl_dev = CLUSTERS // dev_count
    rows_here, width = embeddings.shape
    cluster_ids = jnp.arange(CLUSTERS, dtype=jnp.int32)
    member = assignment[:, None] == cluster_ids[None, :]
    onehot = member.astype(jnp.float32)
    partial_sums = jnp.einsum("rc,rd->cd", onehot, embeddings, precision=lax.Precision.HIGHEST)
    partial_counts = jnp.sum(onehot, axis=0)
    total_sums, count_all = lax.psum((partial_sums, partial_counts), "rows")
    table = total_sums / count_all[:, None]
    own_centroids = lax.dynamic_slice_in_dim(table, lax.axis_index("rows") * cl_dev, cl_dev, 0)
    centred = embeddings - jnp.take(table, assignment, axis=0)
    unit = (centred * lax.rsqrt(jnp.mean(centred * centred, axis=1, keepdims=True) + 1e-06)).astype(
        jnp.bfloat16
    )
    row_ids = jnp.arange(rows_here, dtype=jnp.int32)
    same_cluster = assignment[:, None] == assignment[None, :]
    earlier = row_ids[None, :] < row_ids[:, None]
    copy_index = jnp.sum((same_cluster & earlier).astype(jnp.int32), axis=1)
    row_position = jnp.sum(jnp.where(member, cluster_ids[None, :], 0), axis=1)
    slot_index = row_position * SLOTS + copy_index
    send_rows = jnp.zeros((CLUSTERS * SLOTS, width), jnp.bfloat16).at[slot_index].set(unit)
    send_rows = send_rows.reshape(dev_count, cl_dev, SLOTS, width)
    send_flags = jnp.zeros((CLUSTERS * SLOTS,), jnp.bfloat16).at[slot_index].set(1.0)
    send_flags = send_flags.reshape(dev_count, cl_dev, SLOTS)
    found = owner_work(
        (
            lax.all_to_all(send_rows, "rows", split_axis=0, concat_axis=0, tiled=True),
            lax.all_to_all(send_flags, "rows", split_axis=0, concat_axis=0, tiled=True),
        )
    )
    returned = lax.all_to_all(found, "rows", split_axis=0, concat_axis=0, tiled=True).reshape(-1)
    maxima = jnp.take(returned, slot_index)
    return (maxima, own_centroids)


def solution(mesh):
    placed = (P(("group", "rows"), None), P(("group", "rows")))
    return jax.shard_map(
        on_device,
        mesh=mesh,
        in_specs=placed,
        out_specs=(P(("group", "rows")), P(("group", "rows"), None)),
        check_vma=False,
    )
```

profile of v0, /device:TPU:0, one launch (start us, length us, event | category | flops | bytes accessed | tf_op | source)
XLA Modules:
  0.0 345.6 jit_solution(7659200475672883318)
XLA Ops:
  7.2 9.6 %fusion.10 = f32[256,4096]{1,0:T(8,128)} fusion(f32[384,4096]{1,0:T(8,128)} %param.4, s32[384]{0:T(512)} %param.5), kind=kOutput, calls=%fused_computation.26 | convolution fusion | flops 4831936512 | bytes 10487296 | tf_op jit(solution)/shard_map/rc,rd->cd/dot_general | solution.py:38
  18.0 3.0 scatter_custom_fusion
  22.0 7.3 %all-to-all-start = ((bf16[32,8,2]{1,2,0:T(2,128)(2,1)}), bf16[32,8,2]{1,2,0:T(2,128)(2,1)S(1)}, u32[]{:S(2)}, u32[]{:S(2)}) async-start(bf16[32,8,2]{1,2,0:T(2,128)(2,1)} %copy.20), calls=%async_computation | async-start | bytes 32768 | tf_op jit(solution)/shard_map/all_to_all | solution.py:60
  29.4 40.9 %psum.15 = f32[256]{0:T(256)S(1)} all-reduce(f32[256]{0:T(256)S(1)} %convert_reduce_fusion.1), channel_id=1, replica_groups=mesh['group'=1,'rows'=32] {'rows'}, use_global_device_ids=true, to_apply=%region_4.5 | all-reduce | flops 256 | bytes 2048 | tf_op jit(solution)/shard_map/psum | solution.py:40
  70.3 91.5 %all-reduce.2.cloned.1.call-done = f32[256,4096]{1,0:T(8,128)} async-done(((f32[256,4096]{1,0:T(8,128)}), f32[256,4096]{1,0:T(8,128)}) %all-reduce.2.cloned.1.call-update) | async-done | bytes 4194320 | tf_op jit(solution)/shard_map/psum | solution.py:40
  161.8 4.8 %broadcast_divide_fusion = f32[256,4096]{1,0:T(8,128)} fusion(f32[256,4096]{1,0:T(8,128)} %all-reduce.2.cloned.1.call-done, f32[256]{0:T(256)S(1)} %psum.15), kind=kLoop, calls=%fused_computation.18 | loop fusion | flops 1048576 | bytes 8389632 | tf_op jit(solution)/shard_map/div | solution.py:41
  166.6 10.4 %gather_fusion = f32[384,4096]{1,0:T(8,128)} fusion(f32[256,4096]{1,0:T(8,128)} %broadcast_divide_fusion, s32[1024]{0:T(1024)S(1)} %pad_clamp_fusion.1), kind=kCustom, calls=%fused_computation | custom fusion | bytes 12584448 | tf_op jit(solution)/shard_map/jit(_take)/gather | solution.py:43
  177.0 5.6 %multiply_reduce_fusion = f32[384]{0:T(512)S(1)} fusion(f32[384,4096]{1,0:T(8,128)} %param.4, f32[384,4096]{1,0:T(8,128)} %gather_fusion, pred[384]{0:T(512)(128)(4,1)S(1)} %compare_and_fusion), kind=kLoop, calls=%fused_computation.14 | loop fusion | flops 6291072 | bytes 12584832 | tf_op jit(solution)/shard_map/reduce_sum | solution.py:44
  182.6 11.8 %scatter_custom_fusion.1 = bf16[512,4096]{1,0:T(8,128)(2,1)} fusion(s32[384]{0:T(512)S(1)} %fusion.12, f32[384]{0:T(512)S(1)} %add_rsqrt_fusion, bf16[]{:T(256)} %constant.42.clone.1, f32[384,4096]{1,0:T(8,128)} %param.4, f32[384,4096]{1,0:T(8,128)} %gather_fusion, pred[384]{0:T(512)(128)(4,1)S(1)} %compare_and_fusion), kind=kCustom, calls=%fused_computation.16 | custom fusion | flops 6291456 | bytes 16779778 | tf_op jit(solution)/shard_map/scatter | solution.py:53
  194.4 7.6 %reshape.71 = bf16[32,8,2,4096]{3,2,1,0:T(2,128)(2,1)} reshape(bf16[512,4096]{1,0:T(8,128)(2,1)} %scatter_custom_fusion.1) | data formatting | bytes 8388608 | tf_op jit(solution)/shard_map/reshape | solution.py:54
  202.0 3.6 %all-to-all-start.1 = ((bf16[32,8,2,4096]{3,2,1,0:T(2,128)(2,1)}), bf16[32,8,2,4096]{3,2,1,0:T(2,128)(2,1)}, u32[]{:S(2)}, u32[]{:S(2)}) async-start(bf16[32,8,2,4096]{3,2,1,0:T(2,128)(2,1)} %reshape.71), calls=%async_computation.1 | async-start | bytes 8388608 | tf_op jit(solution)/shard_map/all_to_all | solution.py:59
  205.8 93.7 %all-to-all-done.1 = bf16[32,8,2,4096]{3,2,1,0:T(2,128)(2,1)} async-done(((bf16[32,8,2,4096]{3,2,1,0:T(2,128)(2,1)}), bf16[32,8,2,4096]{3,2,1,0:T(2,128)(2,1)}, u32[]{:S(2)}, u32[]{:S(2)}) %all-to-all-start.1) | async-done | bytes 4194336 | tf_op jit(solution)/shard_map/all_to_all | solution.py:59
  299.5 6.7 %copy.21 = bf16[8,32,2,4096]{3,0,2,1:T(8,128)(2,1)S(1)} copy(bf16[8,32,2,4096]{3,2,0,1:T(2,128)(2,1)} %bitcast.4) | data formatting | bytes 8388608 | tf_op jit(solution)/shard_map/transpose | solution.py:25
  306.2 4.2 %copy.23 = bf16[8,64,4096]{2,1,0:T(8,128)(2,1)} copy(bf16[8,64,4096]{2,0,1:T(8,128)(2,1)S(1)} %bitcast.24) | data formatting | bytes 8388608 | tf_op jit(solution)/shard_map/while | solution.py:27
  310.4 12.6 %while.10 = (s32[]{:T(128)}, f32[8,64]{1,0:T(8,128)S(1)}, pred[8,64]{1,0:T(8,128)(4,1)S(1)}, bf16[8,64,4096]{2,1,0:T(8,128)(2,1)}, s32[]{:T(128)}, /*index=5*/s32[]{:T(128)}) while((s32[]{:T(128)}, f32[8,64]{1,0:T(8,128)S(1)}, pred[8,64]{1,0:T(8,128)(4,1)S(1)}, bf16[8,64,4096]{2,1,0:T(8,128)(2,1)}, s32[]{:T(128)}, ...), condition=%wide.region_10.11_spmd, body=%wide.region_8.10_spmd.sunk | while | flops 33574848 | bytes 525337 | solution.py:27
  312.0 1.5 fusion.19
  313.6 1.5 fusion.19
  315.1 1.5 fusion.19
  318.3 1.5 fusion.19
  321.5 1.5 fusion.19
  323.7 4.0 %all-to-all-start.2 = ((f32[32,8,2]{1,2,0:T(2,128)}), f32[32,8,2]{1,2,0:T(2,128)S(1)}, u32[]{:S(2)}, u32[]{:S(2)}) async-start(f32[32,8,2]{1,2,0:T(2,128)} %bitcast.7), calls=%async_computation.2 | async-start | bytes 65536 | tf_op jit(solution)/shard_map/all_to_all | solution.py:63
  327.7 1.6 constant_dynamic-slice_fusion
  329.3 5.7 %all-to-all-done.2 = f32[32,8,2]{1,2,0:T(2,128)S(1)} async-done(((f32[32,8,2]{1,2,0:T(2,128)}), f32[32,8,2]{1,2,0:T(2,128)S(1)}, u32[]{:S(2)}, u32[]{:S(2)}) %all-to-all-start.2) | async-done | bytes 2080 | tf_op jit(solution)/shard_map/all_to_all | solution.py:63
  335.4 2.8 gather_fusion.1
  (45 shorter events, 9.1 us)
Async XLA Ops:
  7.2 154.7 %all-reduce.2.cloned.1.call-start = ((), (), s32[]{:S(2)}) async-start(), calls=%async_computation.3 | async-start | bytes 8388608 | tf_op jit(solution)/shard_map/psum | solution.py:40
  16.8 0.7 copy-start
  22.0 180.1 %all-to-all-start = ((bf16[32,8,2]{1,2,0:T(2,128)(2,1)}), bf16[32,8,2]{1,2,0:T(2,128)(2,1)S(1)}, u32[]{:S(2)}, u32[]{:S(2)}) async-start(bf16[32,8,2]{1,2,0:T(2,128)(2,1)} %copy.20), calls=%async_computation | async-start | bytes 32768 | tf_op jit(solution)/shard_map/all_to_all | solution.py:60
  202.0 97.5 %all-to-all-start.1 = ((bf16[32,8,2,4096]{3,2,1,0:T(2,128)(2,1)}), bf16[32,8,2,4096]{3,2,1,0:T(2,128)(2,1)}, u32[]{:S(2)}, u32[]{:S(2)}) async-start(bf16[32,8,2,4096]{3,2,1,0:T(2,128)(2,1)} %reshape.71), calls=%async_computation.1 | async-start | bytes 8388608 | tf_op jit(solution)/shard_map/all_to_all | solution.py:59
  323.7 11.2 %all-to-all-start.2 = ((f32[32,8,2]{1,2,0:T(2,128)}), f32[32,8,2]{1,2,0:T(2,128)S(1)}, u32[]{:S(2)}, u32[]{:S(2)}) async-start(f32[32,8,2]{1,2,0:T(2,128)} %bitcast.7), calls=%async_computation.2 | async-start | bytes 65536 | tf_op jit(solution)/shard_map/all_to_all | solution.py:63
Sparse Core Ops, SparseCore 0:
  16.9 144.8 all-reduce.1
where the time goes:
time: 346 us
  waiting for transfers between devices  191 us (55%)
  blocking collectives  40.9 us (12%)
  local copies, waits for them, and re-layouts  39.5 us (11%)
  other arithmetic  23.4 us (7%)
  matrix products  21.7 us (6%)
  starting transfers between devices  14.9 us (4%)
  between operations  14.2 us (4%)
    all_to_all x1, waiting for transfers between devices, on_device(): lax.all_to_all(send_rows, 'rows', split_axis=0, concat_axis=0, tiled=True)  93.7 us
    psum x1, waiting for transfers between devices, on_device(): total_sums, count_all = lax.psum((partial_sums, partial_counts), 'rows')  91.5 us
    psum x1, blocking collectives, on_device(): total_sums, count_all = lax.psum((partial_sums, partial_counts), 'rows')  40.9 us
    dot_general x8, matrix products, full_compare(): lax.dot_general(block, block, (((1,), (1,)), ((), ())), preferred_element...  12.1 us
    scatter x1, other arithmetic, on_device(): jnp.zeros((CLUSTERS * SLOTS, width), jnp.bfloat16).at[slot_index].set(unit)  11.8 us
    gather x1, local copies, waits for them, and re-layouts, on_device(): centred = embeddings - jnp.take(table, assignment, axis=0)  10.4 us
    dot_general x1, matrix products, on_device(): jnp.einsum('rc,rd->cd', onehot, embeddings, precision=lax.Precision.HIGHEST)  9.57 us
    reshape x1, local copies, waits for them, and re-layouts, on_device(): send_rows = send_rows.reshape(dev_count, cl_dev, SLOTS, width)  7.62 us
  transfers between devices with their start and end apart: 4, of which 3 were waited for; matrix products, arithmetic and copies ran while one was open for 13% of the time, Pallas kernels for 0%

commit v1 on v0

v1 whole, which is shorter than its diff:
```python
import functools

import jax
import jax.numpy as jnp
from jax import lax
from jax.experimental import pallas as pl
from jax.experimental.pallas import tpu as pltpu
from jax.sharding import PartitionSpec as P

CLUSTERS = 256
TILE = 512
LANES = 128
PARTS = (1024, 1024, 2048)
F32 = jnp.float32
BF16 = jnp.bfloat16


def iota(shape, axis):
    return lax.broadcasted_iota(jnp.int32, shape, axis)


def mm(a, b):
    return lax.dot_general(a, b, (((1,), (0,)), ((), ())), preferred_element_type=F32)


def to_row(col):
    n = col.shape[0]
    return jnp.sum(jnp.where(iota((n, n), 0) == iota((n, n), 1), col, 0), axis=0, keepdims=True)


def to_col(row):
    n = row.shape[1]
    return jnp.sum(jnp.where(iota((n, n), 0) == iota((n, n), 1), row, 0), axis=1, keepdims=True)


def pack_kernel(assign_ref, x_ref, out_ref, mix_ref, count_ref):
    rows = x_ref.shape[0]
    tile = x_ref.shape[1]

    @pl.when(pl.program_id(0) == 0)
    def _():
        a_row = assign_ref[...]
        a_col = to_col(a_row)
        twin = (a_col == a_row) & (iota((rows, rows), 0) < iota((rows, rows), 1))
        second = jnp.sum(twin.astype(F32), axis=0, keepdims=True)
        member = iota((CLUSTERS, rows), 0) == a_row
        count = jnp.sum(member.astype(F32), axis=1, keepdims=True)
        count_ref[...] = count
        share = jnp.where(count > 1.5, 0.5, 1.0)
        mix_ref[:CLUSTERS] = jnp.where(member, share, 0.0).astype(BF16)
        sign = jnp.where(second > 0.5, -0.5, 0.5)
        mix_ref[CLUSTERS:] = jnp.where(member & (count > 1.5), sign, 0.0).astype(BF16)

    x = x_ref[...]
    high = x.astype(BF16)
    low = (x - high.astype(F32)).astype(BF16)
    mixed = mm(mix_ref[...], high) + mm(mix_ref[...], low)
    mean = mixed[:CLUSTERS]
    half = mixed[CLUSTERS:]
    count = count_ref[...]
    mean_high = mean.astype(BF16)
    mean_low = (mean - mean_high.astype(F32)).astype(BF16)
    out_ref[:, :tile] = jnp.where(count > 0.5, mean_high.astype(F32), jnp.inf).astype(BF16)
    out_ref[:, tile : 2 * tile] = mean_low
    out_ref[:, 2 * tile :] = jnp.where(count > 1.5, half, jnp.inf).astype(BF16)


def pack(assign_row, x, start, width):
    rows = x.shape[0]
    first = start // TILE
    return pl.pallas_call(
        pack_kernel,
        grid=(width // TILE,),
        in_specs=[
            pl.BlockSpec((1, rows), lambda t: (0, 0)),
            pl.BlockSpec((rows, TILE), lambda t: (0, first + t)),
        ],
        out_specs=pl.BlockSpec((CLUSTERS, 3 * TILE), lambda t: (0, t)),
        out_shape=jax.ShapeDtypeStruct((CLUSTERS, 3 * width), BF16),
        scratch_shapes=[pltpu.VMEM((2 * CLUSTERS, rows), BF16), pltpu.VMEM((CLUSTERS, 1), F32)],
    )(assign_row, x)


def compare_kernel(cl_dev, width_all, last, *refs):
    if last:
        got_ref, gram_in_ref, centroid_ref, best_ref, gram_ref, mix_ref, total_ref, live_ref = refs
    else:
        got_ref, gram_in_ref, centroid_ref, gram_ref, mix_ref, total_ref, live_ref = refs
        best_ref = None
    slots = got_ref.shape[0]
    tile = got_ref.shape[1] // 3

    @pl.when(pl.program_id(0) == 0)
    def _():
        gram_ref[...] = gram_in_ref[...]
        live0 = (got_ref[:, :1].astype(F32) < jnp.inf).astype(F32)
        live1 = (got_ref[:, 2 * tile : 2 * tile + 1].astype(F32) < jnp.inf).astype(F32)
        live_ref[:slots] = live0
        live_ref[slots:] = live1
        same = (iota((slots, slots), 0) % cl_dev) == (iota((slots, slots), 1) % cl_dev)
        mix = jnp.where(same, to_row(live0 + live1), 0.0)
        mix_ref[...] = mix.astype(BF16)
        total_ref[...] = jnp.sum(mix, axis=1, keepdims=True)

    live0 = live_ref[:slots] > 0.5
    live1 = live_ref[slots:] > 0.5
    high = jnp.where(live0, got_ref[:, :tile].astype(F32), 0.0)
    low = got_ref[:, tile : 2 * tile]
    half = jnp.where(live1, got_ref[:, 2 * tile :].astype(F32), 0.0)
    mix = mix_ref[...]
    centroid = (mm(mix, high.astype(BF16)) + mm(mix, low)) / total_ref[...]
    centroid_ref[...] = centroid[:cl_dev]
    away = (high - centroid) + low.astype(F32)
    both = jnp.concatenate([away + half, away - half], axis=0).astype(BF16)
    gram_ref[...] += lax.dot_general(both, both, (((1,), (1,)), ((), ())), preferred_element_type=F32)

    if last:

        @pl.when(pl.program_id(0) == pl.num_programs(0) - 1)
        def _():
            n = 2 * slots
            gram = gram_ref[...]
            row = iota((n, n), 0)
            col = iota((n, n), 1)
            diag = jnp.where(row == col, gram, 0.0)
            inv_row = lax.rsqrt(jnp.sum(diag, axis=0, keepdims=True) / width_all + 1e-6)
            inv_col = lax.rsqrt(jnp.sum(diag, axis=1, keepdims=True) / width_all + 1e-6)
            score = gram * inv_col * inv_row / width_all
            usable = ((row % cl_dev) == (col % cl_dev)) & (row != col) & (live_ref[...] > 0.5)
            best = jnp.max(jnp.where(usable, score, -1.0), axis=0, keepdims=True)
            sources = slots // cl_dev
            source = (iota((sources, n), 1) % slots) // cl_dev
            spread = jnp.where(source == iota((sources, n), 0), best, 0.0)
            slot = iota((n, LANES), 0)
            lane = (slot // slots) * cl_dev + slot % cl_dev
            pick = (lane == iota((n, LANES), 1)).astype(F32)
            best_ref[...] = lax.dot_general(
                spread,
                pick,
                (((1,), (0,)), ((), ())),
                precision=lax.Precision.HIGHEST,
                preferred_element_type=F32,
            )


def compare(got, gram, cl_dev, width_all, last):
    slots = got.shape[0]
    width = got.shape[1] // 3
    fixed = lambda t: (0, 0)
    out_shape = [jax.ShapeDtypeStruct((cl_dev, width), F32)]
    out_specs = [pl.BlockSpec((cl_dev, TILE), lambda t: (0, t))]
    scratch = [
        pltpu.VMEM((slots, slots), BF16),
        pltpu.VMEM((slots, 1), F32),
        pltpu.VMEM((2 * slots, 1), F32),
    ]
    if last:
        out_shape.append(jax.ShapeDtypeStruct((slots // cl_dev, LANES), F32))
        out_specs.append(pl.BlockSpec((slots // cl_dev, LANES), fixed))
        scratch.insert(0, pltpu.VMEM((2 * slots, 2 * slots), F32))
    else:
        out_shape.append(jax.ShapeDtypeStruct((2 * slots, 2 * slots), F32))
        out_specs.append(pl.BlockSpec((2 * slots, 2 * slots), fixed))
    return pl.pallas_call(
        functools.partial(compare_kernel, cl_dev, width_all, last),
        grid=(width // TILE,),
        in_specs=[
            pl.BlockSpec((slots, 3 * TILE), lambda t: (0, t)),
            pl.BlockSpec((2 * slots, 2 * slots), fixed),
        ],
        out_specs=out_specs,
        out_shape=out_shape,
        scratch_shapes=scratch,
    )(got, gram)


def on_device(embeddings, assignment):
    dev_count = lax.axis_size("rows")
    cl_dev = CLUSTERS // dev_count
    rows, width = embeddings.shape
    assign_row = assignment.reshape(1, rows)
    exchange = functools.partial(lax.all_to_all, axis_name="rows", split_axis=0, concat_axis=0, tiled=True)
    got = []
    start = 0
    for part in PARTS:
        got.append(exchange(pack(assign_row, embeddings, start, part)))
        start += part
    gram = jnp.zeros((2 * CLUSTERS, 2 * CLUSTERS), F32)
    centroids = []
    for i, piece in enumerate(got):
        c, gram = compare(piece, gram, cl_dev, width, i == len(got) - 1)
        centroids.append(c)
    found = exchange(gram)
    row_ids = jnp.arange(rows, dtype=jnp.int32)
    twin = (assignment[:, None] == assignment[None, :]) & (row_ids[None, :] < row_ids[:, None])
    second = jnp.sum(twin.astype(jnp.int32), axis=1)
    owner = (assignment // cl_dev)[:, None] == jnp.arange(dev_count, dtype=jnp.int32)[None, :]
    lane = (second * cl_dev + assignment % cl_dev)[:, None] == jnp.arange(LANES, dtype=jnp.int32)[None, :]
    lines = lax.dot_general(
        owner.astype(F32), found, (((1,), (0,)), ((), ())), precision=lax.Precision.HIGHEST
    )
    maxima = jnp.sum(jnp.where(lane, lines, 0.0), axis=1)
    return (maxima, jnp.concatenate(centroids, axis=1))


def solution(mesh):
    placed = (P(("group", "rows"), None), P(("group", "rows")))
    return jax.shard_map(
        on_device,
        mesh=mesh,
        in_specs=placed,
        out_specs=(P(("group", "rows")), P(("group", "rows"), None)),
        check_vma=False,
    )
```

time: 346 us -> 191 us (0.55)
  waiting for transfers between devices: 191 us -> 133 us
  blocking collectives: 40.9 us -> 0 us
  local copies, waits for them, and re-layouts: 39.5 us -> 6.33 us
  Pallas kernels: 0 us -> 29 us
  other arithmetic: 23.4 us -> 1.75 us
  matrix products: 21.7 us -> 0.95 us
  between operations: 14.2 us -> 0.7 us
  starting transfers between devices: 14.9 us -> 18.8 us
    psum x1 -> x0, waiting for transfers between devices: 91.5 us -> none  [on_device(): total_sums, count_all = lax.psum((partial_sums, partial_counts), 'rows')]
    psum x1 -> x0, blocking collectives: 40.9 us -> none  [on_device(): total_sums, count_all = lax.psum((partial_sums, partial_counts), 'rows')]
    all_to_all x3 -> x4, waiting for transfers between devices: 99.4 us -> 133 us  [the longest x3 127 us: on_device(): got.append(exchange(pack(assign_row, embeddings, start, part)))]
    pallas_call x0 -> x6, Pallas kernels: none -> 29 us  [the longest x3 15.3 us: compare(): pl.pallas_call(functools.partial(compare_kernel, cl_dev, width_all, last)...]
    dot_general x9 -> x1, matrix products: 21.7 us -> 0.95 us  [on_device(): lax.dot_general(owner.astype(F32), found, (((1,), (0,)), ((), ())), preci...]
    gather x2 -> x0, local copies, waits for them, and re-layouts: 13.2 us -> none  [the longest x1 10.4 us: on_device(): centred = embeddings - jnp.take(table, assignment, axis=0)]
    scatter x1 -> x0, other arithmetic: 11.8 us -> none  [on_device(): jnp.zeros((CLUSTERS * SLOTS, width), jnp.bfloat16).at[slot_index].set(unit)]
    reshape x4 -> x0, local copies, waits for them, and re-layouts: 8.8 us -> none  [the longest x1 7.62 us: on_device(): send_rows = send_rows.reshape(dev_count, cl_dev, SLOTS, width)]
  transfers between devices with their start and end apart: 4 -> 4, of which waited for: 3 -> 4; matrix products, arithmetic and copies ran while one was open for 13% -> 2% of each run, Pallas kernels for 0% -> 10%
where the time goes in v1:
time: 191 us; the launch traced here: 190 us
  waiting for transfers between devices  133 us (70%)
  Pallas kernels  29 us (15%)
  starting transfers between devices  18.8 us (10%)
  local copies, waits for them, and re-layouts  6.33 us (3%)
    all_to_all x3, waiting for transfers between devices, on_device(): got.append(exchange(pack(assign_row, embeddings, start, part)))  127 us
    pallas_call x3, Pallas kernels, compare(): pl.pallas_call(functools.partial(compare_kernel, cl_dev, width_all, last)...  15.3 us
    all_to_all x3, starting transfers between devices, on_device(): got.append(exchange(pack(assign_row, embeddings, start, part)))  14.8 us
    pallas_call x3, Pallas kernels, pack(): pl.pallas_call(pack_kernel, grid=(width // TILE,), in_specs=[pl.BlockSpec...  13.8 us
    all_to_all x1, waiting for transfers between devices, on_device(): found = exchange(gram)  5.62 us
    unnamed x12, local copies, waits for them, and re-layouts  3.94 us
    all_to_all x1, starting transfers between devices, on_device(): found = exchange(gram)  3.93 us
  transfers between devices with their start and end apart: 4, of which 4 were waited for; matrix products, arithmetic and copies ran while one was open for 2% of the time, Pallas kernels for 10%

profile of v1, /device:TPU:0, one launch (start us, length us, event | category | flops | bytes accessed | tf_op | source)
XLA Modules:
  0.0 190.2 jit_solution(11052749261861188288)
XLA Ops:
  0.6 1.2 broadcast_in_dim.7.assign_ref
  1.9 3.8 %shard_map.43 = bf16[256,3072]{1,0:T(8,128)(2,1)} custom-call(s32[1,384]{1,0:T(1,128)} %broadcast_in_dim.7.assign_ref, f32[384,4096]{1,0:T(8,128)} %x_ref.5), custom_call_target="tpu_custom_call" | custom-call | tf_op jit(solution)/shard_map/pallas_call | solution.py:71
  5.7 7.3 %all-to-all-start.2 = ((bf16[32,8,3072]{2,1,0:T(8,128)(2,1)}), bf16[32,8,3072]{2,1,0:T(8,128)(2,1)S(1)}, u32[]{:S(2)}, u32[]{:S(2)}) async-start(bf16[32,8,3072]{2,1,0:T(8,128)(2,1)} %bitcast.16), calls=%async_computation.2 | async-start | bytes 3145728 | tf_op jit(solution)/shard_map/all_to_all | solution.py:186
  13.0 3.9 %shard_map.42 = bf16[256,3072]{1,0:T(8,128)(2,1)} custom-call(s32[1,384]{1,0:T(1,128)} %broadcast_in_dim.7.assign_ref, f32[384,4096]{1,0:T(8,128)} %x_ref.5), custom_call_target="tpu_custom_call" | custom-call | tf_op jit(solution)/shard_map/pallas_call | solution.py:71
  16.9 33.8 %all-to-all-done.2 = bf16[32,8,3072]{2,1,0:T(8,128)(2,1)S(1)} async-done(((bf16[32,8,3072]{2,1,0:T(8,128)(2,1)}), bf16[32,8,3072]{2,1,0:T(8,128)(2,1)S(1)}, u32[]{:S(2)}, u32[]{:S(2)}) %all-to-all-start.2) | async-done | bytes 1572896 | tf_op jit(solution)/shard_map/all_to_all | solution.py:186
  50.8 1.2 copy-done.1
  51.9 3.8 %all-to-all-start.1 = ((bf16[32,8,3072]{2,1,0:T(8,128)(2,1)}), bf16[32,8,3072]{2,1,0:T(8,128)(2,1)S(1)}, u32[]{:S(2)}, u32[]{:S(2)}) async-start(bf16[32,8,3072]{2,1,0:T(8,128)(2,1)} %bitcast.15), calls=%async_computation.1 | async-start | bytes 3145728 | tf_op jit(solution)/shard_map/all_to_all | solution.py:186
  55.7 6.0 %shard_map.41 = bf16[256,6144]{1,0:T(8,128)(2,1)} custom-call(s32[1,384]{1,0:T(1,128)} %broadcast_in_dim.7.assign_ref, f32[384,4096]{1,0:T(8,128)} %x_ref.5), custom_call_target="tpu_custom_call" | custom-call | tf_op jit(solution)/shard_map/pallas_call | solution.py:71
  61.8 31.7 %all-to-all-done.1 = bf16[32,8,3072]{2,1,0:T(8,128)(2,1)S(1)} async-done(((bf16[32,8,3072]{2,1,0:T(8,128)(2,1)}), bf16[32,8,3072]{2,1,0:T(8,128)(2,1)S(1)}, u32[]{:S(2)}, u32[]{:S(2)}) %all-to-all-start.1) | async-done | bytes 1572896 | tf_op jit(solution)/shard_map/all_to_all | solution.py:186
  93.4 1.1 copy-done.2
  94.6 3.8 %all-to-all-start = ((bf16[32,8,6144]{2,1,0:T(8,128)(2,1)}), bf16[32,8,6144]{2,1,0:T(8,128)(2,1)S(1)}, u32[]{:S(2)}, u32[]{:S(2)}) async-start(bf16[32,8,6144]{2,1,0:T(8,128)(2,1)} %bitcast.11), calls=%async_computation | async-start | bytes 6291456 | tf_op jit(solution)/shard_map/all_to_all | solution.py:186
  98.4 0.0 copy-done.3
  98.4 0.2 convert_reduce_fusion
  98.6 1.1 broadcast_in_dim.8.refs_1_
  99.8 4.3 %shard_map.44 = (f32[8,1024]{1,0:T(8,128)}, f32[512,512]{1,0:T(8,128)}) custom-call(bf16[256,3072]{1,0:T(8,128)(2,1)} %bitcast.13, f32[512,512]{1,0:T(8,128)} %broadcast_in_dim.8.refs_1_), custom_call_target="tpu_custom_call" | custom-call | tf_op jit(solution)/shard_map/pallas_call | solution.py:164
  104.1 4.3 %shard_map.45 = (f32[8,1024]{1,0:T(8,128)}, f32[512,512]{1,0:T(8,128)}) custom-call(bf16[256,3072]{1,0:T(8,128)(2,1)} %bitcast.14, f32[512,512]{1,0:T(8,128)} %get-tuple-element.8.refs_1_), custom_call_target="tpu_custom_call" | custom-call | tf_op jit(solution)/shard_map/pallas_call | solution.py:164
  108.4 61.5 %all-to-all-done = bf16[32,8,6144]{2,1,0:T(8,128)(2,1)S(1)} async-done(((bf16[32,8,6144]{2,1,0:T(8,128)(2,1)}), bf16[32,8,6144]{2,1,0:T(8,128)(2,1)S(1)}, u32[]{:S(2)}, u32[]{:S(2)}) %all-to-all-start) | async-done | bytes 3145760 | tf_op jit(solution)/shard_map/all_to_all | solution.py:186
  169.8 1.6 copy-done
  171.5 6.7 %shard_map.46 = (f32[8,2048]{1,0:T(8,128)}, f32[32,128]{1,0:T(8,128)}) custom-call(bf16[256,6144]{1,0:T(8,128)(2,1)} %bitcast.12, f32[512,512]{1,0:T(8,128)} %get-tuple-element.9.refs_1_), custom_call_target="tpu_custom_call" | custom-call | tf_op jit(solution)/shard_map/pallas_call | solution.py:164
  178.1 3.9 %all-to-all-start.3 = ((f32[32,1,128]{2,1,0:T(1,128)}), f32[32,1,128]{2,1,0:T(1,128)S(1)}, u32[]{:S(2)}, u32[]{:S(2)}) async-start(f32[32,1,128]{2,1,0:T(1,128)} %bitcast.18), calls=%async_computation.3 | async-start | bytes 32768 | tf_op jit(solution)/shard_map/all_to_all | solution.py:193
  182.1 0.0 copy-done.4
  182.1 1.5 pad_maximum_fusion
  183.6 5.6 %all-to-all-done.3 = f32[32,1,128]{2,1,0:T(1,128)S(1)} async-done(((f32[32,1,128]{2,1,0:T(1,128)}), f32[32,1,128]{2,1,0:T(1,128)S(1)}, u32[]{:S(2)}, u32[]{:S(2)}) %all-to-all-start.3) | async-done | bytes 16416 | tf_op jit(solution)/shard_map/all_to_all | solution.py:193
  189.2 1.0 fusion
  (8 shorter events, 0.0 us)
Async XLA Ops:
  5.7 45.0 %all-to-all-start.2 = ((bf16[32,8,3072]{2,1,0:T(8,128)(2,1)}), bf16[32,8,3072]{2,1,0:T(8,128)(2,1)S(1)}, u32[]{:S(2)}, u32[]{:S(2)}) async-start(bf16[32,8,3072]{2,1,0:T(8,128)(2,1)} %bitcast.16), calls=%async_computation.2 | async-start | bytes 3145728 | tf_op jit(solution)/shard_map/all_to_all | solution.py:186
  50.8 1.2 copy-start.1
  51.9 41.5 %all-to-all-start.1 = ((bf16[32,8,3072]{2,1,0:T(8,128)(2,1)}), bf16[32,8,3072]{2,1,0:T(8,128)(2,1)S(1)}, u32[]{:S(2)}, u32[]{:S(2)}) async-start(bf16[32,8,3072]{2,1,0:T(8,128)(2,1)} %bitcast.15), calls=%async_computation.1 | async-start | bytes 3145728 | tf_op jit(solution)/shard_map/all_to_all | solution.py:186
  93.4 1.1 copy-start.2
  93.4 4.9 %copy-start.3 = (s32[384]{0:T(512)S(1)}, s32[384]{0:T(512)}, u32[]{:S(2)}) copy-start(s32[384]{0:T(512)} %param.3) | copy-start | bytes 4612
  94.6 75.2 %all-to-all-start = ((bf16[32,8,6144]{2,1,0:T(8,128)(2,1)}), bf16[32,8,6144]{2,1,0:T(8,128)(2,1)S(1)}, u32[]{:S(2)}, u32[]{:S(2)}) async-start(bf16[32,8,6144]{2,1,0:T(8,128)(2,1)} %bitcast.11), calls=%async_computation | async-start | bytes 6291456 | tf_op jit(solution)/shard_map/all_to_all | solution.py:186
  169.8 1.6 copy-start
  171.5 10.6 %copy-start.4 = (f32[8,1024]{1,0:T(8,128)S(1)}, f32[8,1024]{1,0:T(8,128)}, u32[]{:S(2)}) copy-start(f32[8,1024]{1,0:T(8,128)} %get-tuple-element.11) | copy-start | bytes 98308
  171.5 10.6 %copy-start.5 = (f32[8,1024]{1,0:T(8,128)S(1)}, f32[8,1024]{1,0:T(8,128)}, u32[]{:S(2)}) copy-start(f32[8,1024]{1,0:T(8,128)} %get-tuple-element.12) | copy-start | bytes 98308
  178.1 11.1 %all-to-all-start.3 = ((f32[32,1,128]{2,1,0:T(1,128)}), f32[32,1,128]{2,1,0:T(1,128)S(1)}, u32[]{:S(2)}, u32[]{:S(2)}) async-start(f32[32,1,128]{2,1,0:T(1,128)} %bitcast.18), calls=%async_computation.3 | async-start | bytes 32768 | tf_op jit(solution)/shard_map/all_to_all | solution.py:193

commit v2 on v1

v2 whole, which is shorter than its diff:
```python
import functools

import jax
import jax.numpy as jnp
from jax import lax
from jax.experimental import pallas as pl
from jax.experimental.pallas import tpu as pltpu
from jax.sharding import PartitionSpec as P

CLUSTERS = 256
TILE = 512
LANES = 128
PARTS = (1024, 3072)
F32 = jnp.float32
BF16 = jnp.bfloat16


def iota(shape, axis):
    return lax.broadcasted_iota(jnp.int32, shape, axis)


def mm(a, b):
    return lax.dot_general(a, b, (((1,), (0,)), ((), ())), preferred_element_type=F32)


def to_row(col):
    n = col.shape[0]
    return jnp.sum(jnp.where(iota((n, n), 0) == iota((n, n), 1), col, 0), axis=0, keepdims=True)


def to_col(row):
    n = row.shape[1]
    return jnp.sum(jnp.where(iota((n, n), 0) == iota((n, n), 1), row, 0), axis=1, keepdims=True)


def gather_kernel(assign_ref, x_ref, sum_ref, half_ref, mix_ref):
    rows = x_ref.shape[0]

    @pl.when(pl.program_id(0) == 0)
    def _():
        a_row = assign_ref[...]
        a_col = to_col(a_row)
        twin = (a_col == a_row) & (iota((rows, rows), 0) < iota((rows, rows), 1))
        second = jnp.sum(twin.astype(F32), axis=0, keepdims=True)
        member = iota((CLUSTERS, rows), 0) == a_row
        count = jnp.sum(member.astype(F32), axis=1, keepdims=True)
        mix_ref[:CLUSTERS] = jnp.where(member, 1.0, 0.0).astype(BF16)
        sign = jnp.where(second > 0.5, -0.5, 0.5)
        mix_ref[CLUSTERS:] = jnp.where(member & (count > 1.5), sign, 0.0).astype(BF16)

    x = x_ref[...]
    high = x.astype(BF16)
    low = (x - high.astype(F32)).astype(BF16)
    mixed = mm(mix_ref[...], high) + mm(mix_ref[...], low)
    sum_ref[...] = mixed[:CLUSTERS]
    half_ref[...] = mixed[CLUSTERS:]


def gather(assign_row, x, start, width):
    rows = x.shape[0]
    first = start // TILE
    out = jax.ShapeDtypeStruct((CLUSTERS, width), F32)
    spec = pl.BlockSpec((CLUSTERS, TILE), lambda t: (0, t))
    return pl.pallas_call(
        gather_kernel,
        grid=(width // TILE,),
        in_specs=[
            pl.BlockSpec((1, rows), lambda t: (0, 0)),
            pl.BlockSpec((rows, TILE), lambda t: (0, first + t)),
        ],
        out_specs=[spec, spec],
        out_shape=[out, out],
        scratch_shapes=[pltpu.VMEM((2 * CLUSTERS, rows), BF16)],
    )(assign_row, x)


def code_kernel(core_ref, mine_ref, mate_ref, sum_ref, mate_sum_ref, half_ref, out_ref, count_ref):
    rows = mine_ref.shape[1]
    tile = sum_ref.shape[1]

    @pl.when(pl.program_id(0) == 0)
    def _():
        ids = iota((CLUSTERS, rows), 0)
        count_ref[:CLUSTERS] = jnp.sum((ids == mine_ref[...]).astype(F32), axis=1, keepdims=True)
        count_ref[CLUSTERS:] = jnp.sum((ids == mate_ref[...]).astype(F32), axis=1, keepdims=True)

    count = count_ref[:CLUSTERS]
    total = jnp.maximum(count + count_ref[CLUSTERS:], 1.0)
    sums = sum_ref[...]
    half = half_ref[...]
    mean = (sums + mate_sum_ref[...]) / total
    away = sums / jnp.maximum(count, 1.0) - mean
    high = mean.astype(BF16)
    low = (mean - high.astype(F32)).astype(BF16)

    @pl.when(core_ref[0] == 0)
    def _():
        out_ref[:, :tile] = jnp.where(count > 0.5, away + half, jnp.inf).astype(BF16)
        out_ref[:, tile : 2 * tile] = jnp.where(count > 1.5, away - half, jnp.inf).astype(BF16)
        out_ref[:, 2 * tile :] = low[:, : tile // 2]

    @pl.when(core_ref[0] == 1)
    def _():
        flag = jnp.where(count > 0.5, jnp.inf, -jnp.inf)
        out_ref[:, :tile] = jnp.where(count > 1.5, away - half, flag).astype(BF16)
        out_ref[:, tile : 2 * tile] = high
        out_ref[:, 2 * tile :] = low[:, tile // 2 :]


def code(core, mine, mate, sums, mate_sums, half):
    rows = mine.shape[1]
    width = sums.shape[1]
    wide = TILE * 5 // 2
    spec = pl.BlockSpec((CLUSTERS, TILE), lambda t: (0, t))
    line = pl.BlockSpec((1, rows), lambda t: (0, 0))
    return pl.pallas_call(
        code_kernel,
        grid=(width // TILE,),
        in_specs=[pl.BlockSpec(memory_space=pltpu.SMEM), line, line, spec, spec, spec],
        out_specs=pl.BlockSpec((CLUSTERS, wide), lambda t: (0, t)),
        out_shape=jax.ShapeDtypeStruct((CLUSTERS, width // TILE * wide), BF16),
        scratch_shapes=[pltpu.VMEM((2 * CLUSTERS, 1), F32)],
    )(core, mine, mate, sums, mate_sums, half)


def compare_kernel(cl_dev, width_all, first, last, *refs):
    refs = list(refs)
    even_ref, odd_ref = refs[:2]
    refs = refs[2:]
    gram_in_ref = None if first else refs.pop(0)
    centroid_ref = refs.pop(0)
    best_ref = refs.pop(0) if last else None
    gram_ref, mix_ref, total_ref, live_ref = refs
    slots = mix_ref.shape[0]
    tile = centroid_ref.shape[1]

    def part(ref, lo, hi):
        return ref[..., lo:hi].astype(F32).reshape(slots, hi - lo)

    @pl.when(pl.program_id(0) == 0)
    def _():
        gram_ref[...] = jnp.zeros_like(gram_ref) if first else gram_in_ref[...]
        mark = part(odd_ref, 0, LANES)[:, :1]
        live = [
            part(even_ref, 0, LANES)[:, :1] < jnp.inf,
            part(even_ref, tile, tile + LANES)[:, :1] < jnp.inf,
            mark > -jnp.inf,
            jnp.abs(mark) < jnp.inf,
        ]
        live = [x.astype(F32) for x in live]
        for k in range(4):
            live_ref[k * slots : (k + 1) * slots] = live[k]
        same = (iota((slots, slots), 0) % cl_dev) == (iota((slots, slots), 1) % cl_dev)
        mix = jnp.where(same, to_row(live[0] + live[1] + live[2] + live[3]), 0.0)
        mix_ref[...] = mix.astype(BF16)
        total_ref[...] = jnp.sum(mix, axis=1, keepdims=True)

    live = [live_ref[k * slots : (k + 1) * slots] > 0.5 for k in range(4)]
    d0 = jnp.where(live[0], part(even_ref, 0, tile), 0.0)
    d1 = jnp.where(live[1], part(even_ref, tile, 2 * tile), 0.0)
    d3 = jnp.where(live[3], part(odd_ref, 0, tile), 0.0)
    d2 = jnp.where(live[2], -(d0 + d1 + d3), 0.0)
    high = part(odd_ref, tile, 2 * tile)
    end = tile * 5 // 2
    low = jnp.concatenate([part(even_ref, 2 * tile, end), part(odd_ref, 2 * tile, end)], axis=1)
    mix = mix_ref[...]
    centroid = (mm(mix, high.astype(BF16)) + mm(mix, low.astype(BF16))) / total_ref[...]
    centroid_ref[...] = centroid[:cl_dev]
    away = (high - centroid) + low
    every = jnp.concatenate([away + d0, away + d1, away + d2, away + d3], axis=0).astype(BF16)
    gram_ref[...] += lax.dot_general(every, every, (((1,), (1,)), ((), ())), preferred_element_type=F32)

    if last:

        @pl.when(pl.program_id(0) == pl.num_programs(0) - 1)
        def _():
            n = 4 * slots
            gram = gram_ref[...]
            row = iota((n, n), 0)
            col = iota((n, n), 1)
            diag = jnp.where(row == col, gram, 0.0)
            inv_row = lax.rsqrt(jnp.sum(diag, axis=0, keepdims=True) / width_all + 1e-6)
            inv_col = lax.rsqrt(jnp.sum(diag, axis=1, keepdims=True) / width_all + 1e-6)
            score = gram * inv_col * inv_row / width_all
            usable = ((row % cl_dev) == (col % cl_dev)) & (row != col) & (live_ref[...] > 0.5)
            best = jnp.max(jnp.where(usable, score, -1.0), axis=0, keepdims=True)
            sources = 2 * slots // cl_dev
            place = iota((sources, n), 1)
            source = (place % slots) // cl_dev * 2 + place // (2 * slots)
            spread = jnp.where(source == iota((sources, n), 0), best, 0.0)
            place = iota((n, LANES), 0)
            lane = (place // slots) % 2 * cl_dev + place % cl_dev
            pick = (lane == iota((n, LANES), 1)).astype(F32)
            best_ref[...] = lax.dot_general(
                spread,
                pick,
                (((1,), (0,)), ((), ())),
                precision=lax.Precision.HIGHEST,
                preferred_element_type=F32,
            )


def compare(got, gram, cl_dev, width_all, last):
    first = gram is None
    slots = CLUSTERS // 2
    wide = TILE * 5 // 2
    width = got.shape[1] // wide * TILE
    chips = slots // cl_dev
    got = got.reshape(chips, 2, cl_dev, got.shape[1])
    fixed = lambda t: (0, 0)
    if cl_dev % 8 == 0:
        pair = [got, got]
        pair_specs = [
            pl.BlockSpec((chips, None, cl_dev, wide), lambda t: (0, 0, 0, t)),
            pl.BlockSpec((chips, None, cl_dev, wide), lambda t: (0, 1, 0, t)),
        ]
    else:
        pair = [got[:, k].reshape(slots, -1) for k in range(2)]
        pair_specs = [pl.BlockSpec((slots, wide), lambda t: (0, t))] * 2
    square = (4 * slots, 4 * slots)
    if not first:
        pair.append(gram)
        pair_specs.append(pl.BlockSpec(square, fixed))
    out_shape = [jax.ShapeDtypeStruct((cl_dev, width), F32)]
    out_specs = [pl.BlockSpec((cl_dev, TILE), lambda t: (0, t))]
    scratch = [
        pltpu.VMEM((slots, slots), BF16),
        pltpu.VMEM((slots, 1), F32),
        pltpu.VMEM((4 * slots, 1), F32),
    ]
    if last:
        out_shape.append(jax.ShapeDtypeStruct((2 * chips, LANES), F32))
        out_specs.append(pl.BlockSpec((2 * chips, LANES), fixed))
        scratch.insert(0, pltpu.VMEM(square, F32))
    else:
        out_shape.append(jax.ShapeDtypeStruct(square, F32))
        out_specs.append(pl.BlockSpec(square, fixed))
    return pl.pallas_call(
        functools.partial(compare_kernel, cl_dev, width_all, first, last),
        grid=(width // TILE,),
        in_specs=pair_specs,
        out_specs=out_specs,
        out_shape=out_shape,
        scratch_shapes=scratch,
    )(*pair)


def on_device(embeddings, assignment):
    dev_count = lax.axis_size("rows")
    cl_dev = CLUSTERS // dev_count
    rows, width = embeddings.shape
    core = (lax.axis_index("rows") % 2).astype(jnp.int32).reshape(1)
    mine = assignment.reshape(1, rows)
    exchange = functools.partial(lax.all_to_all, axis_name="rows", split_axis=0, concat_axis=0, tiled=True)
    swap = functools.partial(lax.ppermute, axis_name="rows", perm=[(i, i ^ 1) for i in range(dev_count)])
    mate = swap(mine)
    got = []
    start = 0
    for part in PARTS:
        sums, half = gather(mine, embeddings, start, part)
        coded = code(core, mine, mate, sums, swap(sums), half)
        coded, embeddings = lax.optimization_barrier((coded, embeddings))
        got.append(exchange(coded))
        start += part
    gram = None
    centroids = []
    for i, piece in enumerate(got):
        c, gram = compare(piece, gram, cl_dev, width, i == len(got) - 1)
        centroids.append(c)
    found = exchange(gram)
    row_ids = jnp.arange(rows, dtype=jnp.int32)
    twin = (assignment[:, None] == assignment[None, :]) & (row_ids[None, :] < row_ids[:, None])
    second = jnp.sum(twin.astype(jnp.int32), axis=1)
    owner = (assignment // cl_dev)[:, None] == jnp.arange(dev_count, dtype=jnp.int32)[None, :]
    lane = (second * cl_dev + assignment % cl_dev)[:, None] == jnp.arange(LANES, dtype=jnp.int32)[None, :]
    lines = lax.dot_general(
        owner.astype(F32), found, (((1,), (0,)), ((), ())), precision=lax.Precision.HIGHEST
    )
    maxima = jnp.sum(jnp.where(lane, lines, 0.0), axis=1)
    return (maxima, jnp.concatenate(centroids, axis=1))


def solution(mesh):
    placed = (P(("group", "rows"), None), P(("group", "rows")))
    return jax.shard_map(
        on_device,
        mesh=mesh,
        in_specs=placed,
        out_specs=(P(("group", "rows")), P(("group", "rows"), None)),
        check_vma=False,
    )
```

time: 191 us -> 175 us (0.916)
  waiting for transfers between devices: 133 us -> 116 us
  Pallas kernels: 29 us -> 35.5 us
  starting transfers between devices: 18.8 us -> 15.5 us
  local copies, waits for them, and re-layouts: 6.33 us -> 3.38 us
    all_to_all x3 -> x2, waiting for transfers between devices: 127 us -> 108 us  [on_device(): got.append(exchange(coded))]
    pallas_call x6, Pallas kernels: 29 us -> 35.5 us  [the longest x2 12.2 us: gather(): pl.pallas_call(gather_kernel, grid=(width // TILE,), in_specs=[pl.BlockSp...]
    all_to_all x3 -> x2, starting transfers between devices: 14.8 us -> 10.7 us  [on_device(): got.append(exchange(coded))]
    ppermute x0 -> x3, waiting for transfers between devices: none -> 2.43 us  [the longest x1 2.12 us: on_device(): mate = swap(mine)]
  transfers between devices with their start and end apart: 4 -> 6, of which waited for: 4 -> 5; matrix products, arithmetic and copies ran while one was open for 2% -> 1% of each run, Pallas kernels for 10% -> 7%
where the time goes in v2:
time: 175 us; the launch traced here: 174 us
  waiting for transfers between devices  116 us (66%)
  Pallas kernels  35.5 us (20%)
  starting transfers between devices  15.5 us (9%)
  local copies, waits for them, and re-layouts  3.38 us (2%)
  other arithmetic  1.8 us (1%)
    all_to_all x2, waiting for transfers between devices, on_device(): got.append(exchange(coded))  108 us
    pallas_call x2, Pallas kernels, gather(): pl.pallas_call(gather_kernel, grid=(width // TILE,), in_specs=[pl.BlockSp...  12.2 us
    pallas_call x2, Pallas kernels, compare(): pl.pallas_call(functools.partial(compare_kernel, cl_dev, width_all, first...  12 us
    pallas_call x2, Pallas kernels, code(): pl.pallas_call(code_kernel, grid=(width // TILE,), in_specs=[pl.BlockSpec...  11.3 us
    all_to_all x2, starting transfers between devices, on_device(): got.append(exchange(coded))  10.7 us
    all_to_all x1, waiting for transfers between devices, on_device(): found = exchange(gram)  5.58 us
    all_to_all x1, starting transfers between devices, on_device(): found = exchange(gram)  3.99 us
  transfers between devices with their start and end apart: 6, of which 5 were waited for; matrix products, arithmetic and copies ran while one was open for 1% of the time, Pallas kernels for 7%

profile of v2, /device:TPU:0, one launch (start us, length us, event | category | flops | bytes accessed | tf_op | source)
XLA Modules:
  0.0 174.2 jit_solution(6986827390172160998)
XLA Ops:
  0.6 1.2 broadcast_in_dim.5.assign_ref.mine_ref
  1.9 3.8 %shard_map.41 = (f32[256,1024]{1,0:T(8,128)}, f32[256,1024]{1,0:T(8,128)}) custom-call(s32[1,384]{1,0:T(1,128)} %broadcast_in_dim.5.assign_ref.mine_ref, f32[384,4096]{1,0:T(8,128)} %x_ref.2), custom_call_target="tpu_custom_call" | custom-call | tf_op jit(solution)/shard_map/pallas_call | solution.py:64
  5.7 0.5 collective-permute-start.1
  6.1 0.1 collective-permute-start
  6.2 2.1 %collective-permute-done.mate_ref = s32[1,384]{1,0:T(1,128)S(1)} collective-permute-done((s32[1,384]{1,0:T(1,128)S(1)}, s32[1,384]{1,0:T(1,128)S(1)}, u32[]{:S(2)}, u32[]{:S(2)}) %collective-permute-start) | collective-permute-done | bytes 1568 | tf_op jit(solution)/shard_map/ppermute | solution.py:256
  8.3 0.3 collective-permute-done.1.mate_sum_ref
  8.6 0.3 copy-done.5
  8.9 0.7 copy-done.1
  9.6 3.3 %shard_map.42 = bf16[256,2560]{1,0:T(8,128)(2,1)} custom-call(s32[1]{0:T(128)} %bitcast.core_ref, s32[1,384]{1,0:T(1,128)} %broadcast_in_dim.5.assign_ref.mine_ref, s32[1,384]{1,0:T(1,128)} %copy-done.5, f32[256,1024]{1,0:T(8,128)} %get-tuple-element.13.sum_ref, f32[256,1024]{1,0:T(8,128)} %copy-done.1, f32[256,1024]{1,0:T(8,128)} %get-tuple-element.14.half_ref), custom_call_target="tpu_custom_call" | custom-call | tf_op jit(solution)/shard_map/pallas_call | solution.py:116
  12.9 8.4 %shard_map.43 = (f32[256,3072]{1,0:T(8,128)}, f32[256,3072]{1,0:T(8,128)}) custom-call(s32[1,384]{1,0:T(1,128)} %broadcast_in_dim.5.assign_ref.mine_ref, f32[384,4096]{1,0:T(8,128)} %x_ref.2), custom_call_target="tpu_custom_call" | custom-call | tf_op jit(solution)/shard_map/pallas_call | solution.py:64
  21.3 0.3 collective-permute-start.2
  21.6 7.0 %all-to-all-start.1 = ((bf16[32,8,2560]{2,1,0:T(8,128)(2,1)}), bf16[32,8,2560]{2,1,0:T(8,128)(2,1)S(1)}, u32[]{:S(2)}, u32[]{:S(2)}) async-start(bf16[32,8,2560]{2,1,0:T(8,128)(2,1)} %bitcast.3), calls=%async_computation.1 | async-start | bytes 2621440 | tf_op jit(solution)/shard_map/all_to_all | solution.py:263
  28.7 8.0 %shard_map.44 = bf16[256,7680]{1,0:T(8,128)(2,1)} custom-call(s32[1]{0:T(128)} %bitcast.core_ref, s32[1,384]{1,0:T(1,128)} %broadcast_in_dim.5.assign_ref.mine_ref, s32[1,384]{1,0:T(1,128)} %copy-done.5, f32[256,3072]{1,0:T(8,128)} %get-tuple-element.16.sum_ref, f32[256,3072]{1,0:T(8,128)} %collective-permute-done.2.mate_sum_ref, ...), custom_call_target="tpu_custom_call" | custom-call | tf_op jit(solution)/shard_map/pallas_call | solution.py:116
  36.7 24.1 %all-to-all-done.1 = bf16[32,8,2560]{2,1,0:T(8,128)(2,1)S(1)} async-done(((bf16[32,8,2560]{2,1,0:T(8,128)(2,1)}), bf16[32,8,2560]{2,1,0:T(8,128)(2,1)S(1)}, u32[]{:S(2)}, u32[]{:S(2)}) %all-to-all-start.1) | async-done | bytes 1310752 | tf_op jit(solution)/shard_map/all_to_all | solution.py:263
  60.8 1.2 copy-done
  61.9 3.7 %all-to-all-start = ((bf16[32,8,7680]{2,1,0:T(8,128)(2,1)}), bf16[32,8,7680]{2,1,0:T(8,128)(2,1)}, u32[]{:S(2)}, u32[]{:S(2)}) async-start(bf16[32,8,7680]{2,1,0:T(8,128)(2,1)} %bitcast.10), calls=%async_computation | async-start | bytes 7864320 | tf_op jit(solution)/shard_map/all_to_all | solution.py:263
  65.6 0.2 convert_reduce_fusion
  65.9 3.8 %shard_map.45 = (f32[8,1024]{1,0:T(8,128)}, f32[512,512]{1,0:T(8,128)}) custom-call(bf16[16,2,8,2560]{3,2,1,0:T(8,128)(2,1)} %bitcast.11, bf16[16,2,8,2560]{3,2,1,0:T(8,128)(2,1)} %bitcast.12), custom_call_target="tpu_custom_call" | custom-call | tf_op jit(solution)/shard_map/pallas_call | solution.py:238
  69.7 84.2 %all-to-all-done = bf16[32,8,7680]{2,1,0:T(8,128)(2,1)} async-done(((bf16[32,8,7680]{2,1,0:T(8,128)(2,1)}), bf16[32,8,7680]{2,1,0:T(8,128)(2,1)}, u32[]{:S(2)}, u32[]{:S(2)}) %all-to-all-start) | async-done | bytes 3932192 | tf_op jit(solution)/shard_map/all_to_all | solution.py:263
  153.9 8.2 %shard_map.46 = (f32[8,3072]{1,0:T(8,128)}, f32[32,128]{1,0:T(8,128)}) custom-call(bf16[16,2,8,7680]{3,2,1,0:T(8,128)(2,1)} %bitcast.2.refs_0_.refs_1_, bf16[16,2,8,7680]{3,2,1,0:T(8,128)(2,1)} %bitcast.2.refs_0_.refs_1_, f32[512,512]{1,0:T(8,128)} %get-tuple-element.20.refs_2_), custom_call_target="tpu_custom_call" | custom-call | tf_op jit(solution)/shard_map/pallas_call | solution.py:238
  162.1 4.0 %all-to-all-start.2 = ((f32[32,1,128]{2,1,0:T(1,128)}), f32[32,1,128]{2,1,0:T(1,128)S(1)}, u32[]{:S(2)}, u32[]{:S(2)}) async-start(f32[32,1,128]{2,1,0:T(1,128)} %bitcast.14), calls=%async_computation.2 | async-start | bytes 32768 | tf_op jit(solution)/shard_map/all_to_all | solution.py:270
  166.1 1.6 pad_maximum_fusion
  167.7 5.6 %all-to-all-done.2 = f32[32,1,128]{2,1,0:T(1,128)S(1)} async-done(((f32[32,1,128]{2,1,0:T(1,128)}), f32[32,1,128]{2,1,0:T(1,128)S(1)}, u32[]{:S(2)}, u32[]{:S(2)}) %all-to-all-start.2) | async-done | bytes 16416 | tf_op jit(solution)/shard_map/all_to_all | solution.py:270
  173.2 1.0 fusion
  (11 shorter events, 0.0 us)
Async XLA Ops:
  1.9 4.3 %copy-start.2 = (s32[1,384]{1,0:T(1,128)S(1)}, s32[1,384]{1,0:T(1,128)}, u32[]{:S(2)}) copy-start(s32[1,384]{1,0:T(1,128)} %broadcast_in_dim.5.assign_ref.mine_ref) | copy-start | bytes 4612
  5.7 3.0 %collective-permute-start.1 = (f32[256,1024]{1,0:T(8,128)}, f32[256,1024]{1,0:T(8,128)S(1)}, u32[]{:S(2)}, u32[]{:S(2)}) collective-permute-start(f32[256,1024]{1,0:T(8,128)} %get-tuple-element.13.sum_ref), channel_id=1, source_target_pairs={{0,1},{1,0},{2,3},{3,2},{4,5},{5,4},{6,7},{7,6},{8,9},{9,8},{10,11... | collective-permute-start | bytes 3145736 | tf_op jit(solution)/shard_map/ppermute | solution.py:261
  6.1 2.2 %collective-permute-start = (s32[1,384]{1,0:T(1,128)S(1)}, s32[1,384]{1,0:T(1,128)S(1)}, u32[]{:S(2)}, u32[]{:S(2)}) collective-permute-start(s32[1,384]{1,0:T(1,128)S(1)} %copy-done.2), channel_id=1, source_target_pairs={{0,1},{1,0},{2,3},{3,2},{4,5},{5,4},{6,7},{7,6},{8,9},{9,8},{10,11... | collective-permute-start | bytes 4616 | tf_op jit(solution)/shard_map/ppermute | solution.py:256
  8.3 0.6 copy-start.5
  8.6 1.0 copy-start.1
  21.3 7.3 %collective-permute-start.2 = (f32[256,3072]{1,0:T(8,128)}, f32[256,3072]{1,0:T(8,128)}, u32[]{:S(2)}, u32[]{:S(2)}) collective-permute-start(f32[256,3072]{1,0:T(8,128)} %get-tuple-element.16.sum_ref), channel_id=1, source_target_pairs={{0,1},{1,0},{2,3},{3,2},{4,5},{5,4},{6,7},{7,6},{8,9},{9,8},{10,11... | collective-permute-start | bytes 9437192 | tf_op jit(solution)/shard_map/ppermute | solution.py:261
  21.6 39.2 %all-to-all-start.1 = ((bf16[32,8,2560]{2,1,0:T(8,128)(2,1)}), bf16[32,8,2560]{2,1,0:T(8,128)(2,1)S(1)}, u32[]{:S(2)}, u32[]{:S(2)}) async-start(bf16[32,8,2560]{2,1,0:T(8,128)(2,1)} %bitcast.3), calls=%async_computation.1 | async-start | bytes 2621440 | tf_op jit(solution)/shard_map/all_to_all | solution.py:263
  60.8 1.2 copy-start
  60.8 4.9 %copy-start.3 = (s32[384]{0:T(512)S(1)}, s32[384]{0:T(512)}, u32[]{:S(2)}) copy-start(s32[384]{0:T(512)} %param.3) | copy-start | bytes 4612
  61.9 91.9 %all-to-all-start = ((bf16[32,8,7680]{2,1,0:T(8,128)(2,1)}), bf16[32,8,7680]{2,1,0:T(8,128)(2,1)}, u32[]{:S(2)}, u32[]{:S(2)}) async-start(bf16[32,8,7680]{2,1,0:T(8,128)(2,1)} %bitcast.10), calls=%async_computation | async-start | bytes 7864320 | tf_op jit(solution)/shard_map/all_to_all | solution.py:263
  153.9 12.2 %copy-start.4 = (f32[8,1024]{1,0:T(8,128)S(1)}, f32[8,1024]{1,0:T(8,128)}, u32[]{:S(2)}) copy-start(f32[8,1024]{1,0:T(8,128)} %get-tuple-element.22) | copy-start | bytes 98308
  162.1 11.1 %all-to-all-start.2 = ((f32[32,1,128]{2,1,0:T(1,128)}), f32[32,1,128]{2,1,0:T(1,128)S(1)}, u32[]{:S(2)}, u32[]{:S(2)}) async-start(f32[32,1,128]{2,1,0:T(1,128)} %bitcast.14), calls=%async_computation.2 | async-start | bytes 32768 | tf_op jit(solution)/shard_map/all_to_all | solution.py:270

commit v3 on v2

v3 whole, which is shorter than its diff:
```python
import functools

import jax
import jax.numpy as jnp
import numpy as np
from jax import lax
from jax.experimental import pallas as pl
from jax.experimental.pallas import tpu as pltpu
from jax.sharding import PartitionSpec as P

CLUSTERS = 256
TILE = 512
LANES = 128
PARTS = (512, 3584)
F32 = jnp.float32
BF16 = jnp.bfloat16


def iota(shape, axis):
    return lax.broadcasted_iota(jnp.int32, shape, axis)


def mm(a, b):
    return lax.dot_general(a, b, (((1,), (0,)), ((), ())), preferred_element_type=F32)


def to_row(col):
    n = col.shape[0]
    return jnp.sum(jnp.where(iota((n, n), 0) == iota((n, n), 1), col, 0), axis=0, keepdims=True)


def to_col(row):
    n = row.shape[1]
    return jnp.sum(jnp.where(iota((n, n), 0) == iota((n, n), 1), row, 0), axis=1, keepdims=True)


def code_kernel(core_ref, mine_ref, mate_ref, x_ref, y_ref, out_ref, sum_ref, own_ref, num_ref):
    rows, tile = x_ref.shape

    @pl.when(pl.program_id(0) == 0)
    def _():
        mine = mine_ref[...]
        twin = (to_col(mine) == mine) & (iota((rows, rows), 0) < iota((rows, rows), 1))
        second = jnp.sum(twin.astype(F32), axis=0, keepdims=True) > 0.5
        member = iota((CLUSTERS, rows), 0) == mine
        other = iota((CLUSTERS, rows), 0) == mate_ref[...]
        sum_ref[:, :rows] = member.astype(F32).astype(BF16)
        sum_ref[:, rows:] = other.astype(F32).astype(BF16)
        own_ref[:CLUSTERS] = (member & ~second).astype(F32).astype(BF16)
        own_ref[CLUSTERS:] = (member & second).astype(F32).astype(BF16)
        count = jnp.sum(member.astype(F32), axis=1, keepdims=True)
        total = count + jnp.sum(other.astype(F32), axis=1, keepdims=True)
        num_ref[:CLUSTERS] = count
        num_ref[CLUSTERS:] = 1.0 / jnp.maximum(total, 1.0)

    x = x_ref[...]
    y = y_ref[...]
    x_high = x.astype(BF16)
    x_low = (x - x_high.astype(F32)).astype(BF16)
    y_high = y.astype(BF16)
    y_low = (y - y_high.astype(F32)).astype(BF16)
    sums = mm(sum_ref[...], jnp.concatenate([x_high, y_high], axis=0))
    sums += mm(sum_ref[...], jnp.concatenate([x_low, y_low], axis=0))
    mean = sums * num_ref[CLUSTERS:]
    high = mean.astype(BF16)
    low = (mean - high.astype(F32)).astype(BF16)
    count = num_ref[:CLUSTERS]

    @pl.when(core_ref[0] == 0)
    def _():
        own = mm(own_ref[...], x_high) + mm(own_ref[...], x_low)
        out_ref[:, :tile] = jnp.where(count > 0.5, own[:CLUSTERS] - mean, jnp.inf).astype(BF16)
        out_ref[:, tile : 2 * tile] = jnp.where(count > 1.5, own[CLUSTERS:] - mean, jnp.inf).astype(BF16)
        out_ref[:, 2 * tile :] = low[:, : tile // 2]

    @pl.when(core_ref[0] == 1)
    def _():
        own = mm(own_ref[CLUSTERS:], x_high) + mm(own_ref[CLUSTERS:], x_low)
        flag = jnp.where(count > 0.5, jnp.inf, -jnp.inf)
        out_ref[:, :tile] = jnp.where(count > 1.5, own - mean, flag).astype(BF16)
        out_ref[:, tile : 2 * tile] = high
        out_ref[:, 2 * tile :] = low[:, tile // 2 :]


def code(core, mine, mate, x, y, start):
    rows, width = y.shape
    first = start // TILE
    steps = width // TILE
    wide = TILE * 5 // 2
    line = pl.BlockSpec((1, rows), lambda t: (0, 0))
    if steps == 1:
        y = pltpu.with_memory_space_constraint(y, pltpu.VMEM)
        y_spec = pl.BlockSpec(memory_space=pltpu.VMEM)
    else:
        y_spec = pl.BlockSpec((rows, TILE), lambda t: (0, t))
    return pl.pallas_call(
        code_kernel,
        grid=(steps,),
        in_specs=[
            pl.BlockSpec(memory_space=pltpu.SMEM),
            line,
            line,
            pl.BlockSpec((rows, TILE), lambda t: (0, first + t)),
            y_spec,
        ],
        out_specs=pl.BlockSpec((CLUSTERS, wide), lambda t: (0, t)),
        out_shape=jax.ShapeDtypeStruct((CLUSTERS, steps * wide), BF16),
        scratch_shapes=[
            pltpu.VMEM((CLUSTERS, 2 * rows), BF16),
            pltpu.VMEM((2 * CLUSTERS, rows), BF16),
            pltpu.VMEM((2 * CLUSTERS, 1), F32),
        ],
    )(core, mine, mate, x, y)


def compare_kernel(cl_dev, width_all, first, last, *refs):
    refs = list(refs)
    got_ref = refs.pop(0)
    gram_in_ref = None if first else refs.pop(0)
    centroid_ref = refs.pop(0)
    best_ref = refs.pop(0) if last else None
    gram_ref, mix_ref, total_ref, live_ref = refs
    slots = mix_ref.shape[0]
    tile = centroid_ref.shape[1]

    def part(core, lo, hi):
        return got_ref[:, core, :, lo:hi].astype(F32).reshape(slots, hi - lo)

    @pl.when(pl.program_id(0) == 0)
    def _():
        gram_ref[...] = jnp.zeros_like(gram_ref) if first else gram_in_ref[...]
        mark = part(1, 0, LANES)[:, :1]
        live = [
            part(0, 0, LANES)[:, :1] < jnp.inf,
            part(0, tile, tile + LANES)[:, :1] < jnp.inf,
            mark > -jnp.inf,
            jnp.abs(mark) < jnp.inf,
        ]
        live = [x.astype(F32) for x in live]
        for k in range(4):
            live_ref[k * slots : (k + 1) * slots] = live[k]
        same = (iota((slots, slots), 0) % cl_dev) == (iota((slots, slots), 1) % cl_dev)
        mix = jnp.where(same, to_row(live[0] + live[1] + live[2] + live[3]), 0.0)
        mix_ref[...] = mix.astype(BF16)
        total_ref[...] = 1.0 / jnp.sum(mix, axis=1, keepdims=True)

    live = [live_ref[k * slots : (k + 1) * slots] > 0.5 for k in range(4)]
    d0 = jnp.where(live[0], part(0, 0, tile), 0.0)
    d1 = jnp.where(live[1], part(0, tile, 2 * tile), 0.0)
    d3 = jnp.where(live[3], part(1, 0, tile), 0.0)
    d2 = jnp.where(live[2], -(d0 + d1 + d3), 0.0)
    high = part(1, tile, 2 * tile)
    end = tile * 5 // 2
    low = jnp.concatenate([part(0, 2 * tile, end), part(1, 2 * tile, end)], axis=1)
    mix = mix_ref[...]
    centroid = (mm(mix, high.astype(BF16)) + mm(mix, low.astype(BF16))) * total_ref[...]
    centroid_ref[...] = centroid[:cl_dev]
    away = (high - centroid) + low
    every = jnp.concatenate([away + d0, away + d1, away + d2, away + d3], axis=0).astype(BF16)
    gram_ref[...] += lax.dot_general(every, every, (((1,), (1,)), ((), ())), preferred_element_type=F32)

    if last:

        @pl.when(pl.program_id(0) == pl.num_programs(0) - 1)
        def _():
            n = 4 * slots
            gram = gram_ref[...]
            row = iota((n, n), 0)
            col = iota((n, n), 1)
            diag = jnp.where(row == col, gram, 0.0)
            inv_row = lax.rsqrt(jnp.sum(diag, axis=0, keepdims=True) / width_all + 1e-6)
            inv_col = lax.rsqrt(jnp.sum(diag, axis=1, keepdims=True) / width_all + 1e-6)
            score = gram * inv_col * inv_row / width_all
            usable = ((row % cl_dev) == (col % cl_dev)) & (row != col) & (live_ref[...] > 0.5)
            best = jnp.max(jnp.where(usable, score, -1.0), axis=0, keepdims=True)
            sources = 2 * slots // cl_dev
            place = iota((sources, n), 1)
            source = (place % slots) // cl_dev * 2 + place // (2 * slots)
            spread = jnp.where(source == iota((sources, n), 0), best, 0.0)
            place = iota((n, LANES), 0)
            lane = (place // slots) % 2 * cl_dev + place % cl_dev
            pick = (lane == iota((n, LANES), 1)).astype(F32)
            best_ref[...] = lax.dot_general(
                spread,
                pick,
                (((1,), (0,)), ((), ())),
                precision=lax.Precision.HIGHEST,
                preferred_element_type=F32,
            )


def compare(got, gram, cl_dev, width_all, last):
    first = gram is None
    slots = CLUSTERS // 2
    wide = TILE * 5 // 2
    width = got.shape[1] // wide * TILE
    chips = slots // cl_dev
    got = got.reshape(chips, 2, cl_dev, got.shape[1])
    if cl_dev % 8:
        got = jnp.moveaxis(got, 1, 0).reshape(1, 2, slots, got.shape[3])
    fixed = lambda t: (0, 0)
    args = [got]
    if width == TILE:
        args = [pltpu.with_memory_space_constraint(got, pltpu.VMEM)]
        specs = [pl.BlockSpec(memory_space=pltpu.VMEM)]
    else:
        specs = [pl.BlockSpec((*got.shape[:3], wide), lambda t: (0, 0, 0, t))]
    square = (4 * slots, 4 * slots)
    if not first:
        args.append(gram)
        specs.append(pl.BlockSpec(square, fixed))
    out_shape = [jax.ShapeDtypeStruct((cl_dev, width), F32)]
    out_specs = [pl.BlockSpec((cl_dev, TILE), lambda t: (0, t))]
    scratch = [
        pltpu.VMEM((slots, slots), BF16),
        pltpu.VMEM((slots, 1), F32),
        pltpu.VMEM((4 * slots, 1), F32),
    ]
    if last:
        out_shape.append(jax.ShapeDtypeStruct((2 * chips, LANES), F32))
        out_specs.append(pl.BlockSpec((2 * chips, LANES), fixed))
        scratch.insert(0, pltpu.VMEM(square, F32))
    else:
        out_shape.append(jax.ShapeDtypeStruct(square, F32))
        out_specs.append(pl.BlockSpec(square, fixed))
    return pl.pallas_call(
        functools.partial(compare_kernel, cl_dev, width_all, first, last),
        grid=(width // TILE,),
        in_specs=specs,
        out_specs=out_specs,
        out_shape=out_shape,
        scratch_shapes=scratch,
    )(*args)


def on_device(embeddings, assignment):
    dev_count = lax.axis_size("rows")
    cl_dev = CLUSTERS // dev_count
    rows, width = embeddings.shape
    core = (lax.axis_index("rows") % 2).astype(jnp.int32).reshape(1)
    mine = assignment.reshape(1, rows)
    exchange = functools.partial(lax.all_to_all, axis_name="rows", split_axis=0, concat_axis=0, tiled=True)
    swap = functools.partial(lax.ppermute, axis_name="rows", perm=[(i, i ^ 1) for i in range(dev_count)])
    mate = swap(assignment).reshape(1, rows)
    others = []
    for part, end in zip(PARTS, np.cumsum(PARTS)):
        piece = embeddings[:, end - part : end]
        if others:
            piece, others[-1] = lax.optimization_barrier((piece, others[-1]))
        others.append(swap(piece))
    got = []
    start = 0
    for i, part in enumerate(PARTS):
        coded = code(core, mine, mate, embeddings, others[i], start)
        coded, embeddings = lax.optimization_barrier((coded, embeddings))
        got.append(exchange(coded))
        start += part
    gram = None
    centroids = []
    for i, piece in enumerate(got):
        c, gram = compare(piece, gram, cl_dev, width, i == len(got) - 1)
        centroids.append(c)
    found = exchange(gram)
    row_ids = jnp.arange(rows, dtype=jnp.int32)
    twin = (assignment[:, None] == assignment[None, :]) & (row_ids[None, :] < row_ids[:, None])
    second = jnp.sum(twin.astype(jnp.int32), axis=1)
    owner = (assignment // cl_dev)[:, None] == jnp.arange(dev_count, dtype=jnp.int32)[None, :]
    lane = (second * cl_dev + assignment % cl_dev)[:, None] == jnp.arange(LANES, dtype=jnp.int32)[None, :]
    lines = lax.dot_general(
        owner.astype(F32), found, (((1,), (0,)), ((), ())), precision=lax.Precision.HIGHEST
    )
    maxima = jnp.sum(jnp.where(lane, lines, 0.0), axis=1)
    return (maxima, jnp.concatenate(centroids, axis=1))


def solution(mesh):
    placed = (P(("group", "rows"), None), P(("group", "rows")))
    return jax.shard_map(
        on_device,
        mesh=mesh,
        in_specs=placed,
        out_specs=(P(("group", "rows")), P(("group", "rows"), None)),
        check_vma=False,
    )
```

time: 175 us -> 171 us (0.977)
  Pallas kernels: 35.5 us -> 27.5 us
  local copies, waits for them, and re-layouts: 3.38 us -> 7.7 us
    pallas_call x4 -> x2, Pallas kernels: 23.5 us -> 16.5 us  [code(): pl.pallas_call(code_kernel, grid=(steps,), in_specs=[pl.BlockSpec(memory_...]
    slice x0 -> x2, local copies, waits for them, and re-layouts: none -> 6.56 us  [on_device(): piece = embeddings[:, end - part:end]]
    all_to_all x2, waiting for transfers between devices: 108 us -> 105 us  [on_device(): got.append(exchange(coded))]
    unnamed x12 -> x4, local copies, waits for them, and re-layouts: 2.13 us -> 0.01 us
    ppermute x3, waiting for transfers between devices: 2.43 us -> 4.34 us  [the longest x1 4.33 us: on_device(): mate = swap(assignment).reshape(1, rows)]
  transfers between devices with their start and end apart: 6 -> 6, of which waited for: 5 -> 4; matrix products, arithmetic and copies ran while one was open for 1% -> 5% of each run, Pallas kernels for 7% -> 11%
where the time goes in v3:
time: 171 us; the launch traced here: 170 us
  waiting for transfers between devices  115 us (67%)
  Pallas kernels  27.5 us (16%)
  starting transfers between devices  16.1 us (9%)
  local copies, waits for them, and re-layouts  7.7 us (5%)
  other arithmetic  1.81 us (1%)
    all_to_all x2, waiting for transfers between devices, on_device(): got.append(exchange(coded))  105 us
    pallas_call x2, Pallas kernels, code(): pl.pallas_call(code_kernel, grid=(steps,), in_specs=[pl.BlockSpec(memory_...  16.5 us
    all_to_all x2, starting transfers between devices, on_device(): got.append(exchange(coded))  11.2 us
    pallas_call x2, Pallas kernels, compare(): pl.pallas_call(functools.partial(compare_kernel, cl_dev, width_all, first...  10.9 us
    slice x2, local copies, waits for them, and re-layouts, on_device(): piece = embeddings[:, end - part:end]  6.56 us
    all_to_all x1, waiting for transfers between devices, on_device(): found = exchange(gram)  5.57 us
    ppermute x1, waiting for transfers between devices, on_device(): mate = swap(assignment).reshape(1, rows)  4.33 us
    all_to_all x1, starting transfers between devices, on_device(): found = exchange(gram)  3.82 us
  transfers between devices with their start and end apart: 6, of which 4 were waited for; matrix products, arithmetic and copies ran while one was open for 5% of the time, Pallas kernels for 11%

profile of v3, /device:TPU:0, one launch (start us, length us, event | category | flops | bytes accessed | tf_op | source)
XLA Modules:
  0.0 169.9 jit_solution(7731216575419421720)
XLA Ops:
  0.6 1.2 slice.7
  1.8 0.0 copy-start
  1.8 0.5 collective-permute-start.1
  2.3 5.4 %slice.6 = f32[384,3584]{1,0:T(8,128)} slice(f32[384,4096]{1,0:T(8,128)} %x_ref.2), slice={[0:384], [512:4096]} | slice | bytes 11010048 | tf_op jit(solution)/shard_map/slice | solution.py:247
  7.7 0.0 collective-permute-done.1.y_ref
  7.7 0.1 collective-permute-start.2
  7.8 0.5 collective-permute-start
  8.2 0.6 broadcast_in_dim.5.mine_ref
  8.8 4.3 %collective-permute-done = s32[384]{0:T(512)S(1)} collective-permute-done((s32[384]{0:T(512)S(1)}, s32[384]{0:T(512)S(1)}, u32[]{:S(2)}, u32[]{:S(2)}) %collective-permute-start) | collective-permute-done | bytes 1568 | tf_op jit(solution)/shard_map/ppermute | solution.py:244
  13.1 0.6 reshape.30.mate_ref
  13.7 3.6 %shard_map.41 = bf16[256,1280]{1,0:T(8,128)(2,1)} custom-call(s32[1]{0:T(128)} %bitcast.core_ref, s32[1,384]{1,0:T(1,128)} %broadcast_in_dim.5.mine_ref, s32[1,384]{1,0:T(1,128)} %reshape.30.mate_ref, f32[384,4096]{1,0:T(8,128)} %x_ref.2, f32[384,512]{1,0:T(8,128)S(1)} %collective-permute-done.1.y_ref), custom_call_target="tpu_custom_call" | custom-call | tf_op jit(solution)/shard_map/pallas_call | solution.py:96
  17.3 7.6 %all-to-all-start.1 = ((bf16[32,8,1280]{2,1,0:T(8,128)(2,1)}), bf16[32,8,1280]{2,1,0:T(8,128)(2,1)S(1)}, u32[]{:S(2)}, u32[]{:S(2)}) async-start(bf16[32,8,1280]{2,1,0:T(8,128)(2,1)} %bitcast.12), calls=%async_computation.1 | async-start | bytes 1310720 | tf_op jit(solution)/shard_map/all_to_all | solution.py:256
  24.8 0.0 collective-permute-done.2.y_ref
  24.9 13.0 %shard_map.42 = bf16[256,8960]{1,0:T(8,128)(2,1)} custom-call(s32[1]{0:T(128)} %bitcast.core_ref, s32[1,384]{1,0:T(1,128)} %broadcast_in_dim.5.mine_ref, s32[1,384]{1,0:T(1,128)} %reshape.30.mate_ref, f32[384,4096]{1,0:T(8,128)} %x_ref.2, f32[384,3584]{1,0:T(8,128)} %collective-permute-done.2.y_ref), custom_call_target="tpu_custom_call" | custom-call | tf_op jit(solution)/shard_map/pallas_call | solution.py:96
  37.8 5.0 %all-to-all-done.1 = bf16[32,8,1280]{2,1,0:T(8,128)(2,1)S(1)} async-done(((bf16[32,8,1280]{2,1,0:T(8,128)(2,1)}), bf16[32,8,1280]{2,1,0:T(8,128)(2,1)S(1)}, u32[]{:S(2)}, u32[]{:S(2)}) %all-to-all-start.1) | async-done | bytes 655392 | tf_op jit(solution)/shard_map/all_to_all | solution.py:256
  42.8 3.6 %all-to-all-start = ((bf16[32,8,8960]{2,1,0:T(8,128)(2,1)}), bf16[32,8,8960]{2,1,0:T(8,128)(2,1)}, u32[]{:S(2)}, u32[]{:S(2)}) async-start(bf16[32,8,8960]{2,1,0:T(8,128)(2,1)} %bitcast.11), calls=%async_computation | async-start | bytes 9175040 | tf_op jit(solution)/shard_map/all_to_all | solution.py:256
  46.4 0.2 convert_reduce_fusion
  46.7 1.8 %shard_map.43 = (f32[8,512]{1,0:T(8,128)}, f32[512,512]{1,0:T(8,128)}) custom-call(bf16[16,2,8,1280]{3,2,1,0:T(8,128)(2,1)S(1)} %bitcast.10), custom_call_target="tpu_custom_call" | custom-call | tf_op jit(solution)/shard_map/pallas_call | solution.py:226
  48.5 100.4 %all-to-all-done = bf16[32,8,8960]{2,1,0:T(8,128)(2,1)} async-done(((bf16[32,8,8960]{2,1,0:T(8,128)(2,1)}), bf16[32,8,8960]{2,1,0:T(8,128)(2,1)}, u32[]{:S(2)}, u32[]{:S(2)}) %all-to-all-start) | async-done | bytes 4587552 | tf_op jit(solution)/shard_map/all_to_all | solution.py:256
  148.8 9.1 %shard_map.44 = (f32[8,3584]{1,0:T(8,128)}, f32[32,128]{1,0:T(8,128)}) custom-call(bf16[16,2,8,8960]{3,2,1,0:T(8,128)(2,1)} %bitcast.2.refs_0_, f32[512,512]{1,0:T(8,128)} %get-tuple-element.16.refs_1_), custom_call_target="tpu_custom_call" | custom-call | tf_op jit(solution)/shard_map/pallas_call | solution.py:226
  158.0 3.8 %all-to-all-start.2 = ((f32[32,1,128]{2,1,0:T(1,128)}), f32[32,1,128]{2,1,0:T(1,128)S(1)}, u32[]{:S(2)}, u32[]{:S(2)}) async-start(f32[32,1,128]{2,1,0:T(1,128)} %bitcast.14), calls=%async_computation.2 | async-start | bytes 32768 | tf_op jit(solution)/shard_map/all_to_all | solution.py:263
  161.8 1.6 pad_maximum_fusion
  163.4 5.6 %all-to-all-done.2 = f32[32,1,128]{2,1,0:T(1,128)S(1)} async-done(((f32[32,1,128]{2,1,0:T(1,128)}), f32[32,1,128]{2,1,0:T(1,128)S(1)}, u32[]{:S(2)}, u32[]{:S(2)}) %all-to-all-start.2) | async-done | bytes 16416 | tf_op jit(solution)/shard_map/all_to_all | solution.py:263
  168.9 1.0 fusion
  (4 shorter events, 0.0 us)
Async XLA Ops:
  1.8 6.0 %copy-start = (s32[384]{0:T(512)S(1)}, s32[384]{0:T(512)}, u32[]{:S(2)}) copy-start(s32[384]{0:T(512)} %param.3) | copy-start | bytes 4612
  1.8 5.9 %collective-permute-start.1 = (f32[384,512]{1,0:T(8,128)S(1)}, f32[384,512]{1,0:T(8,128)S(1)}, u32[]{:S(2)}, u32[]{:S(2)}) collective-permute-start(f32[384,512]{1,0:T(8,128)S(1)} %slice.7), channel_id=1, source_target_pairs={{0,1},{1,0},{2,3},{3,2},{4,5},{5,4},{6,7},{7,6},{8,9},{9,8},{10,11... | collective-permute-start | bytes 2359304 | tf_op jit(solution)/shard_map/ppermute | solution.py:250
  7.7 17.1 %collective-permute-start.2 = (f32[384,3584]{1,0:T(8,128)}, f32[384,3584]{1,0:T(8,128)}, u32[]{:S(2)}, u32[]{:S(2)}) collective-permute-start(f32[384,3584]{1,0:T(8,128)} %slice.6), channel_id=1, source_target_pairs={{0,1},{1,0},{2,3},{3,2},{4,5},{5,4},{6,7},{7,6},{8,9},{9,8},{10,11... | collective-permute-start | bytes 16515080 | tf_op jit(solution)/shard_map/ppermute | solution.py:250
  7.8 5.3 %collective-permute-start = (s32[384]{0:T(512)S(1)}, s32[384]{0:T(512)S(1)}, u32[]{:S(2)}, u32[]{:S(2)}) collective-permute-start(s32[384]{0:T(512)S(1)} %copy-done), channel_id=1, source_target_pairs={{0,1},{1,0},{2,3},{3,2},{4,5},{5,4},{6,7},{7,6},{8,9},{9,8},{10,11... | collective-permute-start | bytes 4616 | tf_op jit(solution)/shard_map/ppermute | solution.py:244
  17.3 25.5 %all-to-all-start.1 = ((bf16[32,8,1280]{2,1,0:T(8,128)(2,1)}), bf16[32,8,1280]{2,1,0:T(8,128)(2,1)S(1)}, u32[]{:S(2)}, u32[]{:S(2)}) async-start(bf16[32,8,1280]{2,1,0:T(8,128)(2,1)} %bitcast.12), calls=%async_computation.1 | async-start | bytes 1310720 | tf_op jit(solution)/shard_map/all_to_all | solution.py:256
  42.8 106.1 %all-to-all-start = ((bf16[32,8,8960]{2,1,0:T(8,128)(2,1)}), bf16[32,8,8960]{2,1,0:T(8,128)(2,1)}, u32[]{:S(2)}, u32[]{:S(2)}) async-start(bf16[32,8,8960]{2,1,0:T(8,128)(2,1)} %bitcast.11), calls=%async_computation | async-start | bytes 9175040 | tf_op jit(solution)/shard_map/all_to_all | solution.py:256
  48.5 113.3 %copy-start.1 = (f32[8,512]{1,0:T(8,128)S(1)}, f32[8,512]{1,0:T(8,128)}, u32[]{:S(2)}) copy-start(f32[8,512]{1,0:T(8,128)} %get-tuple-element.18) | copy-start | bytes 49156
  158.0 11.0 %all-to-all-start.2 = ((f32[32,1,128]{2,1,0:T(1,128)}), f32[32,1,128]{2,1,0:T(1,128)S(1)}, u32[]{:S(2)}, u32[]{:S(2)}) async-start(f32[32,1,128]{2,1,0:T(1,128)} %bitcast.14), calls=%async_computation.2 | async-start | bytes 32768 | tf_op jit(solution)/shard_map/all_to_all | solution.py:263

commit v4 on v3

--- a/solution.py
+++ b/solution.py
@@ -2,16 +2,14 @@
 
 import jax
 import jax.numpy as jnp
-import numpy as np
 from jax import lax
 from jax.experimental import pallas as pl
 from jax.experimental.pallas import tpu as pltpu
 from jax.sharding import PartitionSpec as P
 
 CLUSTERS = 256
-TILE = 512
 LANES = 128
-PARTS = (512, 3584)
+PARTS = ((3584, 512, 512), (0, 3584, 1792))
 F32 = jnp.float32
 BF16 = jnp.bfloat16
 
@@ -34,7 +32,12 @@
     return jnp.sum(jnp.where(iota((n, n), 0) == iota((n, n), 1), row, 0), axis=1, keepdims=True)
 
 
-def code_kernel(core_ref, mine_ref, mate_ref, x_ref, y_ref, out_ref, sum_ref, own_ref, num_ref):
+def split(x):
+    high = x.astype(BF16)
+    return jnp.concatenate([high, (x - high.astype(F32)).astype(BF16)], axis=0)
+
+
+def code_kernel(core_ref, mine_ref, mate_ref, x_ref, y_ref, out_ref, own_ref, other_ref, num_ref):
     rows, tile = x_ref.shape
 
     @pl.when(pl.program_id(0) == 0)
@@ -43,71 +46,61 @@
         twin = (to_col(mine) == mine) & (iota((rows, rows), 0) < iota((rows, rows), 1))
         second = jnp.sum(twin.astype(F32), axis=0, keepdims=True) > 0.5
         member = iota((CLUSTERS, rows), 0) == mine
-        other = iota((CLUSTERS, rows), 0) == mate_ref[...]
-        sum_ref[:, :rows] = member.astype(F32).astype(BF16)
-        sum_ref[:, rows:] = other.astype(F32).astype(BF16)
-        own_ref[:CLUSTERS] = (member & ~second).astype(F32).astype(BF16)
-        own_ref[CLUSTERS:] = (member & second).astype(F32).astype(BF16)
+        other = (iota((CLUSTERS, rows), 0) == mate_ref[...]).astype(F32)
+        for k in range(2):
+            cols = slice(k * rows, (k + 1) * rows)
+            own_ref[:CLUSTERS, cols] = (member & ~second).astype(F32).astype(BF16)
+            own_ref[CLUSTERS:, cols] = (member & second).astype(F32).astype(BF16)
+            other_ref[:, cols] = other.astype(BF16)
         count = jnp.sum(member.astype(F32), axis=1, keepdims=True)
-        total = count + jnp.sum(other.astype(F32), axis=1, keepdims=True)
+        total = count + jnp.sum(other, axis=1, keepdims=True)
         num_ref[:CLUSTERS] = count
         num_ref[CLUSTERS:] = 1.0 / jnp.maximum(total, 1.0)
 
-    x = x_ref[...]
-    y = y_ref[...]
-    x_high = x.astype(BF16)
-    x_low = (x - x_high.astype(F32)).astype(BF16)
-    y_high = y.astype(BF16)
-    y_low = (y - y_high.astype(F32)).astype(BF16)
-    sums = mm(sum_ref[...], jnp.concatenate([x_high, y_high], axis=0))
-    sums += mm(sum_ref[...], jnp.concatenate([x_low, y_low], axis=0))
-    mean = sums * num_ref[CLUSTERS:]
-    high = mean.astype(BF16)
-    low = (mean - high.astype(F32)).astype(BF16)
+    own = mm(own_ref[...], split(x_ref[...]))
+    others = mm(other_ref[...], split(y_ref[...]))
     count = num_ref[:CLUSTERS]
 
     @pl.when(core_ref[0] == 0)
     def _():
-        own = mm(own_ref[...], x_high) + mm(own_ref[...], x_low)
+        mean = ((own[:CLUSTERS] + own[CLUSTERS:]) + others) * num_ref[CLUSTERS:]
+        low = (mean - mean.astype(BF16).astype(F32)).astype(BF16)
         out_ref[:, :tile] = jnp.where(count > 0.5, own[:CLUSTERS] - mean, jnp.inf).astype(BF16)
         out_ref[:, tile : 2 * tile] = jnp.where(count > 1.5, own[CLUSTERS:] - mean, jnp.inf).astype(BF16)
         out_ref[:, 2 * tile :] = low[:, : tile // 2]
 
     @pl.when(core_ref[0] == 1)
     def _():
-        own = mm(own_ref[CLUSTERS:], x_high) + mm(own_ref[CLUSTERS:], x_low)
+        mean = ((own[:CLUSTERS] + own[CLUSTERS:]) + others) * num_ref[CLUSTERS:]
+        high = mean.astype(BF16)
+        low = (mean - high.astype(F32)).astype(BF16)
         flag = jnp.where(count > 0.5, jnp.inf, -jnp.inf)
-        out_ref[:, :tile] = jnp.where(count > 1.5, own - mean, flag).astype(BF16)
+        out_ref[:, :tile] = jnp.where(count > 1.5, own[CLUSTERS:] - mean, flag).astype(BF16)
         out_ref[:, tile : 2 * tile] = high
         out_ref[:, 2 * tile :] = low[:, tile // 2 :]
 
 
-def code(core, mine, mate, x, y, start):
-    rows, width = y.shape
-    first = start // TILE
-    steps = width // TILE
-    wide = TILE * 5 // 2
+def code(core, mine, mate, x, y, start, width, tile):
+    rows = x.shape[0]
+    first = start // tile
+    steps = width // tile
+    wide = tile * 5 // 2
     line = pl.BlockSpec((1, rows), lambda t: (0, 0))
-    if steps == 1:
+    block = pl.BlockSpec((rows, tile), lambda t: (0, first + t))
+    if y.shape[1] == tile:
         y = pltpu.with_memory_space_constraint(y, pltpu.VMEM)
         y_spec = pl.BlockSpec(memory_space=pltpu.VMEM)
     else:
-        y_spec = pl.BlockSpec((rows, TILE), lambda t: (0, t))
+        y_spec = block
     return pl.pallas_call(
         code_kernel,
         grid=(steps,),
-        in_specs=[
-            pl.BlockSpec(memory_space=pltpu.SMEM),
-            line,
-            line,
-            pl.BlockSpec((rows, TILE), lambda t: (0, first + t)),
-            y_spec,
-        ],
+        in_specs=[pl.BlockSpec(memory_space=pltpu.SMEM), line, line, block, y_spec],
         out_specs=pl.BlockSpec((CLUSTERS, wide), lambda t: (0, t)),
         out_shape=jax.ShapeDtypeStruct((CLUSTERS, steps * wide), BF16),
         scratch_shapes=[
+            pltpu.VMEM((2 * CLUSTERS, 2 * rows), BF16),
             pltpu.VMEM((CLUSTERS, 2 * rows), BF16),
-            pltpu.VMEM((2 * CLUSTERS, rows), BF16),
             pltpu.VMEM((2 * CLUSTERS, 1), F32),
         ],
     )(core, mine, mate, x, y)
@@ -189,18 +182,18 @@
             )
 
 
-def compare(got, gram, cl_dev, width_all, last):
+def compare(got, gram, cl_dev, width_all, last, tile):
     first = gram is None
     slots = CLUSTERS // 2
-    wide = TILE * 5 // 2
-    width = got.shape[1] // wide * TILE
+    wide = tile * 5 // 2
+    width = got.shape[1] // wide * tile
     chips = slots // cl_dev
     got = got.reshape(chips, 2, cl_dev, got.shape[1])
     if cl_dev % 8:
         got = jnp.moveaxis(got, 1, 0).reshape(1, 2, slots, got.shape[3])
     fixed = lambda t: (0, 0)
     args = [got]
-    if width == TILE:
+    if width == tile:
         args = [pltpu.with_memory_space_constraint(got, pltpu.VMEM)]
         specs = [pl.BlockSpec(memory_space=pltpu.VMEM)]
     else:
@@ -210,7 +203,7 @@
         args.append(gram)
         specs.append(pl.BlockSpec(square, fixed))
     out_shape = [jax.ShapeDtypeStruct((cl_dev, width), F32)]
-    out_specs = [pl.BlockSpec((cl_dev, TILE), lambda t: (0, t))]
+    out_specs = [pl.BlockSpec((cl_dev, tile), lambda t: (0, t))]
     scratch = [
         pltpu.VMEM((slots, slots), BF16),
         pltpu.VMEM((slots, 1), F32),
@@ -225,7 +218,7 @@
         out_specs.append(pl.BlockSpec(square, fixed))
     return pl.pallas_call(
         functools.partial(compare_kernel, cl_dev, width_all, first, last),
-        grid=(width // TILE,),
+        grid=(width // tile,),
         in_specs=specs,
         out_specs=out_specs,
         out_shape=out_shape,
@@ -242,23 +235,19 @@
     exchange = functools.partial(lax.all_to_all, axis_name="rows", split_axis=0, concat_axis=0, tiled=True)
     swap = functools.partial(lax.ppermute, axis_name="rows", perm=[(i, i ^ 1) for i in range(dev_count)])
     mate = swap(assignment).reshape(1, rows)
-    others = []
-    for part, end in zip(PARTS, np.cumsum(PARTS)):
-        piece = embeddings[:, end - part : end]
-        if others:
-            piece, others[-1] = lax.optimization_barrier((piece, others[-1]))
-        others.append(swap(piece))
+    first, part, _ = PARTS[0]
+    head = swap(embeddings[:, first : first + part])
+    whole, head, mate = lax.optimization_barrier((embeddings, head, mate))
+    tail = swap(whole)
     got = []
-    start = 0
-    for i, part in enumerate(PARTS):
-        coded = code(core, mine, mate, embeddings, others[i], start)
+    for start, part, tile in PARTS:
+        coded = code(core, mine, mate, embeddings, tail if got else head, start, part, tile)
         coded, embeddings = lax.optimization_barrier((coded, embeddings))
         got.append(exchange(coded))
-        start += part
     gram = None
     centroids = []
-    for i, piece in enumerate(got):
-        c, gram = compare(piece, gram, cl_dev, width, i == len(got) - 1)
+    for i, (_, _, tile) in enumerate(PARTS):
+        c, gram = compare(got[i], gram, cl_dev, width, i == len(got) - 1, tile)
         centroids.append(c)
     found = exchange(gram)
     row_ids = jnp.arange(rows, dtype=jnp.int32)
@@ -270,7 +259,7 @@
         owner.astype(F32), found, (((1,), (0,)), ((), ())), precision=lax.Precision.HIGHEST
     )
     maxima = jnp.sum(jnp.where(lane, lines, 0.0), axis=1)
-    return (maxima, jnp.concatenate(centroids, axis=1))
+    return (maxima, jnp.concatenate(centroids[::-1], axis=1))
 
 
 def solution(mesh):

time: 171 us -> 160 us (0.936)
  Pallas kernels: 27.5 us -> 22.3 us
  local copies, waits for them, and re-layouts: 7.7 us -> 3 us
    slice x2 -> x1, local copies, waits for them, and re-layouts: 6.56 us -> 1.19 us  [on_device(): head = swap(embeddings[:, first:first + part])]
    pallas_call x2, Pallas kernels: 16.5 us -> 13.9 us  [code(): pl.pallas_call(code_kernel, grid=(steps,), in_specs=[pl.BlockSpec(memory_...]
    pallas_call x2, Pallas kernels: 10.9 us -> 8.39 us  [compare(): pl.pallas_call(functools.partial(compare_kernel, cl_dev, width_all, first...]
    ppermute x1, waiting for transfers between devices: 4.33 us -> 1.96 us  [on_device(): mate = swap(assignment).reshape(1, rows)]
    all_to_all x2, waiting for transfers between devices: 105 us -> 108 us  [on_device(): got.append(exchange(coded))]
  transfers between devices with their start and end apart: 6 -> 6, of which waited for: 4 -> 4; matrix products, arithmetic and copies ran while one was open for 5% -> 2% of each run, Pallas kernels for 11% -> 10%
where the time goes in v4:
time: 160 us; the launch traced here: 159 us
  waiting for transfers between devices  115 us (72%)
  Pallas kernels  22.3 us (14%)
  starting transfers between devices  15.4 us (10%)
  local copies, waits for them, and re-layouts  3 us (2%)
  other arithmetic  1.82 us (1%)
    all_to_all x2, waiting for transfers between devices, on_device(): got.append(exchange(coded))  108 us
    pallas_call x2, Pallas kernels, code(): pl.pallas_call(code_kernel, grid=(steps,), in_specs=[pl.BlockSpec(memory_...  13.9 us
    all_to_all x2, starting transfers between devices, on_device(): got.append(exchange(coded))  10.8 us
    pallas_call x2, Pallas kernels, compare(): pl.pallas_call(functools.partial(compare_kernel, cl_dev, width_all, first...  8.39 us
    all_to_all x1, waiting for transfers between devices, on_device(): found = exchange(gram)  5.56 us
    all_to_all x1, starting transfers between devices, on_device(): found = exchange(gram)  3.83 us
  transfers between devices with their start and end apart: 6, of which 4 were waited for; matrix products, arithmetic and copies ran while one was open for 2% of the time, Pallas kernels for 10%

profile of v4, /device:TPU:0, one launch (start us, length us, event | category | flops | bytes accessed | tf_op | source)
XLA Modules:
  0.0 159.3 jit_solution(12549260273563496493)
XLA Ops:
  0.6 1.2 slice.3
  1.8 0.5 collective-permute-start
  2.3 0.1 collective-permute-start.1
  2.4 2.0 %collective-permute-done.1 = s32[384]{0:T(512)S(1)} collective-permute-done((s32[384]{0:T(512)}, s32[384]{0:T(512)S(1)}, u32[]{:S(2)}, u32[]{:S(2)}) %collective-permute-start.1) | collective-permute-done | bytes 1568 | tf_op jit(solution)/shard_map/ppermute | solution.py:237
  4.4 0.6 reshape.30.mate_ref
  4.9 0.0 collective-permute-done.y_ref
  4.9 0.1 collective-permute-start.2
  5.1 1.2 broadcast_in_dim.5.mine_ref
  6.3 3.3 %shard_map.41 = bf16[256,1280]{1,0:T(8,128)(2,1)} custom-call(s32[1]{0:T(128)} %bitcast.core_ref, s32[1,384]{1,0:T(1,128)} %broadcast_in_dim.5.mine_ref, s32[1,384]{1,0:T(1,128)} %reshape.30.mate_ref, f32[384,4096]{1,0:T(8,128)} %x_ref.2, f32[384,512]{1,0:T(8,128)S(1)} %collective-permute-done.y_ref), custom_call_target="tpu_custom_call" | custom-call | tf_op jit(solution)/shard_map/pallas_call | solution.py:95
  9.6 7.2 %all-to-all-start.1 = ((bf16[32,8,1280]{2,1,0:T(8,128)(2,1)}), bf16[32,8,1280]{2,1,0:T(8,128)(2,1)S(1)}, u32[]{:S(2)}, u32[]{:S(2)}) async-start(bf16[32,8,1280]{2,1,0:T(8,128)(2,1)} %bitcast.12), calls=%async_computation.1 | async-start | bytes 1310720 | tf_op jit(solution)/shard_map/all_to_all | solution.py:246
  16.8 0.0 collective-permute-done.2.y_ref
  16.8 10.6 %shard_map.42 = bf16[256,8960]{1,0:T(8,128)(2,1)} custom-call(s32[1]{0:T(128)} %bitcast.core_ref, s32[1,384]{1,0:T(1,128)} %broadcast_in_dim.5.mine_ref, s32[1,384]{1,0:T(1,128)} %reshape.30.mate_ref, f32[384,4096]{1,0:T(8,128)} %x_ref.2, f32[384,4096]{1,0:T(8,128)} %collective-permute-done.2.y_ref), custom_call_target="tpu_custom_call" | custom-call | tf_op jit(solution)/shard_map/pallas_call | solution.py:95
  27.5 0.0 copy-start
  27.5 7.3 %all-to-all-done.1 = bf16[32,8,1280]{2,1,0:T(8,128)(2,1)S(1)} async-done(((bf16[32,8,1280]{2,1,0:T(8,128)(2,1)}), bf16[32,8,1280]{2,1,0:T(8,128)(2,1)S(1)}, u32[]{:S(2)}, u32[]{:S(2)}) %all-to-all-start.1) | async-done | bytes 655392 | tf_op jit(solution)/shard_map/all_to_all | solution.py:246
  34.7 3.6 %all-to-all-start = ((bf16[32,8,8960]{2,1,0:T(8,128)(2,1)}), bf16[32,8,8960]{2,1,0:T(8,128)(2,1)}, u32[]{:S(2)}, u32[]{:S(2)}) async-start(bf16[32,8,8960]{2,1,0:T(8,128)(2,1)} %bitcast.11), calls=%async_computation | async-start | bytes 9175040 | tf_op jit(solution)/shard_map/all_to_all | solution.py:246
  38.4 0.0 copy-done
  38.4 0.2 convert_reduce_fusion
  38.6 1.9 %shard_map.43 = (f32[8,512]{1,0:T(8,128)}, f32[512,512]{1,0:T(8,128)}) custom-call(bf16[16,2,8,1280]{3,2,1,0:T(8,128)(2,1)S(1)} %bitcast.10), custom_call_target="tpu_custom_call" | custom-call | tf_op jit(solution)/shard_map/pallas_call | solution.py:219
  40.5 100.3 %all-to-all-done = bf16[32,8,8960]{2,1,0:T(8,128)(2,1)} async-done(((bf16[32,8,8960]{2,1,0:T(8,128)(2,1)}), bf16[32,8,8960]{2,1,0:T(8,128)(2,1)}, u32[]{:S(2)}, u32[]{:S(2)}) %all-to-all-start) | async-done | bytes 4587552 | tf_op jit(solution)/shard_map/all_to_all | solution.py:246
  140.8 6.5 %shard_map.44 = (f32[8,3584]{1,0:T(8,128)}, f32[32,128]{1,0:T(8,128)}) custom-call(bf16[16,2,8,8960]{3,2,1,0:T(8,128)(2,1)} %bitcast.2.refs_0_, f32[512,512]{1,0:T(8,128)} %get-tuple-element.18.refs_1_), custom_call_target="tpu_custom_call" | custom-call | tf_op jit(solution)/shard_map/pallas_call | solution.py:219
  147.3 3.8 %all-to-all-start.2 = ((f32[32,1,128]{2,1,0:T(1,128)}), f32[32,1,128]{2,1,0:T(1,128)S(1)}, u32[]{:S(2)}, u32[]{:S(2)}) async-start(f32[32,1,128]{2,1,0:T(1,128)} %bitcast.14), calls=%async_computation.2 | async-start | bytes 32768 | tf_op jit(solution)/shard_map/all_to_all | solution.py:252
  151.2 1.6 pad_maximum_fusion
  152.7 5.6 %all-to-all-done.2 = f32[32,1,128]{2,1,0:T(1,128)S(1)} async-done(((f32[32,1,128]{2,1,0:T(1,128)}), f32[32,1,128]{2,1,0:T(1,128)S(1)}, u32[]{:S(2)}, u32[]{:S(2)}) %all-to-all-start.2) | async-done | bytes 16416 | tf_op jit(solution)/shard_map/all_to_all | solution.py:252
  158.3 1.0 fusion
  (1 shorter events, 0.0 us)
Async XLA Ops:
  1.8 3.1 %collective-permute-start = (f32[384,512]{1,0:T(8,128)S(1)}, f32[384,512]{1,0:T(8,128)S(1)}, u32[]{:S(2)}, u32[]{:S(2)}) collective-permute-start(f32[384,512]{1,0:T(8,128)S(1)} %slice.3), channel_id=1, source_target_pairs={{0,1},{1,0},{2,3},{3,2},{4,5},{5,4},{6,7},{7,6},{8,9},{9,8},{10,11... | collective-permute-start | bytes 2359304 | tf_op jit(solution)/shard_map/ppermute | solution.py:239
  2.3 2.0 %collective-permute-start.1 = (s32[384]{0:T(512)}, s32[384]{0:T(512)S(1)}, u32[]{:S(2)}, u32[]{:S(2)}) collective-permute-start(s32[384]{0:T(512)} %param.3), channel_id=1, source_target_pairs={{0,1},{1,0},{2,3},{3,2},{4,5},{5,4},{6,7},{7,6},{8,9},{9,8},{10,11... | collective-permute-start | bytes 4616 | tf_op jit(solution)/shard_map/ppermute | solution.py:237
  4.9 11.9 %collective-permute-start.2 = (f32[384,4096]{1,0:T(8,128)}, f32[384,4096]{1,0:T(8,128)}, u32[]{:S(2)}, u32[]{:S(2)}) collective-permute-start(f32[384,4096]{1,0:T(8,128)} %x_ref.2), channel_id=1, source_target_pairs={{0,1},{1,0},{2,3},{3,2},{4,5},{5,4},{6,7},{7,6},{8,9},{9,8},{10,11... | collective-permute-start | bytes 18874376 | tf_op jit(solution)/shard_map/ppermute | solution.py:241
  9.6 25.1 %all-to-all-start.1 = ((bf16[32,8,1280]{2,1,0:T(8,128)(2,1)}), bf16[32,8,1280]{2,1,0:T(8,128)(2,1)S(1)}, u32[]{:S(2)}, u32[]{:S(2)}) async-start(bf16[32,8,1280]{2,1,0:T(8,128)(2,1)} %bitcast.12), calls=%async_computation.1 | async-start | bytes 1310720 | tf_op jit(solution)/shard_map/all_to_all | solution.py:246
  27.5 10.9 %copy-start = (s32[384]{0:T(512)S(1)}, s32[384]{0:T(512)}, u32[]{:S(2)}) copy-start(s32[384]{0:T(512)} %param.3) | copy-start | bytes 4612
  34.7 106.1 %all-to-all-start = ((bf16[32,8,8960]{2,1,0:T(8,128)(2,1)}), bf16[32,8,8960]{2,1,0:T(8,128)(2,1)}, u32[]{:S(2)}, u32[]{:S(2)}) async-start(bf16[32,8,8960]{2,1,0:T(8,128)(2,1)} %bitcast.11), calls=%async_computation | async-start | bytes 9175040 | tf_op jit(solution)/shard_map/all_to_all | solution.py:246
  147.3 11.0 %all-to-all-start.2 = ((f32[32,1,128]{2,1,0:T(1,128)}), f32[32,1,128]{2,1,0:T(1,128)S(1)}, u32[]{:S(2)}, u32[]{:S(2)}) async-start(f32[32,1,128]{2,1,0:T(1,128)} %bitcast.14), calls=%async_computation.2 | async-start | bytes 32768 | tf_op jit(solution)/shard_map/all_to_all | solution.py:252

commit v5 on v4

v5 whole, which is shorter than its diff:
```python
import functools

import jax
import jax.numpy as jnp
from jax import lax
from jax.experimental import pallas as pl
from jax.experimental.pallas import tpu as pltpu
from jax.sharding import PartitionSpec as P

CLUSTERS = 256
LANES = 128
PARTS = ((3840, 256, 128), (0, 3840, 640))
F32 = jnp.float32
BF16 = jnp.bfloat16


def iota(shape, axis):
    return lax.broadcasted_iota(jnp.int32, shape, axis)


def mm(a, b):
    return lax.dot_general(a, b, (((1,), (0,)), ((), ())), preferred_element_type=F32)


def to_row(col):
    n = col.shape[0]
    return jnp.sum(jnp.where(iota((n, n), 0) == iota((n, n), 1), col, 0), axis=0, keepdims=True)


def to_col(row):
    n = row.shape[1]
    return jnp.sum(jnp.where(iota((n, n), 0) == iota((n, n), 1), row, 0), axis=1, keepdims=True)


def split(x):
    high = x.astype(BF16)
    return jnp.concatenate([high, (x - high.astype(F32)).astype(BF16)], axis=0)


def code_kernel(core_ref, mine_ref, mate_ref, x_ref, y_ref, out_ref, pick0_ref, pick1_ref, num_ref):
    rows, tile = x_ref.shape
    core = core_ref[0]

    @pl.when(pl.program_id(0) == 0)
    def _():
        mine = mine_ref[...].reshape(1, rows)
        mate = mate_ref[...].reshape(1, rows)
        counts = []
        for k, pick_ref in enumerate((pick0_ref, pick1_ref)):
            ids = jnp.where(core == k, mine, mate)
            twin = (to_col(ids) == ids) & (iota((rows, rows), 0) < iota((rows, rows), 1))
            second = jnp.sum(twin.astype(F32), axis=0, keepdims=True) > 0.5
            member = iota((CLUSTERS, rows), 0) == ids
            upper = member & ~second if k == 0 else member
            for j in range(2):
                cols = slice(j * rows, (j + 1) * rows)
                pick_ref[:CLUSTERS, cols] = upper.astype(F32).astype(BF16)
                pick_ref[CLUSTERS:, cols] = (member & second).astype(F32).astype(BF16)
            counts.append(jnp.sum(member.astype(F32), axis=1, keepdims=True))
        num_ref[:CLUSTERS] = counts[0]
        num_ref[CLUSTERS : 2 * CLUSTERS] = counts[1]
        num_ref[2 * CLUSTERS :] = 1.0 / jnp.maximum(counts[0] + counts[1], 1.0)

    def body(x0_ref, x1_ref):
        rows0 = mm(pick0_ref[...], split(x0_ref[...]))
        rows1 = mm(pick1_ref[...], split(x1_ref[...]))
        count0 = num_ref[:CLUSTERS]
        count1 = num_ref[CLUSTERS : 2 * CLUSTERS]
        row0 = rows0[:CLUSTERS]
        row1 = rows0[CLUSTERS:]
        row3 = rows1[CLUSTERS:]
        mean = ((row0 + row1) + rows1[:CLUSTERS]) * num_ref[2 * CLUSTERS :]
        high = mean.astype(BF16)
        flag = jnp.where(count1 > 0.5, jnp.inf, -jnp.inf)
        out_ref[:, :tile] = jnp.where(count0 > 0.5, row0 - mean, jnp.inf).astype(BF16)
        out_ref[:, tile : 2 * tile] = jnp.where(count0 > 1.5, row1 - mean, jnp.inf).astype(BF16)
        out_ref[:, 2 * tile : 3 * tile] = jnp.where(count1 > 1.5, row3 - mean, flag).astype(BF16)
        out_ref[:, 3 * tile : 4 * tile] = high
        out_ref[:, 4 * tile :] = (mean - high.astype(F32)).astype(BF16)

    @pl.when(core == 0)
    def _():
        body(x_ref, y_ref)

    @pl.when(core == 1)
    def _():
        body(y_ref, x_ref)


def code(core, mine, mate, x, y, start, width, tile):
    rows = x.shape[0]
    first = start // tile
    steps = width // 2 // tile
    line = pl.BlockSpec((rows,), lambda t, core: (0,))
    block = pl.BlockSpec((rows, tile), lambda t, core: (0, first + core[0] * steps + t))
    if y.shape[1] == tile:
        y = pltpu.with_memory_space_constraint(y, pltpu.VMEM)
        y_spec = pl.BlockSpec(memory_space=pltpu.VMEM)
    else:
        y_spec = block
    return pl.pallas_call(
        code_kernel,
        grid_spec=pltpu.PrefetchScalarGridSpec(
            num_scalar_prefetch=1,
            grid=(steps,),
            in_specs=[line, pl.BlockSpec(memory_space=pltpu.VMEM), block, y_spec],
            out_specs=pl.BlockSpec((CLUSTERS, 5 * tile), lambda t, core: (0, t)),
            scratch_shapes=[
                pltpu.VMEM((2 * CLUSTERS, 2 * rows), BF16),
                pltpu.VMEM((2 * CLUSTERS, 2 * rows), BF16),
                pltpu.VMEM((3 * CLUSTERS, 1), F32),
            ],
        ),
        out_shape=jax.ShapeDtypeStruct((CLUSTERS, steps * 5 * tile), BF16),
    )(core, mine, pltpu.with_memory_space_constraint(mate, pltpu.VMEM), x, y)


def compare_kernel(cl_dev, width_all, first, last, *refs):
    refs = list(refs)
    got_ref = refs.pop(0)
    gram_in_ref = None if first else refs.pop(0)
    centroid_refs = [refs.pop(0), refs.pop(0)]
    best_ref = refs.pop(0) if last else None
    gram_ref, mix_ref, total_ref, live_ref = refs
    slots = mix_ref.shape[0]
    tile = centroid_refs[0].shape[1]

    def part(core, lo, hi):
        return got_ref[:, core, :, lo:hi].astype(F32).reshape(slots, hi - lo)

    @pl.when(pl.program_id(0) == 0)
    def _():
        gram_ref[...] = jnp.zeros_like(gram_ref) if first else gram_in_ref[...]
        mark = part(0, 2 * tile, 2 * tile + LANES)[:, :1]
        live = [
            part(0, 0, LANES)[:, :1] < jnp.inf,
            part(0, tile, tile + LANES)[:, :1] < jnp.inf,
            mark > -jnp.inf,
            jnp.abs(mark) < jnp.inf,
        ]
        live = [x.astype(F32) for x in live]
        for k in range(4):
            live_ref[k * slots : (k + 1) * slots] = live[k]
        same = (iota((slots, slots), 0) % cl_dev) == (iota((slots, slots), 1) % cl_dev)
        mix = jnp.where(same, to_row(live[0] + live[1] + live[2] + live[3]), 0.0)
        mix_ref[...] = mix.astype(BF16)
        total_ref[...] = 1.0 / jnp.sum(mix, axis=1, keepdims=True)

    live = [live_ref[k * slots : (k + 1) * slots] > 0.5 for k in range(4)]
    mix = mix_ref[...]
    scale = total_ref[...]
    gram = gram_ref[...]
    for core in range(2):
        d0 = jnp.where(live[0], part(core, 0, tile), 0.0)
        d1 = jnp.where(live[1], part(core, tile, 2 * tile), 0.0)
        d3 = jnp.where(live[3], part(core, 2 * tile, 3 * tile), 0.0)
        d2 = jnp.where(live[2], -(d0 + d1 + d3), 0.0)
        high = part(core, 3 * tile, 4 * tile)
        low = part(core, 4 * tile, 5 * tile)
        centroid = (mm(mix, high.astype(BF16)) + mm(mix, low.astype(BF16))) * scale
        centroid_refs[core][...] = centroid[:cl_dev]
        away = (high - centroid) + low
        every = jnp.concatenate([away + d0, away + d1, away + d2, away + d3], axis=0).astype(BF16)
        gram += lax.dot_general(every, every, (((1,), (1,)), ((), ())), preferred_element_type=F32)
    gram_ref[...] = gram

    if last:

        @pl.when(pl.program_id(0) == pl.num_programs(0) - 1)
        def _():
            n = 4 * slots
            gram = gram_ref[...]
            row = iota((n, n), 0)
            col = iota((n, n), 1)
            diag = jnp.where(row == col, gram, 0.0)
            inv_row = lax.rsqrt(jnp.sum(diag, axis=0, keepdims=True) / width_all + 1e-6)
            inv_col = lax.rsqrt(jnp.sum(diag, axis=1, keepdims=True) / width_all + 1e-6)
            score = gram * inv_col * inv_row / width_all
            usable = ((row % cl_dev) == (col % cl_dev)) & (row != col) & (live_ref[...] > 0.5)
            best = jnp.max(jnp.where(usable, score, -1.0), axis=0, keepdims=True)
            sources = 2 * slots // cl_dev
            place = iota((sources, n), 1)
            source = (place % slots) // cl_dev * 2 + place // (2 * slots)
            spread = jnp.where(source == iota((sources, n), 0), best, 0.0)
            place = iota((n, LANES), 0)
            lane = (place // slots) % 2 * cl_dev + place % cl_dev
            pick = (lane == iota((n, LANES), 1)).astype(F32)
            best_ref[...] = lax.dot_general(
                spread,
                pick,
                (((1,), (0,)), ((), ())),
                precision=lax.Precision.HIGHEST,
                preferred_element_type=F32,
            )


def compare(got, gram, cl_dev, width_all, last, tile):
    first = gram is None
    slots = CLUSTERS // 2
    half = got.shape[1] // 5
    chips = slots // cl_dev
    got = got.reshape(chips, 2, cl_dev, got.shape[1])
    if cl_dev % 8:
        got = jnp.moveaxis(got, 1, 0).reshape(1, 2, slots, got.shape[3])
    fixed = lambda t: (0, 0)
    args = [got]
    if half == tile:
        args = [pltpu.with_memory_space_constraint(got, pltpu.VMEM)]
        specs = [pl.BlockSpec(memory_space=pltpu.VMEM)]
    else:
        specs = [pl.BlockSpec((*got.shape[:3], 5 * tile), lambda t: (0, 0, 0, t))]
    square = (4 * slots, 4 * slots)
    if not first:
        args.append(gram)
        specs.append(pl.BlockSpec(square, fixed))
    out_shape = [jax.ShapeDtypeStruct((cl_dev, half), F32)] * 2
    out_specs = [pl.BlockSpec((cl_dev, tile), lambda t: (0, t))] * 2
    scratch = [
        pltpu.VMEM((slots, slots), BF16),
        pltpu.VMEM((slots, 1), F32),
        pltpu.VMEM((4 * slots, 1), F32),
    ]
    if last:
        out_shape.append(jax.ShapeDtypeStruct((2 * chips, LANES), F32))
        out_specs.append(pl.BlockSpec((2 * chips, LANES), fixed))
        scratch.insert(0, pltpu.VMEM(square, F32))
    else:
        out_shape.append(jax.ShapeDtypeStruct(square, F32))
        out_specs.append(pl.BlockSpec(square, fixed))
    return pl.pallas_call(
        functools.partial(compare_kernel, cl_dev, width_all, first, last),
        grid=(half // tile,),
        in_specs=specs,
        out_specs=out_specs,
        out_shape=out_shape,
        scratch_shapes=scratch,
    )(*args)


def on_device(embeddings, assignment):
    dev_count = lax.axis_size("rows")
    cl_dev = CLUSTERS // dev_count
    rows, width = embeddings.shape
    core = lax.axis_index("rows") % 2
    exchange = functools.partial(lax.all_to_all, axis_name="rows", split_axis=0, concat_axis=0, tiled=True)
    swap = functools.partial(lax.ppermute, axis_name="rows", perm=[(i, i ^ 1) for i in range(dev_count)])
    mate = swap(assignment)
    first, part, _ = PARTS[0]
    half = part // 2
    head = swap(lax.dynamic_slice_in_dim(embeddings, first + (1 - core) * half, half, 1))
    whole, head, mate = lax.optimization_barrier((embeddings, head, mate))
    tail = swap(whole)
    got = []
    for start, part, tile in PARTS:
        coded = code(core.astype(jnp.int32).reshape(1), assignment, mate, embeddings, tail if got else head, start, part, tile)
        coded, embeddings = lax.optimization_barrier((coded, embeddings))
        got.append(exchange(coded))
    gram = None
    centroids = []
    for i, (_, _, tile) in enumerate(PARTS):
        *c, gram = compare(got[i], gram, cl_dev, width, i == len(got) - 1, tile)
        centroids = c + centroids
    found = exchange(gram)
    row_ids = jnp.arange(rows, dtype=jnp.int32)
    twin = (assignment[:, None] == assignment[None, :]) & (row_ids[None, :] < row_ids[:, None])
    second = jnp.sum(twin.astype(jnp.int32), axis=1)
    owner = (assignment // cl_dev)[:, None] == jnp.arange(dev_count, dtype=jnp.int32)[None, :]
    lane = (second * cl_dev + assignment % cl_dev)[:, None] == jnp.arange(LANES, dtype=jnp.int32)[None, :]
    lines = lax.dot_general(
        owner.astype(F32), found, (((1,), (0,)), ((), ())), precision=lax.Precision.HIGHEST
    )
    maxima = jnp.sum(jnp.where(lane, lines, 0.0), axis=1)
    return (maxima, jnp.concatenate(centroids, axis=1))


def solution(mesh):
    placed = (P(("group", "rows"), None), P(("group", "rows")))
    return jax.shard_map(
        on_device,
        mesh=mesh,
        in_specs=placed,
        out_specs=(P(("group", "rows")), P(("group", "rows"), None)),
        check_vma=False,
    )
```

time: 160 us -> 160 us (level)
  waiting for transfers between devices: 115 us -> 118 us
  local copies, waits for them, and re-layouts: 3 us -> 0.95 us
    all_to_all x2, waiting for transfers between devices: 108 us -> 111 us  [on_device(): got.append(exchange(coded))]
    pallas_call x2, Pallas kernels: 13.9 us -> 11.2 us  [code(): pl.pallas_call(code_kernel, grid_spec=pltpu.PrefetchScalarGridSpec(num_sc...]
    pallas_call x2, Pallas kernels: 8.39 us -> 10.1 us  [compare(): pl.pallas_call(functools.partial(compare_kernel, cl_dev, width_all, first...]
  transfers between devices with their start and end apart: 6 -> 6, of which waited for: 4 -> 5; matrix products, arithmetic and copies ran while one was open for 2% -> 1% of each run, Pallas kernels for 10% -> 8%
where the time goes in v5:
time: 160 us; the launch traced here: 159 us
  waiting for transfers between devices  118 us (74%)
  Pallas kernels  21.3 us (13%)
  starting transfers between devices  15.6 us (10%)
  other arithmetic  1.78 us (1%)
    all_to_all x2, waiting for transfers between devices, on_device(): got.append(exchange(coded))  111 us
    pallas_call x2, Pallas kernels, code(): pl.pallas_call(code_kernel, grid_spec=pltpu.PrefetchScalarGridSpec(num_sc...  11.2 us
    all_to_all x2, starting transfers between devices, on_device(): got.append(exchange(coded))  11 us
    pallas_call x2, Pallas kernels, compare(): pl.pallas_call(functools.partial(compare_kernel, cl_dev, width_all, first...  10.1 us
    all_to_all x1, waiting for transfers between devices, on_device(): found = exchange(gram)  5.62 us
    all_to_all x1, starting transfers between devices, on_device(): found = exchange(gram)  3.69 us
  transfers between devices with their start and end apart: 6, of which 5 were waited for; matrix products, arithmetic and copies ran while one was open for 1% of the time, Pallas kernels for 8%

profile of v5, /device:TPU:0, one launch (start us, length us, event | category | flops | bytes accessed | tf_op | source)
XLA Modules:
  0.0 159.2 jit_solution(15260779145252832658)
XLA Ops:
  0.6 0.9 constant_dynamic-slice_fusion
  1.6 0.5 collective-permute-start
  2.1 0.1 collective-permute-start.1
  2.2 1.3 collective-permute-done.1.mate_ref
  3.5 0.0 collective-permute-done.y_ref
  3.5 0.3 collective-permute-start.2
  3.8 2.8 %shard_map.41 = bf16[256,640]{1,0:T(8,128)(2,1)} custom-call(s32[1]{0:T(128)} %bitcast.core_ref, s32[384]{0:T(512)} %mine_ref.3, s32[384]{0:T(512)S(1)} %collective-permute-done.1.mate_ref, f32[384,4096]{1,0:T(8,128)} %x_ref.2, f32[384,128]{1,0:T(8,128)S(1)} %collective-permute-done.y_ref), custom_call_target="tpu_custom_call" | custom-call | tf_op jit(solution)/shard_map/pallas_call | solution.py:101
  6.6 7.1 %all-to-all-start.1 = ((bf16[32,8,640]{2,1,0:T(8,128)(2,1)}), bf16[32,8,640]{2,1,0:T(8,128)(2,1)S(1)}, u32[]{:S(2)}, u32[]{:S(2)}) async-start(bf16[32,8,640]{2,1,0:T(8,128)(2,1)} %bitcast.12), calls=%async_computation.1 | async-start | bytes 655360 | tf_op jit(solution)/shard_map/all_to_all | solution.py:257
  13.7 0.3 collective-permute-done.2.y_ref
  14.0 8.4 %shard_map.42 = bf16[256,9600]{1,0:T(8,128)(2,1)} custom-call(s32[1]{0:T(128)} %bitcast.core_ref, s32[384]{0:T(512)} %mine_ref.3, s32[384]{0:T(512)S(1)} %collective-permute-done.1.mate_ref, f32[384,4096]{1,0:T(8,128)} %x_ref.2, f32[384,4096]{1,0:T(8,128)} %collective-permute-done.2.y_ref), custom_call_target="tpu_custom_call" | custom-call | tf_op jit(solution)/shard_map/pallas_call | solution.py:101
  22.3 0.0 copy-start
  22.4 3.3 %all-to-all-done.1 = bf16[32,8,640]{2,1,0:T(8,128)(2,1)S(1)} async-done(((bf16[32,8,640]{2,1,0:T(8,128)(2,1)}), bf16[32,8,640]{2,1,0:T(8,128)(2,1)S(1)}, u32[]{:S(2)}, u32[]{:S(2)}) %all-to-all-start.1) | async-done | bytes 327712 | tf_op jit(solution)/shard_map/all_to_all | solution.py:257
  25.7 3.9 %all-to-all-start = ((bf16[32,8,9600]{2,1,0:T(8,128)(2,1)}), bf16[32,8,9600]{2,1,0:T(8,128)(2,1)}, u32[]{:S(2)}, u32[]{:S(2)}) async-start(bf16[32,8,9600]{2,1,0:T(8,128)(2,1)} %bitcast.11), calls=%async_computation | async-start | bytes 9830400 | tf_op jit(solution)/shard_map/all_to_all | solution.py:257
  29.6 0.0 copy-done
  29.6 0.2 convert_reduce_fusion
  29.9 1.9 %shard_map.43 = (f32[8,128]{1,0:T(8,128)}, f32[8,128]{1,0:T(8,128)}, f32[512,512]{1,0:T(8,128)}) custom-call(bf16[16,2,8,640]{3,2,1,0:T(8,128)(2,1)S(1)} %bitcast.10), custom_call_target="tpu_custom_call" | custom-call | tf_op jit(solution)/shard_map/pallas_call | solution.py:230
  31.8 107.4 %all-to-all-done = bf16[32,8,9600]{2,1,0:T(8,128)(2,1)} async-done(((bf16[32,8,9600]{2,1,0:T(8,128)(2,1)}), bf16[32,8,9600]{2,1,0:T(8,128)(2,1)}, u32[]{:S(2)}, u32[]{:S(2)}) %all-to-all-start) | async-done | bytes 4915232 | tf_op jit(solution)/shard_map/all_to_all | solution.py:257
  139.2 8.2 %shard_map.44 = (f32[8,1920]{1,0:T(8,128)}, f32[8,1920]{1,0:T(8,128)}, f32[32,128]{1,0:T(8,128)}) custom-call(bf16[16,2,8,9600]{3,2,1,0:T(8,128)(2,1)} %bitcast.2.refs_0_, f32[512,512]{1,0:T(8,128)} %get-tuple-element.20.refs_1_), custom_call_target="tpu_custom_call" | custom-call | tf_op jit(solution)/shard_map/pallas_call | solution.py:230
  147.4 3.7 %all-to-all-start.2 = ((f32[32,1,128]{2,1,0:T(1,128)}), f32[32,1,128]{2,1,0:T(1,128)S(1)}, u32[]{:S(2)}, u32[]{:S(2)}) async-start(f32[32,1,128]{2,1,0:T(1,128)} %bitcast.14), calls=%async_computation.2 | async-start | bytes 32768 | tf_op jit(solution)/shard_map/all_to_all | solution.py:263
  151.1 1.5 pad_maximum_fusion
  152.6 5.6 %all-to-all-done.2 = f32[32,1,128]{2,1,0:T(1,128)S(1)} async-done(((f32[32,1,128]{2,1,0:T(1,128)}), f32[32,1,128]{2,1,0:T(1,128)S(1)}, u32[]{:S(2)}, u32[]{:S(2)}) %all-to-all-start.2) | async-done | bytes 16416 | tf_op jit(solution)/shard_map/all_to_all | solution.py:263
  158.2 1.0 fusion
  (1 shorter events, 0.0 us)
Async XLA Ops:
  1.6 1.9 %collective-permute-start = (f32[384,128]{1,0:T(8,128)S(1)}, f32[384,128]{1,0:T(8,128)S(1)}, u32[]{:S(2)}, u32[]{:S(2)}) collective-permute-start(f32[384,128]{1,0:T(8,128)S(1)} %constant_dynamic-slice_fusion), channel_id=1, source_target_pairs={{0,1},{1,0},{2,3},{3,2},{4,5},{5,4},{6,7},{7,6},{8,9},{9,8},{10,11... | collective-permute-start | bytes 589832 | tf_op jit(solution)/shard_map/ppermute | solution.py:250
  2.1 1.4 collective-permute-start.1
  3.5 10.5 %collective-permute-start.2 = (f32[384,4096]{1,0:T(8,128)}, f32[384,4096]{1,0:T(8,128)}, u32[]{:S(2)}, u32[]{:S(2)}) collective-permute-start(f32[384,4096]{1,0:T(8,128)} %x_ref.2), channel_id=1, source_target_pairs={{0,1},{1,0},{2,3},{3,2},{4,5},{5,4},{6,7},{7,6},{8,9},{9,8},{10,11... | collective-permute-start | bytes 18874376 | tf_op jit(solution)/shard_map/ppermute | solution.py:252
  6.6 19.1 %all-to-all-start.1 = ((bf16[32,8,640]{2,1,0:T(8,128)(2,1)}), bf16[32,8,640]{2,1,0:T(8,128)(2,1)S(1)}, u32[]{:S(2)}, u32[]{:S(2)}) async-start(bf16[32,8,640]{2,1,0:T(8,128)(2,1)} %bitcast.12), calls=%async_computation.1 | async-start | bytes 655360 | tf_op jit(solution)/shard_map/all_to_all | solution.py:257
  22.3 7.3 %copy-start = (s32[384]{0:T(512)S(1)}, s32[384]{0:T(512)}, u32[]{:S(2)}) copy-start(s32[384]{0:T(512)} %mine_ref.3) | copy-start | bytes 4612
  25.7 113.5 %all-to-all-start = ((bf16[32,8,9600]{2,1,0:T(8,128)(2,1)}), bf16[32,8,9600]{2,1,0:T(8,128)(2,1)}, u32[]{:S(2)}, u32[]{:S(2)}) async-start(bf16[32,8,9600]{2,1,0:T(8,128)(2,1)} %bitcast.11), calls=%async_computation | async-start | bytes 9830400 | tf_op jit(solution)/shard_map/all_to_all | solution.py:257
  147.4 10.8 %all-to-all-start.2 = ((f32[32,1,128]{2,1,0:T(1,128)}), f32[32,1,128]{2,1,0:T(1,128)S(1)}, u32[]{:S(2)}, u32[]{:S(2)}) async-start(f32[32,1,128]{2,1,0:T(1,128)} %bitcast.14), calls=%async_computation.2 | async-start | bytes 32768 | tf_op jit(solution)/shard_map/all_to_all | solution.py:263

commit v6 on v5

--- a/solution.py
+++ b/solution.py
@@ -9,6 +9,8 @@
 
 CLUSTERS = 256
 LANES = 128
+PIECES = 1
+VMEM_LIMIT = 40 * 2**20
 PARTS = ((3840, 256, 128), (0, 3840, 640))
 F32 = jnp.float32
 BF16 = jnp.bfloat16
@@ -37,7 +39,7 @@
     return jnp.concatenate([high, (x - high.astype(F32)).astype(BF16)], axis=0)
 
 
-def code_kernel(core_ref, mine_ref, mate_ref, x_ref, y_ref, out_ref, pick0_ref, pick1_ref, num_ref):
+def code_kernel(mark, core_ref, mine_ref, mate_ref, x_ref, y_ref, out_ref, pick0_ref, pick1_ref, num_ref):
     rows, tile = x_ref.shape
     core = core_ref[0]
 
@@ -71,9 +73,10 @@
         row3 = rows1[CLUSTERS:]
         mean = ((row0 + row1) + rows1[:CLUSTERS]) * num_ref[2 * CLUSTERS :]
         high = mean.astype(BF16)
-        flag = jnp.where(count1 > 0.5, jnp.inf, -jnp.inf)
-        out_ref[:, :tile] = jnp.where(count0 > 0.5, row0 - mean, jnp.inf).astype(BF16)
-        out_ref[:, tile : 2 * tile] = jnp.where(count0 > 1.5, row1 - mean, jnp.inf).astype(BF16)
+        none = jnp.inf if mark else 0.0
+        flag = jnp.where(count1 > 0.5, none, -none)
+        out_ref[:, :tile] = jnp.where(count0 > 0.5, row0 - mean, none).astype(BF16)
+        out_ref[:, tile : 2 * tile] = jnp.where(count0 > 1.5, row1 - mean, none).astype(BF16)
         out_ref[:, 2 * tile : 3 * tile] = jnp.where(count1 > 1.5, row3 - mean, flag).astype(BF16)
         out_ref[:, 3 * tile : 4 * tile] = high
         out_ref[:, 4 * tile :] = (mean - high.astype(F32)).astype(BF16)
@@ -87,7 +90,7 @@
         body(y_ref, x_ref)
 
 
-def code(core, mine, mate, x, y, start, width, tile):
+def code(core, mine, mate, x, y, start, width, tile, mark):
     rows = x.shape[0]
     first = start // tile
     steps = width // 2 // tile
@@ -99,7 +102,7 @@
     else:
         y_spec = block
     return pl.pallas_call(
-        code_kernel,
+        functools.partial(code_kernel, mark),
         grid_spec=pltpu.PrefetchScalarGridSpec(
             num_scalar_prefetch=1,
             grid=(steps,),
@@ -115,52 +118,75 @@
     )(core, mine, pltpu.with_memory_space_constraint(mate, pltpu.VMEM), x, y)
 
 
-def compare_kernel(cl_dev, width_all, first, last, *refs):
+def compare_kernel(cl_dev, width_all, pieces, first, last, *refs):
     refs = list(refs)
-    got_ref = refs.pop(0)
-    gram_in_ref = None if first else refs.pop(0)
+    got_refs = [refs.pop(0) for _ in range(pieces)]
+    if not first:
+        gram_in_ref, live_ref = refs.pop(0), refs.pop(0)
     centroid_refs = [refs.pop(0), refs.pop(0)]
     best_ref = refs.pop(0) if last else None
-    gram_ref, mix_ref, total_ref, live_ref = refs
-    slots = mix_ref.shape[0]
+    gram_ref = refs.pop(0)
+    if first:
+        live_ref = refs.pop(0)
+    count_ref, total_ref = refs
+    slots = live_ref.shape[0] // 4
     tile = centroid_refs[0].shape[1]
+    blocks = cl_dev % 8 == 0
 
     def part(core, lo, hi):
-        return got_ref[:, core, :, lo:hi].astype(F32).reshape(slots, hi - lo)
+        found = [ref[:, core, :, lo:hi].astype(F32).reshape(-1, hi - lo) for ref in got_refs]
+        return found[0] if pieces == 1 else jnp.concatenate(found, axis=0)
 
     @pl.when(pl.program_id(0) == 0)
     def _():
         gram_ref[...] = jnp.zeros_like(gram_ref) if first else gram_in_ref[...]
-        mark = part(0, 2 * tile, 2 * tile + LANES)[:, :1]
-        live = [
-            part(0, 0, LANES)[:, :1] < jnp.inf,
-            part(0, tile, tile + LANES)[:, :1] < jnp.inf,
-            mark > -jnp.inf,
-            jnp.abs(mark) < jnp.inf,
-        ]
-        live = [x.astype(F32) for x in live]
-        for k in range(4):
-            live_ref[k * slots : (k + 1) * slots] = live[k]
+        if first:
+            mark = part(0, 2 * tile, 2 * tile + LANES)[:, :1]
+            live = [
+                part(0, 0, LANES)[:, :1] < jnp.inf,
+                part(0, tile, tile + LANES)[:, :1] < jnp.inf,
+                mark > -jnp.inf,
+                jnp.abs(mark) < jnp.inf,
+            ]
+            for k in range(4):
+                live_ref[k * slots : (k + 1) * slots] = live[k].astype(F32)
+        live = [live_ref[k * slots : (k + 1) * slots] for k in range(4)]
+        count = live[0] + live[1] + live[2] + live[3]
+        count_ref[...] = count
         same = (iota((slots, slots), 0) % cl_dev) == (iota((slots, slots), 1) % cl_dev)
-        mix = jnp.where(same, to_row(live[0] + live[1] + live[2] + live[3]), 0.0)
-        mix_ref[...] = mix.astype(BF16)
-        total_ref[...] = 1.0 / jnp.sum(mix, axis=1, keepdims=True)
+        total_ref[...] = 1.0 / jnp.sum(jnp.where(same, to_row(count), 0.0), axis=1, keepdims=True)
 
     live = [live_ref[k * slots : (k + 1) * slots] > 0.5 for k in range(4)]
-    mix = mix_ref[...]
-    scale = total_ref[...]
+    count = count_ref[...]
+    if not blocks:
+        same = (iota((slots, slots), 0) % cl_dev) == (iota((slots, slots), 1) % cl_dev)
+        mix = same.astype(F32)
     gram = gram_ref[...]
     for core in range(2):
-        d0 = jnp.where(live[0], part(core, 0, tile), 0.0)
-        d1 = jnp.where(live[1], part(core, tile, 2 * tile), 0.0)
-        d3 = jnp.where(live[3], part(core, 2 * tile, 3 * tile), 0.0)
-        d2 = jnp.where(live[2], -(d0 + d1 + d3), 0.0)
-        high = part(core, 3 * tile, 4 * tile)
-        low = part(core, 4 * tile, 5 * tile)
-        centroid = (mm(mix, high.astype(BF16)) + mm(mix, low.astype(BF16))) * scale
+        d0, d1, d3 = [part(core, k * tile, (k + 1) * tile) for k in range(3)]
+        if first:
+            d0 = jnp.where(live[0], d0, 0.0)
+            d1 = jnp.where(live[1], d1, 0.0)
+            d3 = jnp.where(live[3], d3, 0.0)
+        mean = part(core, 3 * tile, 4 * tile) + part(core, 4 * tile, 5 * tile)
+        if blocks:
+            chips = slots // cl_dev
+            sums = jnp.sum((mean * count).reshape(chips, cl_dev, tile), axis=0)
+            centroid = sums * total_ref[:cl_dev]
+            away = (mean.reshape(chips, cl_dev, tile) - centroid[None]).reshape(slots, tile)
+        else:
+            sums = lax.dot_general(
+                mix,
+                mean * count,
+                (((1,), (0,)), ((), ())),
+                precision=lax.Precision.HIGHEST,
+                preferred_element_type=F32,
+            )
+            centroid = sums * total_ref[...]
+            away = mean - centroid
         centroid_refs[core][...] = centroid[:cl_dev]
-        away = (high - centroid) + low
-        every = jnp.concatenate([away + d0, away + d1, away + d2, away + d3], axis=0).astype(BF16)
+        rest = away - (d0 + d1 + d3)
+        every = jnp.concatenate([away + d0, away + d1, rest, away + d3], axis=0).astype(BF16)
         gram += lax.dot_general(every, every, (((1,), (1,)), ((), ())), preferred_element_type=F32)
     gram_ref[...] = gram
 
@@ -169,7 +195,6 @@
         @pl.when(pl.program_id(0) == pl.num_programs(0) - 1)
         def _():
             n = 4 * slots
-            gram = gram_ref[...]
             row = iota((n, n), 0)
             col = iota((n, n), 1)
             diag = jnp.where(row == col, gram, 0.0)
@@ -194,8 +219,8 @@
             )
 
 
-def compare(got, gram, cl_dev, width_all, last, tile):
-    first = gram is None
+def compare(got, state, cl_dev, width_all, last, tile, resident):
+    first = state is None
     slots = CLUSTERS // 2
     half = got.shape[1] // 5
     chips = slots // cl_dev
@@ -203,37 +228,43 @@
     if cl_dev % 8:
         got = jnp.moveaxis(got, 1, 0).reshape(1, 2, slots, got.shape[3])
     fixed = lambda t: (0, 0)
-    args = [got]
-    if half == tile:
+    if resident:
+        pieces = 1
         args = [pltpu.with_memory_space_constraint(got, pltpu.VMEM)]
         specs = [pl.BlockSpec(memory_space=pltpu.VMEM)]
     else:
-        specs = [pl.BlockSpec((*got.shape[:3], 5 * tile), lambda t: (0, 0, 0, t))]
-    square = (4 * slots, 4 * slots)
-    if not first:
-        args.append(gram)
-        specs.append(pl.BlockSpec(square, fixed))
+        pieces = PIECES if cl_dev % 8 == 0 else 1
+        args = [got] * pieces
+        shape = (got.shape[0] // pieces, *got.shape[1:3], 5 * tile)
+        specs = [pl.BlockSpec(shape, lambda t, k=k: (k, 0, 0, t)) for k in range(pieces)]
+    square = jax.ShapeDtypeStruct((4 * slots, 4 * slots), F32)
+    column = jax.ShapeDtypeStruct((4 * slots, 1), F32)
+    square_spec = pl.BlockSpec(square.shape, fixed)
+    column_spec = pl.BlockSpec(column.shape, fixed)
     out_shape = [jax.ShapeDtypeStruct((cl_dev, half), F32)] * 2
     out_specs = [pl.BlockSpec((cl_dev, tile), lambda t: (0, t))] * 2
-    scratch = [
-        pltpu.VMEM((slots, slots), BF16),
-        pltpu.VMEM((slots, 1), F32),
-        pltpu.VMEM((4 * slots, 1), F32),
-    ]
+    scratch = [pltpu.VMEM((slots, 1), F32)] * 2
     if last:
         out_shape.append(jax.ShapeDtypeStruct((2 * chips, LANES), F32))
         out_specs.append(pl.BlockSpec((2 * chips, LANES), fixed))
-        scratch.insert(0, pltpu.VMEM(square, F32))
+        scratch.insert(0, pltpu.VMEM(square.shape, F32))
     else:
-        out_shape.append(jax.ShapeDtypeStruct(square, F32))
-        out_specs.append(pl.BlockSpec(square, fixed))
+        out_shape.append(square)
+        out_specs.append(square_spec)
+    if first:
+        out_shape.append(column)
+        out_specs.append(column_spec)
+    else:
+        args += [pltpu.with_memory_space_constraint(x, pltpu.VMEM) for x in state]
+        specs += [pl.BlockSpec(memory_space=pltpu.VMEM)] * 2
     return pl.pallas_call(
-        functools.partial(compare_kernel, cl_dev, width_all, first, last),
+        functools.partial(compare_kernel, cl_dev, width_all, pieces, first, last),
         grid=(half // tile,),
         in_specs=specs,
         out_specs=out_specs,
         out_shape=out_shape,
         scratch_shapes=scratch,
+        compiler_params=pltpu.CompilerParams(vmem_limit_bytes=VMEM_LIMIT),
     )(*args)
 
 
@@ -252,15 +283,12 @@
     tail = swap(whole)
     got = []
     for start, part, tile in PARTS:
-        coded = code(core.astype(jnp.int32).reshape(1), assignment, mate, embeddings, tail if got else head, start, part, tile)
+        coded = code(core.astype(jnp.int32).reshape(1), assignment, mate, embeddings, tail if got else head, start, part, tile, not got)
         coded, embeddings = lax.optimization_barrier((coded, embeddings))
         got.append(exchange(coded))
-    gram = None
-    centroids = []
-    for i, (_, _, tile) in enumerate(PARTS):
-        *c, gram = compare(got[i], gram, cl_dev, width, i == len(got) - 1, tile)
-        centroids = c + centroids
-    found = exchange(gram)
+    c0, c1, *state = compare(got[0], None, cl_dev, width, False, PARTS[0][2], True)
+    c2, c3, best = compare(got[1], state, cl_dev, width, True, PARTS[1][2], False)
+    found = exchange(best)
     row_ids = jnp.arange(rows, dtype=jnp.int32)
     twin = (assignment[:, None] == assignment[None, :]) & (row_ids[None, :] < row_ids[:, None])
     second = jnp.sum(twin.astype(jnp.int32), axis=1)
@@ -270,7 +298,7 @@
         owner.astype(F32), found, (((1,), (0,)), ((), ())), precision=lax.Precision.HIGHEST
     )
     maxima = jnp.sum(jnp.where(lane, lines, 0.0), axis=1)
-    return (maxima, jnp.concatenate(centroids, axis=1))
+    return (maxima, jnp.concatenate([c2, c3, c0, c1], axis=1))
 
 
 def solution(mesh):

time: 160 us -> 158 us (0.988)
  Pallas kernels: 21.3 us -> 18.7 us
  waiting for transfers between devices: 118 us -> 120 us
    pallas_call x4, Pallas kernels: 21.3 us -> 18.7 us  [the longest x2 11.2 us: code(): pl.pallas_call(functools.partial(code_kernel, mark), grid_spec=pltpu.Pref...]
where the time goes in v6:
time: 158 us
  waiting for transfers between devices  120 us (76%)
  Pallas kernels  18.7 us (12%)
  starting transfers between devices  15.6 us (10%)
    all_to_all x2, waiting for transfers between devices, on_device(): got.append(exchange(coded))  112 us
    pallas_call x2, Pallas kernels, code(): pl.pallas_call(functools.partial(code_kernel, mark), grid_spec=pltpu.Pref...  11.2 us
    all_to_all x2, starting transfers between devices, on_device(): got.append(exchange(coded))  11 us
    pallas_call x2, Pallas kernels, compare(): pl.pallas_call(functools.partial(compare_kernel, cl_dev, width_all, piece...  7.51 us
    all_to_all x1, waiting for transfers between devices, on_device(): found = exchange(best)  6.48 us
    all_to_all x1, starting transfers between devices, on_device(): found = exchange(best)  3.68 us
  transfers between devices with their start and end apart: 6, of which 5 were waited for; matrix products, arithmetic and copies ran while one was open for 1% of the time, Pallas kernels for 8%

profile of v6, /device:TPU:0, one launch (start us, length us, event | category | flops | bytes accessed | tf_op | source)
XLA Modules:
  0.0 157.7 jit_solution(6652384017089730791)
XLA Ops:
  0.6 0.9 constant_dynamic-slice_fusion
  1.6 0.5 collective-permute-start
  2.1 0.1 collective-permute-start.1
  2.2 1.3 collective-permute-done.1.mate_ref
  3.5 0.0 collective-permute-done.y_ref
  3.5 0.3 collective-permute-start.2
  3.8 2.8 %shard_map.41 = bf16[256,640]{1,0:T(8,128)(2,1)} custom-call(s32[1]{0:T(128)} %bitcast.core_ref, s32[384]{0:T(512)} %mine_ref.3, s32[384]{0:T(512)S(1)} %collective-permute-done.1.mate_ref, f32[384,4096]{1,0:T(8,128)} %x_ref.2, f32[384,128]{1,0:T(8,128)S(1)} %collective-permute-done.y_ref), custom_call_target="tpu_custom_call" | custom-call | tf_op jit(solution)/shard_map/pallas_call | solution.py:104
  6.6 7.1 %all-to-all-start.1 = ((bf16[32,8,640]{2,1,0:T(8,128)(2,1)}), bf16[32,8,640]{2,1,0:T(8,128)(2,1)S(1)}, u32[]{:S(2)}, u32[]{:S(2)}) async-start(bf16[32,8,640]{2,1,0:T(8,128)(2,1)} %bitcast.12), calls=%async_computation.1 | async-start | bytes 655360 | tf_op jit(solution)/shard_map/all_to_all | solution.py:288
  13.7 0.3 collective-permute-done.2.y_ref
  14.0 8.4 %shard_map.42 = bf16[256,9600]{1,0:T(8,128)(2,1)} custom-call(s32[1]{0:T(128)} %bitcast.core_ref, s32[384]{0:T(512)} %mine_ref.3, s32[384]{0:T(512)S(1)} %collective-permute-done.1.mate_ref, f32[384,4096]{1,0:T(8,128)} %x_ref.2, f32[384,4096]{1,0:T(8,128)} %collective-permute-done.2.y_ref), custom_call_target="tpu_custom_call" | custom-call | tf_op jit(solution)/shard_map/pallas_call | solution.py:104
  22.3 0.0 copy-start
  22.4 3.3 %all-to-all-done.1 = bf16[32,8,640]{2,1,0:T(8,128)(2,1)S(1)} async-done(((bf16[32,8,640]{2,1,0:T(8,128)(2,1)}), bf16[32,8,640]{2,1,0:T(8,128)(2,1)S(1)}, u32[]{:S(2)}, u32[]{:S(2)}) %all-to-all-start.1) | async-done | bytes 327712 | tf_op jit(solution)/shard_map/all_to_all | solution.py:288
  25.7 3.9 %all-to-all-start = ((bf16[32,8,9600]{2,1,0:T(8,128)(2,1)}), bf16[32,8,9600]{2,1,0:T(8,128)(2,1)}, u32[]{:S(2)}, u32[]{:S(2)}) async-start(bf16[32,8,9600]{2,1,0:T(8,128)(2,1)} %bitcast.11), calls=%async_computation | async-start | bytes 9830400 | tf_op jit(solution)/shard_map/all_to_all | solution.py:288
  29.6 0.0 copy-done
  29.6 0.2 convert_reduce_fusion
  29.9 0.7 shard_map.43
  30.6 108.6 %all-to-all-done = bf16[32,8,9600]{2,1,0:T(8,128)(2,1)} async-done(((bf16[32,8,9600]{2,1,0:T(8,128)(2,1)}), bf16[32,8,9600]{2,1,0:T(8,128)(2,1)}, u32[]{:S(2)}, u32[]{:S(2)}) %all-to-all-start) | async-done | bytes 4915232 | tf_op jit(solution)/shard_map/all_to_all | solution.py:288
  139.2 6.8 %shard_map.44 = (f32[8,1920]{1,0:T(8,128)S(1)}, f32[8,1920]{1,0:T(8,128)S(1)}, f32[32,128]{1,0:T(8,128)}) custom-call(bf16[16,2,8,9600]{3,2,1,0:T(8,128)(2,1)} %bitcast.2.refs_0_, f32[512,512]{1,0:T(8,128)S(1)} %get-tuple-element.21.refs_1_, f32[512,1]{1,0:T(8,128)S(1)} %get-tuple-element.22.refs_2_), custom_call_target="tpu_custom_call" | custom-call | tf_op jit(solution)/shard_map/pallas_call | solution.py:260
  146.0 3.7 %all-to-all-start.2 = ((f32[32,1,128]{2,1,0:T(1,128)}), f32[32,1,128]{2,1,0:T(1,128)S(1)}, u32[]{:S(2)}, u32[]{:S(2)}) async-start(f32[32,1,128]{2,1,0:T(1,128)} %bitcast.6), calls=%async_computation.2 | async-start | bytes 32768 | tf_op jit(solution)/shard_map/all_to_all | solution.py:291
  149.6 0.7 pad_maximum_fusion
  150.3 6.5 %all-to-all-done.2 = f32[32,1,128]{2,1,0:T(1,128)S(1)} async-done(((f32[32,1,128]{2,1,0:T(1,128)}), f32[32,1,128]{2,1,0:T(1,128)S(1)}, u32[]{:S(2)}, u32[]{:S(2)}) %all-to-all-start.2) | async-done | bytes 16416 | tf_op jit(solution)/shard_map/all_to_all | solution.py:291
  156.8 1.0 fusion
  (1 shorter events, 0.0 us)
Async XLA Ops:
  1.6 1.9 %collective-permute-start = (f32[384,128]{1,0:T(8,128)S(1)}, f32[384,128]{1,0:T(8,128)S(1)}, u32[]{:S(2)}, u32[]{:S(2)}) collective-permute-start(f32[384,128]{1,0:T(8,128)S(1)} %constant_dynamic-slice_fusion), channel_id=1, source_target_pairs={{0,1},{1,0},{2,3},{3,2},{4,5},{5,4},{6,7},{7,6},{8,9},{9,8},{10,11... | collective-permute-start | bytes 589832 | tf_op jit(solution)/shard_map/ppermute | solution.py:281
  2.1 1.4 collective-permute-start.1
  3.5 10.5 %collective-permute-start.2 = (f32[384,4096]{1,0:T(8,128)}, f32[384,4096]{1,0:T(8,128)}, u32[]{:S(2)}, u32[]{:S(2)}) collective-permute-start(f32[384,4096]{1,0:T(8,128)} %x_ref.2), channel_id=1, source_target_pairs={{0,1},{1,0},{2,3},{3,2},{4,5},{5,4},{6,7},{7,6},{8,9},{9,8},{10,11... | collective-permute-start | bytes 18874376 | tf_op jit(solution)/shard_map/ppermute | solution.py:283
  6.6 19.1 %all-to-all-start.1 = ((bf16[32,8,640]{2,1,0:T(8,128)(2,1)}), bf16[32,8,640]{2,1,0:T(8,128)(2,1)S(1)}, u32[]{:S(2)}, u32[]{:S(2)}) async-start(bf16[32,8,640]{2,1,0:T(8,128)(2,1)} %bitcast.12), calls=%async_computation.1 | async-start | bytes 655360 | tf_op jit(solution)/shard_map/all_to_all | solution.py:288
  22.3 7.3 %copy-start = (s32[384]{0:T(512)S(1)}, s32[384]{0:T(512)}, u32[]{:S(2)}) copy-start(s32[384]{0:T(512)} %mine_ref.3) | copy-start | bytes 4612
  25.7 113.5 %all-to-all-start = ((bf16[32,8,9600]{2,1,0:T(8,128)(2,1)}), bf16[32,8,9600]{2,1,0:T(8,128)(2,1)}, u32[]{:S(2)}, u32[]{:S(2)}) async-start(bf16[32,8,9600]{2,1,0:T(8,128)(2,1)} %bitcast.11), calls=%async_computation | async-start | bytes 9830400 | tf_op jit(solution)/shard_map/all_to_all | solution.py:288
  146.0 10.8 %all-to-all-start.2 = ((f32[32,1,128]{2,1,0:T(1,128)}), f32[32,1,128]{2,1,0:T(1,128)S(1)}, u32[]{:S(2)}, u32[]{:S(2)}) async-start(f32[32,1,128]{2,1,0:T(1,128)} %bitcast.6), calls=%async_computation.2 | async-start | bytes 32768 | tf_op jit(solution)/shard_map/all_to_all | solution.py:291

commit v7 on v5

v7 whole, which is shorter than its diff:
```python
import functools

import jax
import jax.numpy as jnp
from jax import lax
from jax.experimental import pallas as pl
from jax.experimental.pallas import tpu as pltpu
from jax.sharding import PartitionSpec as P

CLUSTERS = 256
LANES = 128
VMEM_LIMIT = 40 * 2**20
PARTS = ((3840, 256, 128), (0, 3840, 640))
F32 = jnp.float32
BF16 = jnp.bfloat16


def iota(shape, axis):
    return lax.broadcasted_iota(jnp.int32, shape, axis)


def mm(a, b):
    return lax.dot_general(a, b, (((1,), (0,)), ((), ())), preferred_element_type=F32)


def to_row(col):
    n = col.shape[0]
    return jnp.sum(jnp.where(iota((n, n), 0) == iota((n, n), 1), col, 0), axis=0, keepdims=True)


def to_col(row):
    n = row.shape[1]
    return jnp.sum(jnp.where(iota((n, n), 0) == iota((n, n), 1), row, 0), axis=1, keepdims=True)


def split(x):
    high = x.astype(BF16)
    return jnp.concatenate([high, (x - high.astype(F32)).astype(BF16)], axis=0)


def code_kernel(mark, core_ref, mine_ref, mate_ref, x_ref, y_ref, out_ref, pick0_ref, pick1_ref, num_ref):
    rows, tile = x_ref.shape
    core = core_ref[0]

    @pl.when(pl.program_id(0) == 0)
    def _():
        mine = mine_ref[...].reshape(1, rows)
        mate = mate_ref[...].reshape(1, rows)
        counts = []
        for k, pick_ref in enumerate((pick0_ref, pick1_ref)):
            ids = jnp.where(core == k, mine, mate)
            twin = (to_col(ids) == ids) & (iota((rows, rows), 0) < iota((rows, rows), 1))
            second = jnp.sum(twin.astype(F32), axis=0, keepdims=True) > 0.5
            member = iota((CLUSTERS, rows), 0) == ids
            upper = member & ~second if k == 0 else member
            for j in range(2):
                cols = slice(j * rows, (j + 1) * rows)
                pick_ref[:CLUSTERS, cols] = upper.astype(F32).astype(BF16)
                pick_ref[CLUSTERS:, cols] = (member & second).astype(F32).astype(BF16)
            counts.append(jnp.sum(member.astype(F32), axis=1, keepdims=True))
        num_ref[:CLUSTERS] = counts[0]
        num_ref[CLUSTERS : 2 * CLUSTERS] = counts[1]
        num_ref[2 * CLUSTERS :] = 1.0 / jnp.maximum(counts[0] + counts[1], 1.0)

    def body(x0_ref, x1_ref):
        rows0 = mm(pick0_ref[...], split(x0_ref[...]))
        rows1 = mm(pick1_ref[...], split(x1_ref[...]))
        count0 = num_ref[:CLUSTERS]
        count1 = num_ref[CLUSTERS : 2 * CLUSTERS]
        row0 = rows0[:CLUSTERS]
        row1 = rows0[CLUSTERS:]
        row3 = rows1[CLUSTERS:]
        mean = ((row0 + row1) + rows1[:CLUSTERS]) * num_ref[2 * CLUSTERS :]
        high = mean.astype(BF16)
        none = jnp.inf if mark else 0.0
        flag = jnp.where(count1 > 0.5, none, -none)
        out_ref[:, :tile] = jnp.where(count0 > 0.5, row0 - mean, none).astype(BF16)
        out_ref[:, tile : 2 * tile] = jnp.where(count0 > 1.5, row1 - mean, none).astype(BF16)
        out_ref[:, 2 * tile : 3 * tile] = jnp.where(count1 > 1.5, row3 - mean, flag).astype(BF16)
        out_ref[:, 3 * tile : 4 * tile] = high
        out_ref[:, 4 * tile :] = (mean - high.astype(F32)).astype(BF16)

    @pl.when(core == 0)
    def _():
        body(x_ref, y_ref)

    @pl.when(core == 1)
    def _():
        body(y_ref, x_ref)


def code(core, mine, mate, x, y, start, width, tile, mark):
    rows = x.shape[0]
    first = start // tile
    steps = width // 2 // tile
    line = pl.BlockSpec((rows,), lambda t, core: (0,))
    block = pl.BlockSpec((rows, tile), lambda t, core: (0, first + core[0] * steps + t))
    if y.shape[1] == tile:
        y = pltpu.with_memory_space_constraint(y, pltpu.VMEM)
        y_spec = pl.BlockSpec(memory_space=pltpu.VMEM)
    else:
        y_spec = block
    return pl.pallas_call(
        functools.partial(code_kernel, mark),
        grid_spec=pltpu.PrefetchScalarGridSpec(
            num_scalar_prefetch=1,
            grid=(steps,),
            in_specs=[line, pl.BlockSpec(memory_space=pltpu.VMEM), block, y_spec],
            out_specs=pl.BlockSpec((CLUSTERS, 5 * tile), lambda t, core: (0, t)),
            scratch_shapes=[
                pltpu.VMEM((2 * CLUSTERS, 2 * rows), BF16),
                pltpu.VMEM((2 * CLUSTERS, 2 * rows), BF16),
                pltpu.VMEM((3 * CLUSTERS, 1), F32),
            ],
        ),
        out_shape=jax.ShapeDtypeStruct((CLUSTERS, steps * 5 * tile), BF16),
    )(core, mine, pltpu.with_memory_space_constraint(mate, pltpu.VMEM), x, y)


def compare_kernel(cl_dev, width_all, tile, first, *refs):
    if first:
        got_ref, *centroid_refs, gram_ref, live_ref = refs
        slots = CLUSTERS // 2
        buffers = [got_ref]
    else:
        got_ref, gram_in_ref, live_ref, *centroid_refs, best_ref, gram_ref, buf_ref, sems = refs
        slots = live_ref.shape[0] // 4
        buffers = [buf_ref.at[t] for t in range(buf_ref.shape[0])]
        copies = [
            pltpu.make_async_copy(got_ref.at[:, :, :, t * 5 * tile : (t + 1) * 5 * tile], buffer, sems.at[t])
            for t, buffer in enumerate(buffers)
        ]
        for copy in copies:
            copy.start()

    def part(buffer, core, k):
        return buffer[:, core, :, k * tile : (k + 1) * tile].astype(F32).reshape(slots, tile)

    if first:
        mark = part(got_ref, 0, 2)[:, :1]
        live = [
            part(got_ref, 0, 0)[:, :1] < jnp.inf,
            part(got_ref, 0, 1)[:, :1] < jnp.inf,
            mark > -jnp.inf,
            jnp.abs(mark) < jnp.inf,
        ]
        for k in range(4):
            live_ref[k * slots : (k + 1) * slots] = live[k].astype(F32)
    alive = [live_ref[k * slots : (k + 1) * slots] for k in range(4)]
    count = alive[0] + alive[1] + alive[2] + alive[3]
    same = (iota((slots, slots), 0) % cl_dev) == (iota((slots, slots), 1) % cl_dev)
    scale = 1.0 / jnp.sum(jnp.where(same, to_row(count), 0.0), axis=1, keepdims=True)
    half = 2 * slots
    for t, buffer in enumerate(buffers):
        if not first:
            copies[t].wait()
        rows = []
        for core in range(2):
            d0, d1, d3 = [part(buffer, core, k) for k in range(3)]
            if first:
                d0 = jnp.where(live[0], d0, 0.0)
                d1 = jnp.where(live[1], d1, 0.0)
                d3 = jnp.where(live[3], d3, 0.0)
            mean = part(buffer, core, 3) + part(buffer, core, 4)
            if cl_dev % 8 == 0:
                chips = slots // cl_dev
                centroid = jnp.sum((mean * count).reshape(chips, cl_dev, tile), axis=0) * scale[:cl_dev]
                away = (mean.reshape(chips, cl_dev, tile) - centroid[None]).reshape(slots, tile)
            else:
                sums = lax.dot_general(
                    same.astype(F32),
                    mean * count,
                    (((1,), (0,)), ((), ())),
                    precision=lax.Precision.HIGHEST,
                    preferred_element_type=F32,
                )
                centroid = sums * scale
                away = mean - centroid
            centroid_refs[core][:, t * tile : (t + 1) * tile] = centroid[:cl_dev]
            rest = away - (d0 + d1 + d3)
            rows.append(jnp.concatenate([away + d0, away + d1, rest, away + d3], axis=0).astype(BF16))
        every = jnp.concatenate(rows, axis=1)
        upper = lax.dot_general(every[:half], every, (((1,), (1,)), ((), ())), preferred_element_type=F32)
        lower = lax.dot_general(every[half:], every[half:], (((1,), (1,)), ((), ())), preferred_element_type=F32)
        if first:
            gram_ref[:half] = upper
            gram_ref[half:, half:] = lower
            gram_ref[half:, :half] = jnp.zeros((half, half), F32)
        else:
            old_ref = gram_ref if t else gram_in_ref
            gram_ref[:half] = old_ref[:half] + upper
            gram_ref[half:, half:] = old_ref[half:, half:] + lower

    if not first:
        gram_ref[half:, :half] = jnp.transpose(gram_ref[:half, half:])
        n = 4 * slots
        gram = gram_ref[...]
        row = iota((n, n), 0)
        col = iota((n, n), 1)
        diag = jnp.where(row == col, gram, 0.0)
        inv_row = lax.rsqrt(jnp.sum(diag, axis=0, keepdims=True) / width_all + 1e-6)
        inv_col = lax.rsqrt(jnp.sum(diag, axis=1, keepdims=True) / width_all + 1e-6)
        score = gram * inv_col * inv_row / width_all
        usable = ((row % cl_dev) == (col % cl_dev)) & (row != col) & (live_ref[...] > 0.5)
        best = jnp.max(jnp.where(usable, score, -1.0), axis=0, keepdims=True)
        sources = 2 * slots // cl_dev
        place = iota((sources, n), 1)
        source = (place % slots) // cl_dev * 2 + place // (2 * slots)
        spread = jnp.where(source == iota((sources, n), 0), best, 0.0)
        place = iota((n, LANES), 0)
        lane = (place // slots) % 2 * cl_dev + place % cl_dev
        pick = (lane == iota((n, LANES), 1)).astype(F32)
        best_ref[...] = lax.dot_general(
            spread,
            pick,
            (((1,), (0,)), ((), ())),
            precision=lax.Precision.HIGHEST,
            preferred_element_type=F32,
        )


def compare(got, state, cl_dev, width_all, tile):
    first = state is None
    slots = CLUSTERS // 2
    half = got.shape[1] // 5
    chips = slots // cl_dev
    got = got.reshape(chips, 2, cl_dev, got.shape[1])
    if cl_dev % 8:
        got = jnp.moveaxis(got, 1, 0).reshape(1, 2, slots, got.shape[3])
    near = lambda x: pltpu.with_memory_space_constraint(x, pltpu.VMEM)
    vmem = pl.BlockSpec(memory_space=pltpu.VMEM)
    square = jax.ShapeDtypeStruct((4 * slots, 4 * slots), F32)
    out_shape = [jax.ShapeDtypeStruct((cl_dev, half), F32)] * 2
    if first:
        args = [near(got)]
        specs = [vmem]
        out_shape += [square, jax.ShapeDtypeStruct((4 * slots, 1), F32)]
        scratch = []
    else:
        args = [got] + [near(x) for x in state]
        specs = [pl.BlockSpec(memory_space=pl.ANY), vmem, vmem]
        out_shape.append(jax.ShapeDtypeStruct((2 * chips, LANES), F32))
        steps = half // tile
        scratch = [
            pltpu.VMEM(square.shape, F32),
            pltpu.VMEM((steps, *got.shape[:3], 5 * tile), BF16),
            pltpu.SemaphoreType.DMA((steps,)),
        ]
    return pl.pallas_call(
        functools.partial(compare_kernel, cl_dev, width_all, tile, first),
        in_specs=specs,
        out_specs=[vmem] * len(out_shape),
        out_shape=out_shape,
        scratch_shapes=scratch,
        compiler_params=pltpu.CompilerParams(vmem_limit_bytes=VMEM_LIMIT),
    )(*args)


def on_device(embeddings, assignment):
    dev_count = lax.axis_size("rows")
    cl_dev = CLUSTERS // dev_count
    rows, width = embeddings.shape
    core = lax.axis_index("rows") % 2
    exchange = functools.partial(lax.all_to_all, axis_name="rows", split_axis=0, concat_axis=0, tiled=True)
    swap = functools.partial(lax.ppermute, axis_name="rows", perm=[(i, i ^ 1) for i in range(dev_count)])
    mate = swap(assignment)
    first, part, _ = PARTS[0]
    half = part // 2
    head = swap(lax.dynamic_slice_in_dim(embeddings, first + (1 - core) * half, half, 1))
    whole, head, mate = lax.optimization_barrier((embeddings, head, mate))
    tail = swap(whole)
    got = []
    for start, part, tile in PARTS:
        coded = code(core.astype(jnp.int32).reshape(1), assignment, mate, embeddings, tail if got else head, start, part, tile, not got)
        coded, embeddings = lax.optimization_barrier((coded, embeddings))
        got.append(exchange(coded))
    c0, c1, *state = compare(got[0], None, cl_dev, width, PARTS[0][2])
    c2, c3, best = compare(got[1], state, cl_dev, width, PARTS[1][2])
    found = exchange(best)
    row_ids = jnp.arange(rows, dtype=jnp.int32)
    twin = (assignment[:, None] == assignment[None, :]) & (row_ids[None, :] < row_ids[:, None])
    second = jnp.sum(twin.astype(jnp.int32), axis=1)
    owner = (assignment // cl_dev)[:, None] == jnp.arange(dev_count, dtype=jnp.int32)[None, :]
    lane = (second * cl_dev + assignment % cl_dev)[:, None] == jnp.arange(LANES, dtype=jnp.int32)[None, :]
    lines = lax.dot_general(
        owner.astype(F32), found, (((1,), (0,)), ((), ())), precision=lax.Precision.HIGHEST
    )
    maxima = jnp.sum(jnp.where(lane, lines, 0.0), axis=1)
    return (maxima, jnp.concatenate([c2, c3, c0, c1], axis=1))


def solution(mesh):
    placed = (P(("group", "rows"), None), P(("group", "rows")))
    return jax.shard_map(
        on_device,
        mesh=mesh,
        in_specs=placed,
        out_specs=(P(("group", "rows")), P(("group", "rows"), None)),
        check_vma=False,
    )
```

time: 160 us -> 157 us (0.981)
  Pallas kernels: 21.3 us -> 17.3 us
  waiting for transfers between devices: 118 us -> 120 us
    pallas_call x4, Pallas kernels: 21.3 us -> 17.3 us  [the longest x2 11.2 us: code(): pl.pallas_call(functools.partial(code_kernel, mark), grid_spec=pltpu.Pref...]
  transfers between devices with their start and end apart: 6 -> 6, of which waited for: 5 -> 5; matrix products, arithmetic and copies ran while one was open for 1% -> 1% of each run, Pallas kernels for 8% -> 7%
where the time goes in v7:
time: 157 us
  waiting for transfers between devices  120 us (76%)
  Pallas kernels  17.3 us (11%)
  starting transfers between devices  15.6 us (10%)
    all_to_all x2, waiting for transfers between devices, on_device(): got.append(exchange(coded))  112 us
    pallas_call x2, Pallas kernels, code(): pl.pallas_call(functools.partial(code_kernel, mark), grid_spec=pltpu.Pref...  11.2 us
    all_to_all x2, starting transfers between devices, on_device(): got.append(exchange(coded))  11 us
    all_to_all x1, waiting for transfers between devices, on_device(): found = exchange(best)  6.48 us
    pallas_call x2, Pallas kernels, compare(): pl.pallas_call(functools.partial(compare_kernel, cl_dev, width_all, tile,...  6.06 us
    all_to_all x1, starting transfers between devices, on_device(): found = exchange(best)  3.7 us
  transfers between devices with their start and end apart: 6, of which 5 were waited for; matrix products, arithmetic and copies ran while one was open for 1% of the time, Pallas kernels for 7%

profile of v7, /device:TPU:0, one launch (start us, length us, event | category | flops | bytes accessed | tf_op | source)
XLA Modules:
  0.0 156.5 jit_solution(7232021000778734129)
XLA Ops:
  0.6 0.9 constant_dynamic-slice_fusion
  1.6 0.5 collective-permute-start
  2.1 0.1 collective-permute-start.1
  2.2 1.3 collective-permute-done.1.mate_ref
  3.5 0.0 collective-permute-done.y_ref
  3.5 0.3 collective-permute-start.2
  3.8 2.8 %shard_map.41 = bf16[256,640]{1,0:T(8,128)(2,1)} custom-call(s32[1]{0:T(128)} %bitcast.core_ref, s32[384]{0:T(512)} %mine_ref.3, s32[384]{0:T(512)S(1)} %collective-permute-done.1.mate_ref, f32[384,4096]{1,0:T(8,128)} %x_ref.2, f32[384,128]{1,0:T(8,128)S(1)} %collective-permute-done.y_ref), custom_call_target="tpu_custom_call" | custom-call | tf_op jit(solution)/shard_map/pallas_call | solution.py:103
  6.6 7.1 %all-to-all-start.1 = ((bf16[32,8,640]{2,1,0:T(8,128)(2,1)}), bf16[32,8,640]{2,1,0:T(8,128)(2,1)S(1)}, u32[]{:S(2)}, u32[]{:S(2)}) async-start(bf16[32,8,640]{2,1,0:T(8,128)(2,1)} %bitcast.12), calls=%async_computation.1 | async-start | bytes 655360 | tf_op jit(solution)/shard_map/all_to_all | solution.py:276
  13.7 0.3 collective-permute-done.2.y_ref
  14.0 8.4 %shard_map.42 = bf16[256,9600]{1,0:T(8,128)(2,1)} custom-call(s32[1]{0:T(128)} %bitcast.core_ref, s32[384]{0:T(512)} %mine_ref.3, s32[384]{0:T(512)S(1)} %collective-permute-done.1.mate_ref, f32[384,4096]{1,0:T(8,128)} %x_ref.2, f32[384,4096]{1,0:T(8,128)} %collective-permute-done.2.y_ref), custom_call_target="tpu_custom_call" | custom-call | tf_op jit(solution)/shard_map/pallas_call | solution.py:103
  22.3 0.0 copy-start
  22.4 3.3 %all-to-all-done.1 = bf16[32,8,640]{2,1,0:T(8,128)(2,1)S(1)} async-done(((bf16[32,8,640]{2,1,0:T(8,128)(2,1)}), bf16[32,8,640]{2,1,0:T(8,128)(2,1)S(1)}, u32[]{:S(2)}, u32[]{:S(2)}) %all-to-all-start.1) | async-done | bytes 327712 | tf_op jit(solution)/shard_map/all_to_all | solution.py:276
  25.7 3.9 %all-to-all-start = ((bf16[32,8,9600]{2,1,0:T(8,128)(2,1)}), bf16[32,8,9600]{2,1,0:T(8,128)(2,1)}, u32[]{:S(2)}, u32[]{:S(2)}) async-start(bf16[32,8,9600]{2,1,0:T(8,128)(2,1)} %bitcast.11), calls=%async_computation | async-start | bytes 9830400 | tf_op jit(solution)/shard_map/all_to_all | solution.py:276
  29.6 0.0 copy-done
  29.6 0.2 convert_reduce_fusion
  29.9 0.5 shard_map.43
  30.4 108.8 %all-to-all-done = bf16[32,8,9600]{2,1,0:T(8,128)(2,1)} async-done(((bf16[32,8,9600]{2,1,0:T(8,128)(2,1)}), bf16[32,8,9600]{2,1,0:T(8,128)(2,1)}, u32[]{:S(2)}, u32[]{:S(2)}) %all-to-all-start) | async-done | bytes 4915232 | tf_op jit(solution)/shard_map/all_to_all | solution.py:276
  139.2 5.5 %shard_map.44 = (f32[8,1920]{1,0:T(8,128)S(1)}, f32[8,1920]{1,0:T(8,128)S(1)}, f32[32,128]{1,0:T(8,128)}) custom-call(bf16[16,2,8,9600]{3,2,1,0:T(8,128)(2,1)} %bitcast.2.refs_0_, f32[512,512]{1,0:T(8,128)S(1)} %get-tuple-element.21.refs_1_, f32[512,1]{1,0:T(8,128)S(1)} %get-tuple-element.22.refs_2_), custom_call_target="tpu_custom_call" | custom-call | tf_op jit(solution)/shard_map/pallas_call | solution.py:249
  144.7 3.7 %all-to-all-start.2 = ((f32[32,1,128]{2,1,0:T(1,128)}), f32[32,1,128]{2,1,0:T(1,128)S(1)}, u32[]{:S(2)}, u32[]{:S(2)}) async-start(f32[32,1,128]{2,1,0:T(1,128)} %bitcast.6), calls=%async_computation.2 | async-start | bytes 32768 | tf_op jit(solution)/shard_map/all_to_all | solution.py:279
  148.4 0.7 pad_maximum_fusion
  149.1 6.5 %all-to-all-done.2 = f32[32,1,128]{2,1,0:T(1,128)S(1)} async-done(((f32[32,1,128]{2,1,0:T(1,128)}), f32[32,1,128]{2,1,0:T(1,128)S(1)}, u32[]{:S(2)}, u32[]{:S(2)}) %all-to-all-start.2) | async-done | bytes 16416 | tf_op jit(solution)/shard_map/all_to_all | solution.py:279
  155.6 1.0 fusion
  (1 shorter events, 0.0 us)
Async XLA Ops:
  1.6 1.9 %collective-permute-start = (f32[384,128]{1,0:T(8,128)S(1)}, f32[384,128]{1,0:T(8,128)S(1)}, u32[]{:S(2)}, u32[]{:S(2)}) collective-permute-start(f32[384,128]{1,0:T(8,128)S(1)} %constant_dynamic-slice_fusion), channel_id=1, source_target_pairs={{0,1},{1,0},{2,3},{3,2},{4,5},{5,4},{6,7},{7,6},{8,9},{9,8},{10,11... | collective-permute-start | bytes 589832 | tf_op jit(solution)/shard_map/ppermute | solution.py:269
  2.1 1.4 collective-permute-start.1
  3.5 10.5 %collective-permute-start.2 = (f32[384,4096]{1,0:T(8,128)}, f32[384,4096]{1,0:T(8,128)}, u32[]{:S(2)}, u32[]{:S(2)}) collective-permute-start(f32[384,4096]{1,0:T(8,128)} %x_ref.2), channel_id=1, source_target_pairs={{0,1},{1,0},{2,3},{3,2},{4,5},{5,4},{6,7},{7,6},{8,9},{9,8},{10,11... | collective-permute-start | bytes 18874376 | tf_op jit(solution)/shard_map/ppermute | solution.py:271
  6.6 19.1 %all-to-all-start.1 = ((bf16[32,8,640]{2,1,0:T(8,128)(2,1)}), bf16[32,8,640]{2,1,0:T(8,128)(2,1)S(1)}, u32[]{:S(2)}, u32[]{:S(2)}) async-start(bf16[32,8,640]{2,1,0:T(8,128)(2,1)} %bitcast.12), calls=%async_computation.1 | async-start | bytes 655360 | tf_op jit(solution)/shard_map/all_to_all | solution.py:276
  22.3 7.3 %copy-start = (s32[384]{0:T(512)S(1)}, s32[384]{0:T(512)}, u32[]{:S(2)}) copy-start(s32[384]{0:T(512)} %mine_ref.3) | copy-start | bytes 4612
  25.7 113.5 %all-to-all-start = ((bf16[32,8,9600]{2,1,0:T(8,128)(2,1)}), bf16[32,8,9600]{2,1,0:T(8,128)(2,1)}, u32[]{:S(2)}, u32[]{:S(2)}) async-start(bf16[32,8,9600]{2,1,0:T(8,128)(2,1)} %bitcast.11), calls=%async_computation | async-start | bytes 9830400 | tf_op jit(solution)/shard_map/all_to_all | solution.py:276
  144.7 10.8 %all-to-all-start.2 = ((f32[32,1,128]{2,1,0:T(1,128)}), f32[32,1,128]{2,1,0:T(1,128)S(1)}, u32[]{:S(2)}, u32[]{:S(2)}) async-start(f32[32,1,128]{2,1,0:T(1,128)} %bitcast.6), calls=%async_computation.2 | async-start | bytes 32768 | tf_op jit(solution)/shard_map/all_to_all | solution.py:279

commit v8 on v7

--- a/solution.py
+++ b/solution.py
@@ -10,7 +10,7 @@
 CLUSTERS = 256
 LANES = 128
 VMEM_LIMIT = 40 * 2**20
-PARTS = ((3840, 256, 128), (0, 3840, 640))
+PARTS = ((3584, 512, 256), (0, 3584, 896))
 F32 = jnp.float32
 BF16 = jnp.bfloat16
 

time: 157 us -> 156 us (level)
  transfers between devices with their start and end apart: 6 -> 6, of which waited for: 5 -> 4; matrix products, arithmetic and copies ran while one was open for 1% -> 1% of each run, Pallas kernels for 7% -> 8%
where the time goes in v8:
time: 156 us; the launch traced here: 155 us
  waiting for transfers between devices  119 us (76%)
  Pallas kernels  16.9 us (11%)
  starting transfers between devices  15.4 us (10%)
    all_to_all x2, waiting for transfers between devices, on_device(): got.append(exchange(coded))  111 us
    pallas_call x2, Pallas kernels, code(): pl.pallas_call(functools.partial(code_kernel, mark), grid_spec=pltpu.Pref...  11.1 us
    all_to_all x2, starting transfers between devices, on_device(): got.append(exchange(coded))  10.6 us
    all_to_all x1, waiting for transfers between devices, on_device(): found = exchange(best)  6.48 us
    pallas_call x2, Pallas kernels, compare(): pl.pallas_call(functools.partial(compare_kernel, cl_dev, width_all, tile,...  5.89 us
    all_to_all x1, starting transfers between devices, on_device(): found = exchange(best)  3.83 us
  transfers between devices with their start and end apart: 6, of which 4 were waited for; matrix products, arithmetic and copies ran while one was open for 1% of the time, Pallas kernels for 8%

profile of v8, /device:TPU:0, one launch (start us, length us, event | category | flops | bytes accessed | tf_op | source)
XLA Modules:
  0.0 155.4 jit_solution(12197944414469856026)
XLA Ops:
  0.6 1.0 constant_dynamic-slice_fusion
  1.7 0.5 collective-permute-start
  2.2 0.1 collective-permute-start.1
  2.3 1.5 collective-permute-done.1.mate_ref
  3.8 0.0 collective-permute-done.y_ref
  3.8 0.4 collective-permute-start.2
  4.1 3.1 %shard_map.41 = bf16[256,1280]{1,0:T(8,128)(2,1)} custom-call(s32[1]{0:T(128)} %bitcast.core_ref, s32[384]{0:T(512)} %mine_ref.3, s32[384]{0:T(512)S(1)} %collective-permute-done.1.mate_ref, f32[384,4096]{1,0:T(8,128)} %x_ref.2, f32[384,256]{1,0:T(8,128)S(1)} %collective-permute-done.y_ref), custom_call_target="tpu_custom_call" | custom-call | tf_op jit(solution)/shard_map/pallas_call | solution.py:103
  7.2 7.0 %all-to-all-start.1 = ((bf16[32,8,1280]{2,1,0:T(8,128)(2,1)}), bf16[32,8,1280]{2,1,0:T(8,128)(2,1)S(1)}, u32[]{:S(2)}, u32[]{:S(2)}) async-start(bf16[32,8,1280]{2,1,0:T(8,128)(2,1)} %bitcast.12), calls=%async_computation.1 | async-start | bytes 1310720 | tf_op jit(solution)/shard_map/all_to_all | solution.py:276
  14.2 0.0 collective-permute-done.2.y_ref
  14.3 8.0 %shard_map.42 = bf16[256,8960]{1,0:T(8,128)(2,1)} custom-call(s32[1]{0:T(128)} %bitcast.core_ref, s32[384]{0:T(512)} %mine_ref.3, s32[384]{0:T(512)S(1)} %collective-permute-done.1.mate_ref, f32[384,4096]{1,0:T(8,128)} %x_ref.2, f32[384,4096]{1,0:T(8,128)} %collective-permute-done.2.y_ref), custom_call_target="tpu_custom_call" | custom-call | tf_op jit(solution)/shard_map/pallas_call | solution.py:103
  22.2 0.0 copy-start
  22.2 9.9 %all-to-all-done.1 = bf16[32,8,1280]{2,1,0:T(8,128)(2,1)S(1)} async-done(((bf16[32,8,1280]{2,1,0:T(8,128)(2,1)}), bf16[32,8,1280]{2,1,0:T(8,128)(2,1)S(1)}, u32[]{:S(2)}, u32[]{:S(2)}) %all-to-all-start.1) | async-done | bytes 655392 | tf_op jit(solution)/shard_map/all_to_all | solution.py:276
  32.1 3.6 %all-to-all-start = ((bf16[32,8,8960]{2,1,0:T(8,128)(2,1)}), bf16[32,8,8960]{2,1,0:T(8,128)(2,1)}, u32[]{:S(2)}, u32[]{:S(2)}) async-start(bf16[32,8,8960]{2,1,0:T(8,128)(2,1)} %bitcast.11), calls=%async_computation | async-start | bytes 9175040 | tf_op jit(solution)/shard_map/all_to_all | solution.py:276
  35.8 0.0 copy-done
  35.8 0.2 convert_reduce_fusion
  36.0 0.7 shard_map.43
  36.7 101.5 %all-to-all-done = bf16[32,8,8960]{2,1,0:T(8,128)(2,1)} async-done(((bf16[32,8,8960]{2,1,0:T(8,128)(2,1)}), bf16[32,8,8960]{2,1,0:T(8,128)(2,1)}, u32[]{:S(2)}, u32[]{:S(2)}) %all-to-all-start) | async-done | bytes 4587552 | tf_op jit(solution)/shard_map/all_to_all | solution.py:276
  138.2 5.2 %shard_map.44 = (f32[8,1792]{1,0:T(8,128)S(1)}, f32[8,1792]{1,0:T(8,128)S(1)}, f32[32,128]{1,0:T(8,128)}) custom-call(bf16[16,2,8,8960]{3,2,1,0:T(8,128)(2,1)} %bitcast.2.refs_0_, f32[512,512]{1,0:T(8,128)S(1)} %get-tuple-element.21.refs_1_, f32[512,1]{1,0:T(8,128)S(1)} %get-tuple-element.22.refs_2_), custom_call_target="tpu_custom_call" | custom-call | tf_op jit(solution)/shard_map/pallas_call | solution.py:249
  143.4 3.8 %all-to-all-start.2 = ((f32[32,1,128]{2,1,0:T(1,128)}), f32[32,1,128]{2,1,0:T(1,128)S(1)}, u32[]{:S(2)}, u32[]{:S(2)}) async-start(f32[32,1,128]{2,1,0:T(1,128)} %bitcast.6), calls=%async_computation.2 | async-start | bytes 32768 | tf_op jit(solution)/shard_map/all_to_all | solution.py:279
  147.3 0.7 pad_maximum_fusion
  148.0 6.5 %all-to-all-done.2 = f32[32,1,128]{2,1,0:T(1,128)S(1)} async-done(((f32[32,1,128]{2,1,0:T(1,128)}), f32[32,1,128]{2,1,0:T(1,128)S(1)}, u32[]{:S(2)}, u32[]{:S(2)}) %all-to-all-start.2) | async-done | bytes 16416 | tf_op jit(solution)/shard_map/all_to_all | solution.py:279
  154.4 1.0 fusion
  (1 shorter events, 0.0 us)
Async XLA Ops:
  1.7 2.1 %collective-permute-start = (f32[384,256]{1,0:T(8,128)S(1)}, f32[384,256]{1,0:T(8,128)S(1)}, u32[]{:S(2)}, u32[]{:S(2)}) collective-permute-start(f32[384,256]{1,0:T(8,128)S(1)} %constant_dynamic-slice_fusion), channel_id=1, source_target_pairs={{0,1},{1,0},{2,3},{3,2},{4,5},{5,4},{6,7},{7,6},{8,9},{9,8},{10,11... | collective-permute-start | bytes 1179656 | tf_op jit(solution)/shard_map/ppermute | solution.py:269
  2.2 1.6 %collective-permute-start.1 = (s32[384]{0:T(512)}, s32[384]{0:T(512)S(1)}, u32[]{:S(2)}, u32[]{:S(2)}) collective-permute-start(s32[384]{0:T(512)} %mine_ref.3), channel_id=1, source_target_pairs={{0,1},{1,0},{2,3},{3,2},{4,5},{5,4},{6,7},{7,6},{8,9},{9,8},{10,11... | collective-permute-start | bytes 4616 | tf_op jit(solution)/shard_map/ppermute | solution.py:266
  3.8 10.5 %collective-permute-start.2 = (f32[384,4096]{1,0:T(8,128)}, f32[384,4096]{1,0:T(8,128)}, u32[]{:S(2)}, u32[]{:S(2)}) collective-permute-start(f32[384,4096]{1,0:T(8,128)} %x_ref.2), channel_id=1, source_target_pairs={{0,1},{1,0},{2,3},{3,2},{4,5},{5,4},{6,7},{7,6},{8,9},{9,8},{10,11... | collective-permute-start | bytes 18874376 | tf_op jit(solution)/shard_map/ppermute | solution.py:271
  7.2 24.9 %all-to-all-start.1 = ((bf16[32,8,1280]{2,1,0:T(8,128)(2,1)}), bf16[32,8,1280]{2,1,0:T(8,128)(2,1)S(1)}, u32[]{:S(2)}, u32[]{:S(2)}) async-start(bf16[32,8,1280]{2,1,0:T(8,128)(2,1)} %bitcast.12), calls=%async_computation.1 | async-start | bytes 1310720 | tf_op jit(solution)/shard_map/all_to_all | solution.py:276
  22.2 13.6 %copy-start = (s32[384]{0:T(512)S(1)}, s32[384]{0:T(512)}, u32[]{:S(2)}) copy-start(s32[384]{0:T(512)} %mine_ref.3) | copy-start | bytes 4612
  32.1 106.1 %all-to-all-start = ((bf16[32,8,8960]{2,1,0:T(8,128)(2,1)}), bf16[32,8,8960]{2,1,0:T(8,128)(2,1)}, u32[]{:S(2)}, u32[]{:S(2)}) async-start(bf16[32,8,8960]{2,1,0:T(8,128)(2,1)} %bitcast.11), calls=%async_computation | async-start | bytes 9175040 | tf_op jit(solution)/shard_map/all_to_all | solution.py:276
  143.4 11.0 %all-to-all-start.2 = ((f32[32,1,128]{2,1,0:T(1,128)}), f32[32,1,128]{2,1,0:T(1,128)S(1)}, u32[]{:S(2)}, u32[]{:S(2)}) async-start(f32[32,1,128]{2,1,0:T(1,128)} %bitcast.6), calls=%async_computation.2 | async-start | bytes 32768 | tf_op jit(solution)/shard_map/all_to_all | solution.py:279

commit v9 on v8

--- a/solution.py
+++ b/solution.py
@@ -46,18 +46,20 @@
     def _():
         mine = mine_ref[...].reshape(1, rows)
         mate = mate_ref[...].reshape(1, rows)
+        before = (iota((rows, 1), 0) < iota((1, rows), 1)).astype(F32).astype(BF16)
         counts = []
         for k, pick_ref in enumerate((pick0_ref, pick1_ref)):
-            ids = jnp.where(core == k, mine, mate)
-            twin = (to_col(ids) == ids) & (iota((rows, rows), 0) < iota((rows, rows), 1))
-            second = jnp.sum(twin.astype(F32), axis=0, keepdims=True) > 0.5
-            member = iota((CLUSTERS, rows), 0) == ids
-            upper = member & ~second if k == 0 else member
+            member = iota((CLUSTERS, 1), 0) == jnp.where(core == k, mine, mate)
+            marks = member.astype(F32)
+            rank = mm(marks.astype(BF16), before)
+            second = jnp.where(member, rank, 0.0)
+            upper = (marks - second if k == 0 else marks).astype(BF16)
+            second = second.astype(BF16)
             for j in range(2):
                 cols = slice(j * rows, (j + 1) * rows)
-                pick_ref[:CLUSTERS, cols] = upper.astype(F32).astype(BF16)
-                pick_ref[CLUSTERS:, cols] = (member & second).astype(F32).astype(BF16)
-            counts.append(jnp.sum(member.astype(F32), axis=1, keepdims=True))
+                pick_ref[:CLUSTERS, cols] = upper
+                pick_ref[CLUSTERS:, cols] = second
+            counts.append(jnp.sum(marks, axis=1, keepdims=True))
         num_ref[:CLUSTERS] = counts[0]
         num_ref[CLUSTERS : 2 * CLUSTERS] = counts[1]
         num_ref[2 * CLUSTERS :] = 1.0 / jnp.maximum(counts[0] + counts[1], 1.0)
@@ -96,16 +98,14 @@
     line = pl.BlockSpec((rows,), lambda t, core: (0,))
     block = pl.BlockSpec((rows, tile), lambda t, core: (0, first + core[0] * steps + t))
     if y.shape[1] == tile:
-        y = pltpu.with_memory_space_constraint(y, pltpu.VMEM)
-        y_spec = pl.BlockSpec(memory_space=pltpu.VMEM)
-    else:
-        y_spec = block
+        x, y = [pltpu.with_memory_space_constraint(z, pltpu.VMEM) for z in (x, y)]
+        block = pl.BlockSpec(memory_space=pltpu.VMEM)
     return pl.pallas_call(
         functools.partial(code_kernel, mark),
         grid_spec=pltpu.PrefetchScalarGridSpec(
             num_scalar_prefetch=1,
             grid=(steps,),
-            in_specs=[line, pl.BlockSpec(memory_space=pltpu.VMEM), block, y_spec],
+            in_specs=[line, pl.BlockSpec(memory_space=pltpu.VMEM), block, block],
             out_specs=pl.BlockSpec((CLUSTERS, 5 * tile), lambda t, core: (0, t)),
             scratch_shapes=[
                 pltpu.VMEM((2 * CLUSTERS, 2 * rows), BF16),
@@ -267,11 +267,13 @@
     first, part, _ = PARTS[0]
     half = part // 2
     head = swap(lax.dynamic_slice_in_dim(embeddings, first + (1 - core) * half, half, 1))
-    whole, head, mate = lax.optimization_barrier((embeddings, head, mate))
+    near = lax.dynamic_slice_in_dim(embeddings, first + core * half, half, 1)
+    whole, head, mate, near = lax.optimization_barrier((embeddings, head, mate, near))
     tail = swap(whole)
     got = []
     for start, part, tile in PARTS:
-        coded = code(core.astype(jnp.int32).reshape(1), assignment, mate, embeddings, tail if got else head, start, part, tile, not got)
+        pair = (embeddings, tail) if got else (near, head)
+        coded = code(core.astype(jnp.int32).reshape(1), assignment, mate, *pair, start, part, tile, not got)
         coded, embeddings = lax.optimization_barrier((coded, embeddings))
         got.append(exchange(coded))
     c0, c1, *state = compare(got[0], None, cl_dev, width, PARTS[0][2])

time: 156 us -> 155 us (level)
  transfers between devices with their start and end apart: 6 -> 6, of which waited for: 4 -> 5; matrix products, arithmetic and copies ran while one was open for 1% -> 1% of each run, Pallas kernels for 8% -> 7%
where the time goes in v9:
time: 155 us
  waiting for transfers between devices  120 us (77%)
  Pallas kernels  16.3 us (11%)
  starting transfers between devices  15.4 us (10%)
    all_to_all x2, waiting for transfers between devices, on_device(): got.append(exchange(coded))  111 us
    all_to_all x2, starting transfers between devices, on_device(): got.append(exchange(coded))  10.6 us
    pallas_call x2, Pallas kernels, code(): pl.pallas_call(functools.partial(code_kernel, mark), grid_spec=pltpu.Pref...  10.4 us
    all_to_all x1, waiting for transfers between devices, on_device(): found = exchange(best)  6.48 us
    pallas_call x2, Pallas kernels, compare(): pl.pallas_call(functools.partial(compare_kernel, cl_dev, width_all, tile,...  5.89 us
    all_to_all x1, starting transfers between devices, on_device(): found = exchange(best)  3.83 us
  transfers between devices with their start and end apart: 6, of which 5 were waited for; matrix products, arithmetic and copies ran while one was open for 1% of the time, Pallas kernels for 7%

profile of v9, /device:TPU:0, one launch (start us, length us, event | category | flops | bytes accessed | tf_op | source)
XLA Modules:
  0.0 155.1 jit_solution(15291082471493447661)
XLA Ops:
  0.6 1.2 constant_dynamic-slice_fusion
  1.8 0.5 collective-permute-start
  2.3 0.1 collective-permute-start.1
  2.4 1.5 collective-permute-done.1.mate_ref
  3.9 0.0 collective-permute-done.y_ref
  3.9 0.4 collective-permute-start.2
  4.3 2.6 %shard_map.41 = bf16[256,1280]{1,0:T(8,128)(2,1)} custom-call(s32[1]{0:T(128)} %bitcast.core_ref, s32[384]{0:T(512)} %mine_ref.3, s32[384]{0:T(512)S(1)} %collective-permute-done.1.mate_ref, f32[384,256]{1,0:T(8,128)S(1)} %get-tuple-element.17.x_ref, f32[384,256]{1,0:T(8,128)S(1)} %collective-permute-done.y_ref), custom_call_target="tpu_custom_call" | custom-call | tf_op jit(solution)/shard_map/pallas_call | solution.py:103
  6.9 7.0 %all-to-all-start.1 = ((bf16[32,8,1280]{2,1,0:T(8,128)(2,1)}), bf16[32,8,1280]{2,1,0:T(8,128)(2,1)S(1)}, u32[]{:S(2)}, u32[]{:S(2)}) async-start(bf16[32,8,1280]{2,1,0:T(8,128)(2,1)} %bitcast.12), calls=%async_computation.1 | async-start | bytes 1310720 | tf_op jit(solution)/shard_map/all_to_all | solution.py:278
  13.9 0.5 collective-permute-done.2.y_ref
  14.4 7.8 %shard_map.42 = bf16[256,8960]{1,0:T(8,128)(2,1)} custom-call(s32[1]{0:T(128)} %bitcast.core_ref, s32[384]{0:T(512)} %mine_ref.3, s32[384]{0:T(512)S(1)} %collective-permute-done.1.mate_ref, f32[384,4096]{1,0:T(8,128)} %x_ref, f32[384,4096]{1,0:T(8,128)} %collective-permute-done.2.y_ref), custom_call_target="tpu_custom_call" | custom-call | tf_op jit(solution)/shard_map/pallas_call | solution.py:103
  22.2 0.0 copy-start
  22.2 9.6 %all-to-all-done.1 = bf16[32,8,1280]{2,1,0:T(8,128)(2,1)S(1)} async-done(((bf16[32,8,1280]{2,1,0:T(8,128)(2,1)}), bf16[32,8,1280]{2,1,0:T(8,128)(2,1)S(1)}, u32[]{:S(2)}, u32[]{:S(2)}) %all-to-all-start.1) | async-done | bytes 655392 | tf_op jit(solution)/shard_map/all_to_all | solution.py:278
  31.8 3.6 %all-to-all-start = ((bf16[32,8,8960]{2,1,0:T(8,128)(2,1)}), bf16[32,8,8960]{2,1,0:T(8,128)(2,1)}, u32[]{:S(2)}, u32[]{:S(2)}) async-start(bf16[32,8,8960]{2,1,0:T(8,128)(2,1)} %bitcast.11), calls=%async_computation | async-start | bytes 9175040 | tf_op jit(solution)/shard_map/all_to_all | solution.py:278
  35.5 0.0 copy-done
  35.5 0.2 convert_reduce_fusion
  35.7 0.7 shard_map.43
  36.4 101.5 %all-to-all-done = bf16[32,8,8960]{2,1,0:T(8,128)(2,1)} async-done(((bf16[32,8,8960]{2,1,0:T(8,128)(2,1)}), bf16[32,8,8960]{2,1,0:T(8,128)(2,1)}, u32[]{:S(2)}, u32[]{:S(2)}) %all-to-all-start) | async-done | bytes 4587552 | tf_op jit(solution)/shard_map/all_to_all | solution.py:278
  137.9 5.2 %shard_map.44 = (f32[8,1792]{1,0:T(8,128)S(1)}, f32[8,1792]{1,0:T(8,128)S(1)}, f32[32,128]{1,0:T(8,128)}) custom-call(bf16[16,2,8,8960]{3,2,1,0:T(8,128)(2,1)} %bitcast.2.refs_0_, f32[512,512]{1,0:T(8,128)S(1)} %get-tuple-element.23.refs_1_, f32[512,1]{1,0:T(8,128)S(1)} %get-tuple-element.24.refs_2_), custom_call_target="tpu_custom_call" | custom-call | tf_op jit(solution)/shard_map/pallas_call | solution.py:249
  143.1 3.8 %all-to-all-start.2 = ((f32[32,1,128]{2,1,0:T(1,128)}), f32[32,1,128]{2,1,0:T(1,128)S(1)}, u32[]{:S(2)}, u32[]{:S(2)}) async-start(f32[32,1,128]{2,1,0:T(1,128)} %bitcast.6), calls=%async_computation.2 | async-start | bytes 32768 | tf_op jit(solution)/shard_map/all_to_all | solution.py:281
  147.0 0.7 pad_maximum_fusion
  147.7 6.5 %all-to-all-done.2 = f32[32,1,128]{2,1,0:T(1,128)S(1)} async-done(((f32[32,1,128]{2,1,0:T(1,128)}), f32[32,1,128]{2,1,0:T(1,128)S(1)}, u32[]{:S(2)}, u32[]{:S(2)}) %all-to-all-start.2) | async-done | bytes 16416 | tf_op jit(solution)/shard_map/all_to_all | solution.py:281
  154.1 1.0 fusion
  (1 shorter events, 0.0 us)
Async XLA Ops:
  1.8 2.1 %collective-permute-start = (f32[384,256]{1,0:T(8,128)S(1)}, f32[384,256]{1,0:T(8,128)S(1)}, u32[]{:S(2)}, u32[]{:S(2)}) collective-permute-start(f32[384,256]{1,0:T(8,128)S(1)} %get-tuple-element.31), channel_id=1, source_target_pairs={{0,1},{1,0},{2,3},{3,2},{4,5},{5,4},{6,7},{7,6},{8,9},{9,8},{10,11... | collective-permute-start | bytes 1179656 | tf_op jit(solution)/shard_map/ppermute | solution.py:269
  2.3 1.6 %collective-permute-start.1 = (s32[384]{0:T(512)}, s32[384]{0:T(512)S(1)}, u32[]{:S(2)}, u32[]{:S(2)}) collective-permute-start(s32[384]{0:T(512)} %mine_ref.3), channel_id=1, source_target_pairs={{0,1},{1,0},{2,3},{3,2},{4,5},{5,4},{6,7},{7,6},{8,9},{9,8},{10,11... | collective-permute-start | bytes 4616 | tf_op jit(solution)/shard_map/ppermute | solution.py:266
  3.9 10.5 %collective-permute-start.2 = (f32[384,4096]{1,0:T(8,128)}, f32[384,4096]{1,0:T(8,128)}, u32[]{:S(2)}, u32[]{:S(2)}) collective-permute-start(f32[384,4096]{1,0:T(8,128)} %x_ref), channel_id=1, source_target_pairs={{0,1},{1,0},{2,3},{3,2},{4,5},{5,4},{6,7},{7,6},{8,9},{9,8},{10,11... | collective-permute-start | bytes 18874376 | tf_op jit(solution)/shard_map/ppermute | solution.py:272
  6.9 24.9 %all-to-all-start.1 = ((bf16[32,8,1280]{2,1,0:T(8,128)(2,1)}), bf16[32,8,1280]{2,1,0:T(8,128)(2,1)S(1)}, u32[]{:S(2)}, u32[]{:S(2)}) async-start(bf16[32,8,1280]{2,1,0:T(8,128)(2,1)} %bitcast.12), calls=%async_computation.1 | async-start | bytes 1310720 | tf_op jit(solution)/shard_map/all_to_all | solution.py:278
  22.2 13.3 %copy-start = (s32[384]{0:T(512)S(1)}, s32[384]{0:T(512)}, u32[]{:S(2)}) copy-start(s32[384]{0:T(512)} %mine_ref.3) | copy-start | bytes 4612
  31.8 106.1 %all-to-all-start = ((bf16[32,8,8960]{2,1,0:T(8,128)(2,1)}), bf16[32,8,8960]{2,1,0:T(8,128)(2,1)}, u32[]{:S(2)}, u32[]{:S(2)}) async-start(bf16[32,8,8960]{2,1,0:T(8,128)(2,1)} %bitcast.11), calls=%async_computation | async-start | bytes 9175040 | tf_op jit(solution)/shard_map/all_to_all | solution.py:278
  143.1 11.0 %all-to-all-start.2 = ((f32[32,1,128]{2,1,0:T(1,128)}), f32[32,1,128]{2,1,0:T(1,128)S(1)}, u32[]{:S(2)}, u32[]{:S(2)}) async-start(f32[32,1,128]{2,1,0:T(1,128)} %bitcast.6), calls=%async_computation.2 | async-start | bytes 32768 | tf_op jit(solution)/shard_map/all_to_all | solution.py:281

commit v10 on v9

--- a/solution.py
+++ b/solution.py
@@ -203,20 +203,11 @@
         score = gram * inv_col * inv_row / width_all
         usable = ((row % cl_dev) == (col % cl_dev)) & (row != col) & (live_ref[...] > 0.5)
         best = jnp.max(jnp.where(usable, score, -1.0), axis=0, keepdims=True)
-        sources = 2 * slots // cl_dev
-        place = iota((sources, n), 1)
-        source = (place % slots) // cl_dev * 2 + place // (2 * slots)
-        spread = jnp.where(source == iota((sources, n), 0), best, 0.0)
-        place = iota((n, LANES), 0)
-        lane = (place // slots) % 2 * cl_dev + place % cl_dev
-        pick = (lane == iota((n, LANES), 1)).astype(F32)
-        best_ref[...] = lax.dot_general(
-            spread,
-            pick,
-            (((1,), (0,)), ((), ())),
-            precision=lax.Precision.HIGHEST,
-            preferred_element_type=F32,
-        )
+        device = iota((2 * slots // cl_dev, 1), 0)
+        here = device // 2 == iota((1, slots), 1) // cl_dev
+        lines = [best[:, k * slots : (k + 1) * slots] for k in range(4)]
+        lines = [jnp.where(here, jnp.where(device % 2 == 0, lines[k], lines[k + 2]), 0.0) for k in range(2)]
+        best_ref[...] = lines[0] + pltpu.roll(lines[1], slots // 2, 1)
 
 
 def compare(got, state, cl_dev, width_all, tile):
@@ -283,7 +274,8 @@
     twin = (assignment[:, None] == assignment[None, :]) & (row_ids[None, :] < row_ids[:, None])
     second = jnp.sum(twin.astype(jnp.int32), axis=1)
     owner = (assignment // cl_dev)[:, None] == jnp.arange(dev_count, dtype=jnp.int32)[None, :]
-    lane = (second * cl_dev + assignment % cl_dev)[:, None] == jnp.arange(LANES, dtype=jnp.int32)[None, :]
+    place = lax.axis_index("rows").astype(jnp.int32) // 2 * cl_dev + assignment % cl_dev + second * (LANES // 2)
+    lane = (place % LANES)[:, None] == jnp.arange(LANES, dtype=jnp.int32)[None, :]
     lines = lax.dot_general(
         owner.astype(F32), found, (((1,), (0,)), ((), ())), precision=lax.Precision.HIGHEST
     )

time: 155 us -> 155 us (level)
  no operation moved by 1% of the time
where the time goes in v10:
time: 155 us
  waiting for transfers between devices  120 us (77%)
  Pallas kernels  16.2 us (10%)
  starting transfers between devices  15.4 us (10%)
    all_to_all x2, waiting for transfers between devices, on_device(): got.append(exchange(coded))  111 us
    all_to_all x2, starting transfers between devices, on_device(): got.append(exchange(coded))  10.6 us
    pallas_call x2, Pallas kernels, code(): pl.pallas_call(functools.partial(code_kernel, mark), grid_spec=pltpu.Pref...  10.5 us
    all_to_all x1, waiting for transfers between devices, on_device(): found = exchange(best)  6.48 us
    pallas_call x2, Pallas kernels, compare(): pl.pallas_call(functools.partial(compare_kernel, cl_dev, width_all, tile,...  5.73 us
    all_to_all x1, starting transfers between devices, on_device(): found = exchange(best)  3.85 us
  transfers between devices with their start and end apart: 6, of which 5 were waited for; matrix products, arithmetic and copies ran while one was open for 1% of the time, Pallas kernels for 7%

profile of v10, /device:TPU:0, one launch (start us, length us, event | category | flops | bytes accessed | tf_op | source)
XLA Modules:
  0.0 155.0 jit_solution(2981208750737866533)
XLA Ops:
  0.6 1.2 constant_dynamic-slice_fusion
  1.8 0.5 collective-permute-start
  2.3 0.1 collective-permute-start.1
  2.4 1.5 collective-permute-done.1.mate_ref
  3.9 0.0 collective-permute-done.y_ref
  3.9 0.4 collective-permute-start.2
  4.3 2.7 %shard_map.41 = bf16[256,1280]{1,0:T(8,128)(2,1)} custom-call(s32[1]{0:T(128)} %bitcast.core_ref, s32[384]{0:T(512)} %mine_ref.3, s32[384]{0:T(512)S(1)} %collective-permute-done.1.mate_ref, f32[384,256]{1,0:T(8,128)S(1)} %get-tuple-element.17.x_ref, f32[384,256]{1,0:T(8,128)S(1)} %collective-permute-done.y_ref), custom_call_target="tpu_custom_call" | custom-call | tf_op jit(solution)/shard_map/pallas_call | solution.py:103
  6.9 7.0 %all-to-all-start.1 = ((bf16[32,8,1280]{2,1,0:T(8,128)(2,1)}), bf16[32,8,1280]{2,1,0:T(8,128)(2,1)S(1)}, u32[]{:S(2)}, u32[]{:S(2)}) async-start(bf16[32,8,1280]{2,1,0:T(8,128)(2,1)} %bitcast.12), calls=%async_computation.1 | async-start | bytes 1310720 | tf_op jit(solution)/shard_map/all_to_all | solution.py:269
  13.9 0.5 collective-permute-done.2.y_ref
  14.4 7.8 %shard_map.42 = bf16[256,8960]{1,0:T(8,128)(2,1)} custom-call(s32[1]{0:T(128)} %bitcast.core_ref, s32[384]{0:T(512)} %mine_ref.3, s32[384]{0:T(512)S(1)} %collective-permute-done.1.mate_ref, f32[384,4096]{1,0:T(8,128)} %x_ref, f32[384,4096]{1,0:T(8,128)} %collective-permute-done.2.y_ref), custom_call_target="tpu_custom_call" | custom-call | tf_op jit(solution)/shard_map/pallas_call | solution.py:103
  22.2 0.0 copy-start
  22.2 9.7 %all-to-all-done.1 = bf16[32,8,1280]{2,1,0:T(8,128)(2,1)S(1)} async-done(((bf16[32,8,1280]{2,1,0:T(8,128)(2,1)}), bf16[32,8,1280]{2,1,0:T(8,128)(2,1)S(1)}, u32[]{:S(2)}, u32[]{:S(2)}) %all-to-all-start.1) | async-done | bytes 655392 | tf_op jit(solution)/shard_map/all_to_all | solution.py:269
  31.9 3.6 %all-to-all-start = ((bf16[32,8,8960]{2,1,0:T(8,128)(2,1)}), bf16[32,8,8960]{2,1,0:T(8,128)(2,1)}, u32[]{:S(2)}, u32[]{:S(2)}) async-start(bf16[32,8,8960]{2,1,0:T(8,128)(2,1)} %bitcast.11), calls=%async_computation | async-start | bytes 9175040 | tf_op jit(solution)/shard_map/all_to_all | solution.py:269
  35.5 0.0 copy-done
  35.5 0.2 convert_reduce_fusion
  35.8 0.7 shard_map.43
  36.5 101.5 %all-to-all-done = bf16[32,8,8960]{2,1,0:T(8,128)(2,1)} async-done(((bf16[32,8,8960]{2,1,0:T(8,128)(2,1)}), bf16[32,8,8960]{2,1,0:T(8,128)(2,1)}, u32[]{:S(2)}, u32[]{:S(2)}) %all-to-all-start) | async-done | bytes 4587552 | tf_op jit(solution)/shard_map/all_to_all | solution.py:269
  137.9 5.1 %shard_map.44 = (f32[8,1792]{1,0:T(8,128)S(1)}, f32[8,1792]{1,0:T(8,128)S(1)}, f32[32,128]{1,0:T(8,128)}) custom-call(bf16[16,2,8,8960]{3,2,1,0:T(8,128)(2,1)} %bitcast.2.refs_0_, f32[512,512]{1,0:T(8,128)S(1)} %get-tuple-element.23.refs_1_, f32[512,1]{1,0:T(8,128)S(1)} %get-tuple-element.24.refs_2_), custom_call_target="tpu_custom_call" | custom-call | tf_op jit(solution)/shard_map/pallas_call | solution.py:240
  143.0 3.8 %all-to-all-start.2 = ((f32[32,1,128]{2,1,0:T(1,128)}), f32[32,1,128]{2,1,0:T(1,128)S(1)}, u32[]{:S(2)}, u32[]{:S(2)}) async-start(f32[32,1,128]{2,1,0:T(1,128)} %bitcast.6), calls=%async_computation.2 | async-start | bytes 32768 | tf_op jit(solution)/shard_map/all_to_all | solution.py:272
  146.9 0.7 pad_maximum_fusion
  147.5 6.5 %all-to-all-done.2 = f32[32,1,128]{2,1,0:T(1,128)S(1)} async-done(((f32[32,1,128]{2,1,0:T(1,128)}), f32[32,1,128]{2,1,0:T(1,128)S(1)}, u32[]{:S(2)}, u32[]{:S(2)}) %all-to-all-start.2) | async-done | bytes 16416 | tf_op jit(solution)/shard_map/all_to_all | solution.py:272
  154.0 1.0 fusion
  (1 shorter events, 0.0 us)
Async XLA Ops:
  1.8 2.1 %collective-permute-start = (f32[384,256]{1,0:T(8,128)S(1)}, f32[384,256]{1,0:T(8,128)S(1)}, u32[]{:S(2)}, u32[]{:S(2)}) collective-permute-start(f32[384,256]{1,0:T(8,128)S(1)} %get-tuple-element.31), channel_id=1, source_target_pairs={{0,1},{1,0},{2,3},{3,2},{4,5},{5,4},{6,7},{7,6},{8,9},{9,8},{10,11... | collective-permute-start | bytes 1179656 | tf_op jit(solution)/shard_map/ppermute | solution.py:260
  2.3 1.6 %collective-permute-start.1 = (s32[384]{0:T(512)}, s32[384]{0:T(512)S(1)}, u32[]{:S(2)}, u32[]{:S(2)}) collective-permute-start(s32[384]{0:T(512)} %mine_ref.3), channel_id=1, source_target_pairs={{0,1},{1,0},{2,3},{3,2},{4,5},{5,4},{6,7},{7,6},{8,9},{9,8},{10,11... | collective-permute-start | bytes 4616 | tf_op jit(solution)/shard_map/ppermute | solution.py:257
  3.9 10.5 %collective-permute-start.2 = (f32[384,4096]{1,0:T(8,128)}, f32[384,4096]{1,0:T(8,128)}, u32[]{:S(2)}, u32[]{:S(2)}) collective-permute-start(f32[384,4096]{1,0:T(8,128)} %x_ref), channel_id=1, source_target_pairs={{0,1},{1,0},{2,3},{3,2},{4,5},{5,4},{6,7},{7,6},{8,9},{9,8},{10,11... | collective-permute-start | bytes 18874376 | tf_op jit(solution)/shard_map/ppermute | solution.py:263
  6.9 24.9 %all-to-all-start.1 = ((bf16[32,8,1280]{2,1,0:T(8,128)(2,1)}), bf16[32,8,1280]{2,1,0:T(8,128)(2,1)S(1)}, u32[]{:S(2)}, u32[]{:S(2)}) async-start(bf16[32,8,1280]{2,1,0:T(8,128)(2,1)} %bitcast.12), calls=%async_computation.1 | async-start | bytes 1310720 | tf_op jit(solution)/shard_map/all_to_all | solution.py:269
  22.2 13.3 %copy-start = (s32[384]{0:T(512)S(1)}, s32[384]{0:T(512)}, u32[]{:S(2)}) copy-start(s32[384]{0:T(512)} %mine_ref.3) | copy-start | bytes 4612
  31.9 106.1 %all-to-all-start = ((bf16[32,8,8960]{2,1,0:T(8,128)(2,1)}), bf16[32,8,8960]{2,1,0:T(8,128)(2,1)}, u32[]{:S(2)}, u32[]{:S(2)}) async-start(bf16[32,8,8960]{2,1,0:T(8,128)(2,1)} %bitcast.11), calls=%async_computation | async-start | bytes 9175040 | tf_op jit(solution)/shard_map/all_to_all | solution.py:269
  143.0 11.0 %all-to-all-start.2 = ((f32[32,1,128]{2,1,0:T(1,128)}), f32[32,1,128]{2,1,0:T(1,128)S(1)}, u32[]{:S(2)}, u32[]{:S(2)}) async-start(f32[32,1,128]{2,1,0:T(1,128)} %bitcast.6), calls=%async_computation.2 | async-start | bytes 32768 | tf_op jit(solution)/shard_map/all_to_all | solution.py:272
